TPU v7x, 32 devices: a whole 2x2x4 slice. The times are simulated.
32 devices in a mesh: clip: 4 (over z), frame: 4 (over x, core), row: 2 (over y).
Axes of the slice: x: 2, y: 2, z: 4, core: 2. Of those that a mesh axis runs over, the one named last changes fastest.
Arguments:
- features: bfloat16 [4, 16, 2, 32, 384], P('clip', 'frame', 'row'), may hold values from -6 to 6
- time_weight: bfloat16 [3, 384, 768], replicated, may hold values from -0.1875 to 0.1875
- time_bias: float32 [768], replicated, may hold values from -3 to 3
- space_weight: bfloat16 [3, 3, 384, 192], replicated, may hold values from -0.109375 to 0.109375
- pixel_grads: bfloat16 [4, 32, 4, 64, 192], P('clip', ('frame', 'row')), may hold values from -6 to 6
- frame_order: int32 [4, 4, 8], P('clip', 'frame'), may hold values from 0 to 7, each once within a row
Outputs:
- input_grad: bfloat16 [4, 16, 2, 32, 384], P('clip', 'frame', 'row')
- weight_grad: float32 [663552], P(('frame', 'row'))
Inputs may be any that keep to these rules, and one draw needn't show every extreme that they name: `frame_order`: for each clip and frame group, the row lists every one of the group's 8 output frames exactly once.
All inputs are finite; a program needn't handle non-finite values.
Results may differ from a plain program's by a relative error of at most 0.0049.
Values may be sent and summed in bfloat16 or wider, within the bound.
No kernel may reach another device: no remote copies, remote signals or barrier semaphores. Data moves between devices by JAX's collectives and lax.ppermute only.
A program may use at most 64 MiB of HBM per device.

v0:
```python
import math

import jax
import jax.numpy as jnp
from jax import lax
from jax.sharding import PartitionSpec as P


def passed_along(block, axis, distance):
    devices = range(lax.axis_size(axis))
    route = [(i - distance, i) for i in devices if i - distance in devices]
    return lax.ppermute(block, axis, route)


def extended_2(x, sides, width):
    for axis, dim in sides:
        count, length = (lax.axis_size(axis), x.shape[dim])
        up = [(i, (i + 1) % count) for i in range(count - 1)]
        down = [(j, i) for i, j in up]
        last = lax.slice_in_dim(x, length - width, length, axis=dim)
        initial = lax.slice_in_dim(x, 0, width, axis=dim)
        before = lax.ppermute(last, axis, up)
        after = lax.ppermute(initial, axis, down)
        x = jnp.concatenate([before, x, after], axis=dim)
    return x


def time_conv(extended, time_weight, time_bias):
    frames = extended.shape[1] - 2
    total = time_bias
    for offset in range(3):
        total = total + jnp.einsum(
            "cfhwi,io->cfhwo",
            extended[:, offset : offset + frames],
            time_weight[offset],
            preferred_element_type=jnp.float32,
        )
    return total.astype(jnp.bfloat16)


def local(features, time_weight, time_bias, space_weight, pixel_grads, frame_order):
    frames = features.shape[1]
    rows = features.shape[2]
    width = features.shape[3]
    channels = features.shape[4]
    up_rows = 2 * rows
    up_width = 2 * width
    band_count = lax.axis_size("row")
    prior = passed_along(features[:, frames - 2 :], "frame", 1)
    extended = jnp.concatenate((prior, features), axis=1)
    bordered = extended_2(extended, (("row", 2),), 1)
    activation = time_conv(bordered, time_weight, time_bias)
    position = jnp.arange(rows + 2) + lax.axis_index("row") * rows - 1
    inside = (position >= 0) & (position < band_count * rows)
    activation = jnp.where(
        inside[None, None, :, None, None], activation, jnp.zeros((), jnp.bfloat16)
    )
    upsampled = jnp.stack((activation[..., :channels], activation[..., channels:]), axis=2)
    upsampled = upsampled.reshape(1, 2 * frames, rows + 2, width, channels)
    upsampled = jnp.repeat(jnp.repeat(upsampled, 2, axis=2), 2, axis=3)[:, :, 1 : up_rows + 3]
    padded_act = jnp.pad(upsampled, ((0, 0), (0, 0), (0, 0), (1, 1), (0, 0)))
    inverse = jnp.argsort(frame_order[0, 0])
    stored = lax.all_to_all(pixel_grads, "row", split_axis=2, concat_axis=1, tiled=True)
    ordered = jnp.take(stored, inverse, axis=1)
    grad_band = extended_2(ordered, (("row", 2),), 1)
    grad_center = grad_band[:, :, 1 : up_rows + 1]
    tap_terms = []
    for tap_row in range(3):
        for tap_col in range(3):
            window = padded_act[:, :, tap_row : tap_row + up_rows, tap_col : tap_col + up_width]
            tap_terms.append(
                jnp.einsum(
                    "cfhwi,cfhwo->io", window, grad_center, preferred_element_type=jnp.float32
                )
            )
    weight_terms = jnp.stack(tap_terms).reshape(-1)
    out_pixels = (
        2
        * frames
        * up_rows
        * up_width
        * lax.axis_size("clip")
        * lax.axis_size("frame")
        * band_count
    )
    shard = lax.psum_scatter(weight_terms, ("frame", "row"), scatter_dimension=0, tiled=True)
    summed = lax.psum(shard, "clip")
    weight_grad = summed * (1.0 / math.sqrt(out_pixels))
    padded_grad = jnp.pad(grad_band, ((0, 0), (0, 0), (0, 0), (1, 1), (0, 0)))
    up_grad = jnp.zeros((1, 2 * frames, up_rows, up_width, channels), jnp.float32)
    for tap_row in range(3):
        for tap_col in range(3):
            window = padded_grad[
                :, :, 2 - tap_row : 2 - tap_row + up_rows, 2 - tap_col : 2 - tap_col + up_width
            ]
            up_grad = up_grad + jnp.einsum(
                "cfhwo,io->cfhwi",
                window,
                space_weight[tap_row, tap_col],
                preferred_element_type=jnp.float32,
            )
    pooled = up_grad.reshape(1, frames, 2, rows, 2, width, 2, channels).sum(axis=(4, 6))
    act_grad = (
        pooled.transpose(0, 1, 3, 4, 2, 5)
        .reshape(1, frames, rows, width, 2 * channels)
        .astype(jnp.bfloat16)
    )
    later = passed_along(act_grad[:, :2], "frame", -1)
    tail = jnp.concatenate((act_grad, later), axis=1)
    input_grad = jnp.zeros((1, frames, rows, width, channels), jnp.float32)
    for offset in range(3):
        input_grad = input_grad + jnp.einsum(
            "cfhwo,io->cfhwi",
            tail[:, 2 - offset : 2 - offset + frames],
            time_weight[offset],
            preferred_element_type=jnp.float32,
        )
    return (input_grad.astype(jnp.bfloat16), weight_grad)


def solution(mesh):
    return jax.shard_map(
        local,
        mesh=mesh,
        in_specs=(
            P("clip", "frame", "row", None, None),
            P(),
            P(),
            P(),
            P("clip", ("frame", "row"), None, None, None),
            P("clip", "frame", None),
        ),
        out_specs=(P("clip", "frame", "row", None, None), P(("frame", "row"))),
        check_vma=False,
    )
```

profile of v0, /device:TPU:0, one launch (start us, length us, event | category | flops | bytes accessed | tf_op | source)
XLA Modules:
  0.0 169.0 jit_solution(18252574621571368024)
XLA Ops:
  7.2 1.9 %copy.29 = bf16[1,4,4,64,192]{4,3,1,0,2:T(8,128)(2,1)} copy(bf16[1,4,4,64,192]{4,3,2,1,0:T(8,128)(2,1)} %param.10) | data formatting | bytes 786432 | tf_op args[4]
  9.1 4.3 %all-to-all-start = ((bf16[1,4,4,64,192]{4,3,1,0,2:T(8,128)(2,1)}), bf16[1,4,4,64,192]{4,3,1,0,2:T(8,128)(2,1)S(1)}, u32[]{:S(2)}, u32[]{:S(2)}) async-start(bf16[1,4,4,64,192]{4,3,1,0,2:T(8,128)(2,1)} %copy.29), calls=%async_computation | async-start | bytes 1048576 | tf_op jit(solution)/shard_map/all_to_all | solution.py:63
  13.4 1.7 %collective-permute-start.3 = (bf16[1,2,1,32,384]{4,3,2,1,0:T(8,128)(2,1)S(1)}, bf16[1,2,1,32,384]{4,3,2,1,0:T(8,128)(2,1)S(1)}, u32[]{:S(2)}, u32[]{:S(2)}) collective-permute-start(bf16[1,2,1,32,384]{4,3,2,1,0:T(8,128)(2,1)S(1)} %slice.163), channel_id=1, source_target_pairs={{0,2},{2,4},{4,6},{1,3},{3,5},{5,7},{8,10},{10,12},{12,14},{9,11},... | collective-permute-start | bytes 147464 | tf_op jit(solution)/shard_map/ppermute | solution.py:12
  15.1 1.0 sort.17
  16.1 0.6 dynamic-slice
  17.4 1.3 collective-permute-start.5
  18.7 4.6 %collective-permute-start.4 = (bf16[1,6,1,32,384]{4,3,2,1,0:T(8,128)(2,1)S(1)}, bf16[1,6,1,32,384]{4,3,2,1,0:T(8,128)(2,1)S(1)}, u32[]{:S(2)}, u32[]{:S(2)}) collective-permute-start(bf16[1,6,1,32,384]{4,3,2,1,0:T(8,128)(2,1)S(1)} %constant_dynamic-update-slice_fusion.2), channel_id=1, source_target_pairs={{0,1},{2,3},{4,5},{6,7},{8,9},{10,11},{12,13},{14,15},{16,17},{18,... | collective-permute-start | bytes 442376 | tf_op jit(solution)/shard_map/ppermute | solution.py:22
  23.4 0.6 gather_fusion
  24.1 0.8 fusion.97
  25.0 1.3 collective-permute-start.1
  26.3 5.2 %collective-permute-start = (bf16[1,8,1,64,192]{4,3,2,1,0:T(8,128)(2,1)}, bf16[1,8,1,64,192]{4,3,2,1,0:T(8,128)(2,1)S(1)}, u32[]{:S(2)}, u32[]{:S(2)}) collective-permute-start(bf16[1,8,1,64,192]{4,3,2,1,0:T(8,128)(2,1)} %get-tuple-element.18), channel_id=1, source_target_pairs={{0,1},{2,3},{4,5},{6,7},{8,9},{10,11},{12,13},{14,15},{16,17},{18,... | collective-permute-start | bytes 589832 | tf_op jit(solution)/shard_map/ppermute | solution.py:22
  31.6 0.5 convolution_add_fusion.2
  32.1 0.5 convolution_add_fusion.1
  32.6 0.5 fusion.6
  33.4 2.3 %broadcast_in_dim.43 = bf16[8,6,32,2,384]{4,3,2,1,0:T(2,128)(2,1)S(1)} broadcast(bf16[8,6,32,384]{3,2,1,0:T(8,128)(2,1)S(1)} %bitcast.284), dimensions={0,1,2,4} | broadcast | bytes 3538944 | tf_op jit(solution)/shard_map/broadcast_in_dim | solution.py:60
  35.7 2.4 %broadcast_in_dim.44 = bf16[1,8,6,64,384]{4,3,2,1,0:T(8,128)(2,1)} reshape(bf16[8,6,32,2,384]{4,3,2,1,0:T(2,128)(2,1)S(1)} %broadcast_in_dim.43) | data formatting | bytes 4718592 | tf_op jit(solution)/shard_map/broadcast_in_dim | solution.py:60
  38.1 1.6 slice.197
  39.7 0.4 fusion.17
  40.1 1.2 copy-done
  41.8 0.4 fusion.15
  42.2 0.4 fusion.14
  42.7 0.4 fusion.13
  43.1 0.4 fusion.12
  43.5 0.4 fusion.11
  44.0 0.4 fusion.10
  44.4 0.4 fusion.9
  44.8 2.9 %copy.36 = f32[9,384,192]{2,1,0:T(8,128)} copy(f32[9,384,192]{1,2,0:T(8,128)S(1)} %fusion.9) | data formatting | bytes 5308416 | tf_op jit(solution)/shard_map/stack | solution.py:76
  47.7 5.0 %reshape.249 = f32[663552]{0:T(1024)} reshape(f32[9,384,192]{2,1,0:T(8,128)} %copy.36) | data formatting | bytes 5308416 | tf_op jit(solution)/shard_map/reshape | solution.py:76
  53.0 1.1 copy-done.3
  54.1 0.4 fusion.63
  54.5 1.5 fusion.8
  56.1 0.4 fusion.41
  56.5 0.4 fusion.45
  56.9 0.4 fusion.46
  57.4 0.4 fusion.47
  57.8 0.4 fusion.48
  58.2 0.4 fusion.53
  58.7 1.4 fusion.50
  60.0 0.7 add_reduce_fusion
  60.8 0.5 reduce_sum.14
  61.3 1.0 reduce_sum.18
  62.7 1.3 collective-permute-start.2
  64.3 2.5 %collective-permute-done.2 = bf16[1,2,1,32,768]{4,3,1,2,0:T(8,128)(2,1)S(1)} collective-permute-done((bf16[1,2,1,32,768]{4,3,1,2,0:T(8,128)(2,1)S(1)}, bf16[1,2,1,32,768]{4,3,1,2,0:T(8,128)(2,1)S(1)}, u32[]{:S(2)}, u32[]{:S(2)}) %collective-permute-start.2) | collective-permute-done | bytes 98336 | tf_op jit(solution)/shard_map/ppermute | solution.py:12
  66.9 54.9 %all-reduce.8.cloned.1.call-done = f32[663552]{0:T(1024)} async-done(((f32[663552]{0:T(1024)}), f32[663552]{0:T(1024)}) %all-reduce.8.cloned.1.call-update) | async-done | bytes 2654224
  121.7 1.7 %dynamic-slice.1 = f32[82944]{0:T(1024)} dynamic-slice(f32[663552]{0:T(1024)} %all-reduce.8.cloned.1.call-done, u32[]{:T(128)S(6)} %multiply.1), dynamic_slice_sizes={82944} | dynamic-slice | bytes 663556
  123.8 1.0 fusion.20
  124.7 35.7 %all-reduce.6.cloned.1.call-done = f32[82944]{0:T(1024)} async-done(((f32[82944]{0:T(1024)}), f32[82944]{0:T(1024)}) %all-reduce.6.cloned.1.call-update) | async-done | bytes 331792 | tf_op jit(solution)/shard_map/psum | solution.py:87
  160.4 1.7 %broadcast_multiply_fusion = f32[82944]{0:T(1024)} fusion(f32[82944]{0:T(1024)} %all-reduce.6.cloned.1.call-done), kind=kLoop, calls=%fused_computation.107 | loop fusion | flops 82944 | bytes 663552 | tf_op jit(solution)/shard_map/mul | solution.py:88
  (49 shorter events, 2.3 us)
Async XLA Ops:
  7.2 9.0 %copy-start.7 = (u32[32]{0:T(128)S(1)}, u32[32]{0:T(128)}, u32[]{:S(2)}) copy-start(u32[32]{0:T(128)} %constant.43) | copy-start | bytes 388
  7.2 6.2 %copy-start.4 = (bf16[1,4,1,32,384]{4,3,2,1,0:T(8,128)(2,1)S(1)}, bf16[1,4,1,32,384]{4,3,2,1,0:T(8,128)(2,1)}, u32[]{:S(2)}) copy-start(bf16[1,4,1,32,384]{4,3,2,1,0:T(8,128)(2,1)} %param.6) | copy-start | bytes 294916
  7.2 7.9 %copy-start.6 = (s32[1,1,8]{2,1,0:T(1,128)S(1)}, s32[1,1,8]{2,1,0:T(1,128)}, u32[]{:S(2)}) copy-start(s32[1,1,8]{2,1,0:T(1,128)} %param.11) | copy-start | bytes 100
  9.1 14.2 %all-to-all-start = ((bf16[1,4,4,64,192]{4,3,1,0,2:T(8,128)(2,1)}), bf16[1,4,4,64,192]{4,3,1,0,2:T(8,128)(2,1)S(1)}, u32[]{:S(2)}, u32[]{:S(2)}) async-start(bf16[1,4,4,64,192]{4,3,1,0,2:T(8,128)(2,1)} %copy.29), calls=%async_computation | async-start | bytes 1048576 | tf_op jit(solution)/shard_map/all_to_all | solution.py:63
  13.4 108.3 %all-reduce.8.cloned.1.call-start = ((), (), s32[]{:S(2)}) async-start(), calls=%async_computation.2 | async-start | bytes 5308416
  13.4 4.0 %collective-permute-start.3 = (bf16[1,2,1,32,384]{4,3,2,1,0:T(8,128)(2,1)S(1)}, bf16[1,2,1,32,384]{4,3,2,1,0:T(8,128)(2,1)S(1)}, u32[]{:S(2)}, u32[]{:S(2)}) collective-permute-start(bf16[1,2,1,32,384]{4,3,2,1,0:T(8,128)(2,1)S(1)} %slice.163), channel_id=1, source_target_pairs={{0,2},{2,4},{4,6},{1,3},{3,5},{5,7},{8,10},{10,12},{12,14},{9,11},... | collective-permute-start | bytes 147464 | tf_op jit(solution)/shard_map/ppermute | solution.py:12
  17.4 14.1 %collective-permute-start.5 = (bf16[1,6,1,32,384]{4,3,2,1,0:T(8,128)(2,1)S(1)}, bf16[1,6,1,32,384]{4,3,2,1,0:T(8,128)(2,1)S(1)}, u32[]{:S(2)}, u32[]{:S(2)}) collective-permute-start(bf16[1,6,1,32,384]{4,3,2,1,0:T(8,128)(2,1)S(1)} %constant_dynamic-update-slice_fusion.2), channel_id=1, source_target_pairs={{1,0},{3,2},{5,4},{7,6},{9,8},{11,10},{13,12},{15,14},{17,16},{19,... | collective-permute-start | bytes 442376 | tf_op jit(solution)/shard_map/ppermute | solution.py:23
  18.7 12.8 %collective-permute-start.4 = (bf16[1,6,1,32,384]{4,3,2,1,0:T(8,128)(2,1)S(1)}, bf16[1,6,1,32,384]{4,3,2,1,0:T(8,128)(2,1)S(1)}, u32[]{:S(2)}, u32[]{:S(2)}) collective-permute-start(bf16[1,6,1,32,384]{4,3,2,1,0:T(8,128)(2,1)S(1)} %constant_dynamic-update-slice_fusion.2), channel_id=1, source_target_pairs={{0,1},{2,3},{4,5},{6,7},{8,9},{10,11},{12,13},{14,15},{16,17},{18,... | collective-permute-start | bytes 442376 | tf_op jit(solution)/shard_map/ppermute | solution.py:22
  24.0 7.6 %copy-start.1 = (bf16[3,384,768]{2,1,0:T(8,128)(2,1)S(1)}, bf16[3,384,768]{2,1,0:T(8,128)(2,1)}, u32[]{:S(2)}) copy-start(bf16[3,384,768]{2,1,0:T(8,128)(2,1)} %param.7) | copy-start | bytes 5308420
  24.0 7.6 %copy-start.5 = (f32[768]{0:T(1024)S(1)}, f32[768]{0:T(1024)}, u32[]{:S(2)}) copy-start(f32[768]{0:T(1024)} %param.8) | copy-start | bytes 9220
  25.0 29.5 %collective-permute-start.1 = (bf16[1,8,1,64,192]{4,3,2,1,0:T(8,128)(2,1)}, bf16[1,8,1,64,192]{4,3,2,1,0:T(8,128)(2,1)}, u32[]{:S(2)}, u32[]{:S(2)}) collective-permute-start(bf16[1,8,1,64,192]{4,3,2,1,0:T(8,128)(2,1)} %get-tuple-element.19), channel_id=1, source_target_pairs={{1,0},{3,2},{5,4},{7,6},{9,8},{11,10},{13,12},{15,14},{17,16},{19,... | collective-permute-start | bytes 589832 | tf_op jit(solution)/shard_map/ppermute | solution.py:23
  26.3 28.3 %collective-permute-start = (bf16[1,8,1,64,192]{4,3,2,1,0:T(8,128)(2,1)}, bf16[1,8,1,64,192]{4,3,2,1,0:T(8,128)(2,1)S(1)}, u32[]{:S(2)}, u32[]{:S(2)}) collective-permute-start(bf16[1,8,1,64,192]{4,3,2,1,0:T(8,128)(2,1)} %get-tuple-element.18), channel_id=1, source_target_pairs={{0,1},{2,3},{4,5},{6,7},{8,9},{10,11},{12,13},{14,15},{16,17},{18,... | collective-permute-start | bytes 589832 | tf_op jit(solution)/shard_map/ppermute | solution.py:22
  39.7 1.7 copy-start
  52.8 1.3 copy-start.3
  52.8 107.6 %all-reduce.6.cloned.1.call-start = ((), (), s32[]{:S(2)}) async-start(), calls=%async_computation.1 | async-start | bytes 663552 | tf_op jit(solution)/shard_map/psum | solution.py:87
  61.3 2.7 %copy-start.2 = (bf16[3,384,768]{2,1,0:T(8,128)(2,1)S(1)}, bf16[3,384,768]{2,1,0:T(8,128)(2,1)}, u32[]{:S(2)}) copy-start(bf16[3,384,768]{2,1,0:T(8,128)(2,1)} %param.7) | copy-start | bytes 5308420
  62.7 4.2 %collective-permute-start.2 = (bf16[1,2,1,32,768]{4,3,1,2,0:T(8,128)(2,1)S(1)}, bf16[1,2,1,32,768]{4,3,1,2,0:T(8,128)(2,1)S(1)}, u32[]{:S(2)}, u32[]{:S(2)}) collective-permute-start(bf16[1,2,1,32,768]{4,3,1,2,0:T(8,128)(2,1)S(1)} %slice.189), channel_id=1, source_target_pairs={{2,0},{4,2},{6,4},{3,1},{5,3},{7,5},{10,8},{12,10},{14,12},{11,9},... | collective-permute-start | bytes 294920 | tf_op jit(solution)/shard_map/ppermute | solution.py:12
Sparse Core Ops, SparseCore 0:
  52.9 68.7 all-reduce.7
  124.6 35.7 all-reduce.5
where the time goes:
time: 170 us; the launch traced here: 169 us
  waiting for transfers between devices  93.1 us (55%)
  local copies, waits for them, and re-layouts  23.4 us (14%)
  starting transfers between devices  19.8 us (12%)
  between operations  15.2 us (9%)
  matrix products  12 us (7%)
  other arithmetic  5.52 us (3%)
    unnamed x3, waiting for transfers between devices  54.9 us
    psum x1, waiting for transfers between devices, local(): summed = lax.psum(shard, 'clip')  35.7 us
    ppermute x2, starting transfers between devices, extended_2(): before = lax.ppermute(last, axis, up)  9.8 us
    unnamed x21, local copies, waits for them, and re-layouts  6.58 us
    dot_general x9, matrix products, local(): jnp.einsum('cfhwo,io->cfhwi', window, space_weight[tap_row, tap_col], pre...  5.12 us
    reshape x1, local copies, waits for them, and re-layouts, local(): weight_terms = jnp.stack(tap_terms).reshape(-1)  5.02 us
    broadcast_in_dim x2, local copies, waits for them, and re-layouts, local(): jnp.repeat(jnp.repeat(upsampled, 2, axis=2), 2, axis=3)[:, :, 1:up_rows + 3]  4.67 us
    all_to_all x1, starting transfers between devices, local(): lax.all_to_all(pixel_grads, 'row', split_axis=2, concat_axis=1, tiled=True)  4.26 us
  transfers between devices with their start and end apart: 9, of which 3 were waited for; matrix products, arithmetic and copies ran while one was open for 20% of the time, Pallas kernels for 0%

commit v1 on v0

v1 whole, which is shorter than its diff:
```python
import functools
import math

import jax
import jax.numpy as jnp
import numpy as np
from jax import lax
from jax.experimental import pallas as pl
from jax.experimental.pallas import tpu as pltpu
from jax.sharding import PartitionSpec as P

F32 = jnp.float32
BF16 = jnp.bfloat16
VMEM = pl.BlockSpec(memory_space=pltpu.VMEM)
SMEM = pl.BlockSpec(memory_space=pltpu.SMEM)


def struct(shape, dtype):
    return jax.ShapeDtypeStruct(shape, dtype)


def kernel_call(body, outs, n_smem, args, scratch=(), flops=0):
    moved = sum(math.prod(a.shape) * a.dtype.itemsize for a in list(args) + list(outs))
    return pl.pallas_call(
        body,
        out_shape=outs,
        in_specs=[SMEM] * n_smem + [VMEM] * (len(args) - n_smem),
        out_specs=[VMEM] * len(outs),
        scratch_shapes=list(scratch),
        cost_estimate=pl.CostEstimate(flops=flops, bytes_accessed=moved, transcendentals=0),
    )(*args)


def box_matrix(width):
    a, b, s = np.meshgrid(np.arange(3), np.arange(3), np.arange(width), indexing="ij")
    a, b, s = (x.reshape(-1, 1) for x in (a, b, s))
    row, col = np.meshgrid(np.arange(4), np.arange(2 * width), indexing="ij")
    row, col = (x.reshape(1, -1) for x in (row, col))
    dr, dc = row - (2 - a), col - (2 * s + 1 - b)
    return ((dr >= 0) & (dr <= 1) & (dc >= 0) & (dc <= 1)).astype(np.float32)


def box_kernel(sizes, grads, weight, box, g_out, *rest):
    S, HR, W, C, CO, r, n_row = sizes
    bands, padded = rest[: n_row], rest[n_row]
    acts = rest[n_row + 1]
    line = 2 * W
    for s in range(S):
        padded[s, 0:line, :] = jnp.zeros((line, CO), BF16)
        padded[s, line : line * (2 * HR + 1), :] = grads[s]
        padded[s, line * (2 * HR + 1) :, :] = jnp.zeros((line, CO), BF16)
    matrix = box[...]
    for s in range(S):
        for R in range(HR):
            window = padded[s, 2 * R * line : (2 * R + 4) * line, :]
            sums = jnp.dot(matrix, window, preferred_element_type=F32).astype(BF16)
            at = (s * HR + R) * W
            for t in range(9):
                g_out[t, at : at + W, :] = sums[t * W : (t + 1) * W]
    total = jnp.zeros((S * HR * W, C), F32)
    for t in range(9):
        total = total + lax.dot_general(
            g_out[t], weight[t], (((1,), (1,)), ((), ())), preferred_element_type=F32
        )
    acts[...] = total.astype(BF16).reshape(S, HR * W, C)
    me = lax.axis_index("row")
    for d in range(n_row):
        start = pl.multiple_of(lax.rem(me + d, n_row) * (r * W), r * W)
        bands[d][...] = acts[:, pl.ds(start, r * W), :]


def wgrad_kernel(sizes, plan, order, bias, time_weight, g, *rest):
    S, HR, W, C, CO, r, n_row, F = sizes
    own, prior = rest[:n_row], rest[n_row : 2 * n_row]
    n_out = 2 if plan else 1
    outs = rest[2 * n_row : 2 * n_row + n_out]
    ext, acts, picked, terms = rest[2 * n_row + n_out :]
    me = lax.axis_index("row")
    for d in range(n_row):
        source = lax.rem(me - d + n_row, n_row)
        for f in range(F + 2):
            block = prior[d][f] if f < 2 else own[d][f - 2]
            start = pl.multiple_of((f * HR + source * r) * W, W)
            ext[pl.ds(start, r * W), :] = block
    step = HR * W
    total = jnp.broadcast_to(bias[...], (F * step, 2 * C))
    for k in range(3):
        total = total + jnp.dot(
            ext[k * step : (k + F) * step, :], time_weight[k], preferred_element_type=F32
        )
    rounded = total.astype(BF16)
    acts[0] = rounded[:, :C]
    acts[1] = rounded[:, C:]
    for s in range(S):
        o = order[me * S + s]
        start = pl.multiple_of((o // 2) * step, step)
        picked[s * step : (s + 1) * step, :] = acts[o % 2, pl.ds(start, step), :]
    left = picked[...].astype(F32).T.astype(BF16)
    target = terms if plan else outs[0]
    for t in range(9):
        target[t * C : (t + 1) * C, :] = jnp.dot(left, g[t], preferred_element_type=F32)
    if plan:
        n_q, chunk = plan
        core = lax.rem(lax.axis_index("frame"), 2)
        keep, send = outs
        half, low = chunk // 2, CO - 128
        for q in range(n_q):
            for which, out in ((core, keep), (1 - core, send)):
                index = ((q // n_row) * 2 + which) * n_row + q % n_row
                rows = terms[pl.ds(pl.multiple_of(index * chunk, chunk), chunk), :].astype(out.dtype)
                out[q, :chunk, :] = rows[:, :128]
                out[q, chunk:, :] = jnp.concatenate([rows[:half, 128:], rows[half:, 128:]], axis=1)


def join_kernel(n_q, n_row, keep, got, own, *sends):
    q = (lax.axis_index("frame") // 2) * n_row + lax.axis_index("row")
    own[...] = keep[q] + got[q].astype(F32)
    for d in range(1, n_q):
        p = jnp.bitwise_xor(q, d)
        sends[d - 1][...] = (keep[p] + got[p].astype(F32)).astype(BF16)


def square_kernel(n_q, n_clip, base, size, keep, *rest):
    got, mine, sends = rest[: n_q - 1], rest[n_q - 1], rest[n_q : n_q + n_clip - 1]
    total = rest[-1]
    value = keep[...]
    for block in got:
        value = value + block[...].astype(F32)
    total[...] = value
    z = lax.axis_index("clip")
    for d in range(n_clip):
        to = lax.rem(z + d, n_clip)
        piece = total[pl.ds(pl.multiple_of(to * base, 8), size), :]
        if d == 0:
            mine[...] = piece
        else:
            sends[d - 1][...] = piece.astype(BF16)


def piece_kernel(scale, mine, *rest):
    value = mine[...]
    for block in rest[:-1]:
        value = value + block[...].astype(F32)
    rest[-1][...] = (value * scale).astype(BF16)


def final_kernel(n_clip, base, size, chunk, CO, mine, *rest):
    got, out, total, even = rest[: n_clip - 1], rest[n_clip - 1], rest[n_clip], rest[n_clip + 1]
    z = lax.axis_index("clip")
    for d in range(n_clip):
        source = lax.rem(z - d + n_clip, n_clip)
        block = mine if d == 0 else got[d - 1]
        start = pl.multiple_of(source * base, 8)
        total[pl.ds(start, base), :] = block[:base].astype(F32)

        @pl.when(source == n_clip - 1)
        def _():
            total[n_clip * base :, :] = block[base:].astype(F32)

    half, low = chunk // 2, CO - 128
    side = total[chunk:]
    even[:half, :low] = side[:, :low]
    even[half:, :low] = side[:, low:]
    a, b = (total[pl.ds(p, half, stride=2), :] for p in range(2))
    a_side, b_side = (even[pl.ds(p, half, stride=2), :][:, :low] for p in range(2))
    out[pl.ds(0, half, stride=3), :] = a
    out[pl.ds(1, half, stride=3), :] = jnp.concatenate([a_side, b[:, :low]], axis=1)
    out[pl.ds(2, half, stride=3), :] = jnp.concatenate([b[:, low:], b_side], axis=1)


def order_kernel(sizes, order, *rest):
    S, rW, n_row, F = sizes
    bands, natural, first = rest[:n_row], rest[n_row], rest[n_row + 1]
    me = lax.axis_index("row")
    for d in range(n_row):
        source = lax.rem(me - d + n_row, n_row)
        for s in range(S):
            o = order[source * S + s]
            start = pl.multiple_of((o // 2) * rW, rW)
            natural[o % 2, pl.ds(start, rW), :] = bands[d][s]
    first[...] = natural[:, : 2 * rW, :]


def input_kernel(sizes, natural, later, time_weight, out, tail):
    rW, F, C = sizes
    tail[:, : F * rW, :] = natural[...]
    tail[:, F * rW :, :] = later[...]
    total = jnp.zeros((F * rW, C), F32)
    for k in range(3):
        for p in range(2):
            total = total + lax.dot_general(
                tail[p, (2 - k) * rW : (2 - k + F) * rW, :],
                time_weight[k, :, p * C : (p + 1) * C],
                (((1,), (1,)), ((), ())),
                preferred_element_type=F32,
            )
    out[...] = total.astype(BF16)


def local(features, time_weight, time_bias, space_weight, pixel_grads, frame_order):
    _, F, r, W, C = features.shape
    _, S, UR, UW, CO = pixel_grads.shape
    n_row, n_frame, n_clip = (lax.axis_size(a) for a in ("row", "frame", "clip"))
    HR, rW = r * n_row, r * W
    pixels = S * HR * W
    order = frame_order.reshape(-1)
    both = ("frame", "row")

    feats = features.reshape(F, rW, C)
    last = feats[F - 2 :]
    own, prior = [feats], []
    for d in range(1, n_row):
        own.append(lax.ppermute(feats, "row", [(i, (i + d) % n_row) for i in range(n_row)]))
    for d in range(n_row):
        route = [
            (f * n_row + i, (f + 1) * n_row + (i + d) % n_row)
            for f in range(n_frame - 1)
            for i in range(n_row)
        ]
        prior.append(lax.ppermute(last, both, route))

    box = jnp.asarray(box_matrix(W), BF16)
    g, *bands = kernel_call(
        functools.partial(box_kernel, (S, HR, W, C, CO, r, n_row)),
        [struct((9, pixels, CO), BF16)] + [struct((S, rW, C), BF16)] * n_row,
        0,
        [pixel_grads.reshape(S, UR * UW, CO), space_weight.reshape(9, C, CO), box],
        [pltpu.VMEM((S, (UR + 2) * UW, CO), BF16), pltpu.VMEM((S, HR * W, C), BF16)],
        flops=2 * pixels * 9 * C * CO,
    )

    n_total = 9 * C
    n_dev = n_frame * n_row
    n_q = n_dev // 2
    chunk = n_total // n_dev
    fast = (
        n_frame % 2 == 0
        and n_total % n_dev == 0
        and chunk % 16 == 0
        and 1 < n_q <= 8
        and n_q & (n_q - 1) == 0
        and n_clip > 1
        and 128 < CO == 192
    )
    wg_sizes = (S, HR, W, C, CO, r, n_row, F)
    packed = chunk * CO // 128
    wg = kernel_call(
        functools.partial(wgrad_kernel, wg_sizes, (n_q, chunk) if fast else None),
        [struct((n_q, packed, 128), F32), struct((n_q, packed, 128), BF16)]
        if fast
        else [struct((n_total, CO), F32)],
        1,
        [order, time_bias.reshape(1, -1), time_weight, g] + own + prior,
        [
            pltpu.VMEM(((F + 2) * HR * W, C), BF16),
            pltpu.VMEM((2, F * HR * W, C), BF16),
            pltpu.VMEM((pixels, C), BF16),
            pltpu.VMEM((n_total if fast else 8, CO), F32),
        ],
        flops=2 * pixels * 9 * C * CO + 2 * F * HR * W * 6 * C * C,
    )

    scale = 1.0 / math.sqrt(2 * F * UR * UW * n_clip * n_frame)
    if fast:
        keep, send = wg
        got = lax.ppermute(
            send, both, [(i, ((i // n_row) ^ 1) * n_row + i % n_row) for i in range(n_dev)]
        )
        mine, *sends = kernel_call(
            functools.partial(join_kernel, n_q, n_row),
            [struct((packed, 128), F32)] + [struct((packed, 128), BF16)] * (n_q - 1),
            0,
            [keep, got],
        )

        def square(i, d):
            f, j = i // n_row, i % n_row
            p = ((f // 2) * n_row + j) ^ d
            return ((p // n_row) * 2 + f % 2) * n_row + p % n_row

        got = [
            lax.ppermute(sends[d - 1], both, [(i, square(i, d)) for i in range(n_dev)])
            for d in range(1, n_q)
        ]
        base = packed // n_clip // 8 * 8
        size = packed - base * (n_clip - 1)
        mine, *sends = kernel_call(
            functools.partial(square_kernel, n_q, n_clip, base, size),
            [struct((size, 128), F32)] + [struct((size, 128), BF16)] * (n_clip - 1),
            0,
            [mine] + got,
            [pltpu.VMEM((packed, 128), F32)],
        )
        shift = [[(i, (i + d) % n_clip) for i in range(n_clip)] for d in range(1, n_clip)]
        got = [lax.ppermute(x, "clip", route) for x, route in zip(sends, shift)]
        (mine,) = kernel_call(
            functools.partial(piece_kernel, scale), [struct((size, 128), BF16)], 0, [mine] + got
        )
        got = [lax.ppermute(mine, "clip", route) for route in shift]
        (flat,) = kernel_call(
            functools.partial(final_kernel, n_clip, base, size, chunk, CO),
            [struct((packed, 128), F32)],
            0,
            [mine] + got,
            [pltpu.VMEM((packed, 128), F32), pltpu.VMEM((chunk, 128), F32)],
        )
        weight_grad = flat.reshape(-1)
    else:
        shard = lax.psum_scatter(wg[0].reshape(-1), both, scatter_dimension=0, tiled=True)
        weight_grad = lax.psum(shard, "clip") * scale

    bands = [bands[0]] + [
        lax.ppermute(bands[d], "row", [(i, (i + d) % n_row) for i in range(n_row)])
        for d in range(1, n_row)
    ]
    natural, first = kernel_call(
        functools.partial(order_kernel, (S, rW, n_row, F)),
        [struct((2, F * rW, C), BF16), struct((2, 2 * rW, C), BF16)],
        1,
        [order] + bands,
    )
    later = lax.ppermute(first, "frame", [(i + 1, i) for i in range(n_frame - 1)])
    (input_grad,) = kernel_call(
        functools.partial(input_kernel, (rW, F, C)),
        [struct((F * rW, C), BF16)],
        0,
        [natural, later, time_weight],
        [pltpu.VMEM((2, (F + 2) * rW, C), BF16)],
        flops=2 * F * rW * 6 * C * C,
    )
    return input_grad.reshape(features.shape), weight_grad


def solution(mesh):
    return jax.shard_map(
        local,
        mesh=mesh,
        in_specs=(
            P("clip", "frame", "row", None, None),
            P(),
            P(),
            P(),
            P("clip", ("frame", "row"), None, None, None),
            P("clip", "frame", None),
        ),
        out_specs=(P("clip", "frame", "row", None, None), P(("frame", "row"))),
        check_vma=False,
    )
```

time: 170 us -> 71.4 us (0.42)
  waiting for transfers between devices: 93.1 us -> 14.3 us
  Pallas kernels: 0 us -> 21.4 us
  between operations: 15.2 us -> 0.76 us
  local copies, waits for them, and re-layouts: 23.4 us -> 10.5 us
  matrix products: 12 us -> 0 us
  other arithmetic: 5.52 us -> 0 us
  starting transfers between devices: 19.8 us -> 23.9 us
    unnamed x3 -> x0, waiting for transfers between devices: 54.9 us -> none
    psum x1 -> x0, waiting for transfers between devices: 35.7 us -> none  [local(): summed = lax.psum(shard, 'clip')]
    pallas_call x0 -> x8, Pallas kernels: none -> 21.4 us  [kernel_call(): pl.pallas_call(body, out_shape=outs, in_specs=[SMEM] * n_smem + [VMEM] *...]
    dot_general x24 -> x0, matrix products: 12 us -> none  [the longest x9 5.12 us: local(): jnp.einsum('cfhwo,io->cfhwi', window, space_weight[tap_row, tap_col], pre...]
    ppermute x6 -> x15, waiting for transfers between devices: 2.55 us -> 14.3 us  [the longest x1 7.13 us: local(): lax.ppermute(bands[d], 'row', [(i, (i + d) % n_row) for i in range(n_row)])]
    ppermute x6 -> x15, starting transfers between devices: 15.4 us -> 23.9 us  [the longest x3 5.52 us: local(): got = [lax.ppermute(x, 'clip', route) for x, route in zip(sends, shift)]]
    broadcast_in_dim x3 -> x0, local copies, waits for them, and re-layouts: 4.79 us -> none  [the longest x2 4.67 us: local(): jnp.repeat(jnp.repeat(upsampled, 2, axis=2), 2, axis=3)[:, :, 1:up_rows + 3]]
    all_to_all x1 -> x0, starting transfers between devices: 4.26 us -> none  [local(): lax.all_to_all(pixel_grads, 'row', split_axis=2, concat_axis=1, tiled=True)]
  transfers between devices with their start and end apart: 9 -> 15, of which waited for: 3 -> 7; matrix products, arithmetic and copies ran while one was open for 20% -> 8% of each run, Pallas kernels for 0% -> 16%
where the time goes in v1:
time: 71.4 us; the launch traced here: 70.9 us
  starting transfers between devices  23.9 us (33%)
  Pallas kernels  21.4 us (30%)
  waiting for transfers between devices  14.3 us (20%)
  local copies, waits for them, and re-layouts  10.5 us (15%)
  between operations  0.76 us (1%)
    pallas_call x8, Pallas kernels, kernel_call(): pl.pallas_call(body, out_shape=outs, in_specs=[SMEM] * n_smem + [VMEM] *...  21.4 us
    unnamed x33, local copies, waits for them, and re-layouts  8.38 us
    ppermute x1, waiting for transfers between devices, local(): lax.ppermute(bands[d], 'row', [(i, (i + d) % n_row) for i in range(n_row)])  7.13 us
    ppermute x3, starting transfers between devices, local(): got = [lax.ppermute(x, 'clip', route) for x, route in zip(sends, shift)]  5.52 us
    ppermute x2, starting transfers between devices, local(): prior.append(lax.ppermute(last, both, route))  5.35 us
    ppermute x3, starting transfers between devices, local(): got = [lax.ppermute(mine, 'clip', route) for route in shift]  3.54 us
    ppermute x3, starting transfers between devices, local(): lax.ppermute(sends[d - 1], both, [(i, square(i, d)) for i in range(n_dev)])  3.49 us
    ppermute x3, waiting for transfers between devices, local(): got = [lax.ppermute(x, 'clip', route) for x, route in zip(sends, shift)]  3.11 us
  transfers between devices with their start and end apart: 15, of which 7 were waited for; matrix products, arithmetic and copies ran while one was open for 8% of the time, Pallas kernels for 16%

profile of v1, /device:TPU:0, one launch (start us, length us, event | category | flops | bytes accessed | tf_op | source)
XLA Modules:
  0.0 70.9 jit_solution(13839112128420707400)
XLA Ops:
  0.6 3.1 %collective-permute-start.2 = (bf16[4,32,384]{2,1,0:T(8,128)(2,1)}, bf16[4,32,384]{2,1,0:T(8,128)(2,1)S(1)}, u32[]{:S(2)}, u32[]{:S(2)}) collective-permute-start(bf16[4,32,384]{2,1,0:T(8,128)(2,1)} %bitcast.14), channel_id=1, source_target_pairs={{0,1},{1,0},{2,3},{3,2},{4,5},{5,4},{6,7},{7,6},{8,9},{9,8},{10,11... | collective-permute-start | bytes 294920 | tf_op jit(solution)/shard_map/ppermute | solution.py:213
  3.7 0.8 %slice_bitcast_fusion = bf16[2,32,384]{2,1,0:T(8,128)(2,1)S(1)} fusion(bf16[1,4,1,32,384]{4,3,1,2,0:T(8,128)(2,1)} %bitcast.15), kind=kLoop, calls=%fused_computation | loop fusion | bytes 98304 | tf_op jit(solution)/shard_map/slice | solution.py:210
  4.5 1.3 %collective-permute-start.4 = (bf16[2,32,384]{2,1,0:T(8,128)(2,1)S(1)}, bf16[2,32,384]{2,1,0:T(8,128)(2,1)S(1)}, u32[]{:S(2)}, u32[]{:S(2)}) collective-permute-start(bf16[2,32,384]{2,1,0:T(8,128)(2,1)S(1)} %slice_bitcast_fusion), channel_id=1, source_target_pairs={{0,3},{1,2},{2,5},{3,4},{4,7},{5,6},{8,11},{9,10},{10,13},{11,12},... | collective-permute-start | bytes 147464 | tf_op jit(solution)/shard_map/ppermute | solution.py:220
  5.9 4.0 %collective-permute-start.3 = (bf16[2,32,384]{2,1,0:T(8,128)(2,1)S(1)}, bf16[2,32,384]{2,1,0:T(8,128)(2,1)S(1)}, u32[]{:S(2)}, u32[]{:S(2)}) collective-permute-start(bf16[2,32,384]{2,1,0:T(8,128)(2,1)S(1)} %slice_bitcast_fusion), channel_id=1, source_target_pairs={{0,2},{1,3},{2,4},{3,5},{4,6},{5,7},{8,10},{9,11},{10,12},{11,13},... | collective-permute-start | bytes 147464 | tf_op jit(solution)/shard_map/ppermute | solution.py:220
  9.9 1.3 %reshape.30.bias = f32[1,768]{1,0:T(1,128)} reshape(f32[768]{0:T(1024)} %param.9) | data formatting | bytes 6144 | tf_op jit(solution)/shard_map/reshape | solution.py:253
  11.2 3.6 %copy.9 = bf16[3,3,384,192]{3,2,1,0:T(8,128)(2,1)} copy(bf16[3,3,384,192]{2,3,1,0:T(8,128)(2,1)} %param.10) | data formatting | bytes 2654208 | tf_op args[3]
  14.8 3.4 %shard_map.86 = (bf16[9,256,192]{2,1,0:T(8,128)(2,1)}, bf16[4,32,384]{2,1,0:T(8,128)(2,1)}, bf16[4,32,384]{2,1,0:T(8,128)(2,1)}) custom-call(bf16[4,256,192]{2,1,0:T(8,128)(2,1)} %bitcast.12, bf16[9,384,192]{2,1,0:T(8,128)(2,1)} %bitcast.11, bf16[288,256]{1,0:T(8,128)(2,1)} %constant.2.clone.box), custom_call_target="tpu_custom_call" | custom-call | flops 339738624 | bytes 2949120 | tf_op jit(solution)/shard_map/pallas_call | solution.py:24
  18.3 0.0 collective-permute-done.4.rest_3_
  18.3 0.0 collective-permute-done.2.rest_1_
  18.3 0.0 copy-start.5
  18.3 0.6 copy-done.7
  18.9 0.0 copy-done.8
  18.9 0.0 copy-done.5
  18.9 5.5 %shard_map.89 = (f32[4,648,128]{2,1,0:T(8,128)}, bf16[4,648,128]{2,1,0:T(8,128)(2,1)}) custom-call(s32[8]{0:T(128)} %bitcast.18, f32[1,768]{1,0:T(1,128)} %reshape.30.bias, bf16[3,384,768]{2,1,0:T(8,128)(2,1)} %time_weight.3, bf16[9,256,192]{2,1,0:T(8,128)(2,1)} %get-tuple-element.21.g, bf16[4,32,384]{2,1,0:T(8,128)(2,1)} %bitcast.16, ...), custom_call_target="tpu_custom_call" | custom-call | flops 792723456 | bytes 4942880 | tf_op jit(solution)/shard_map/pallas_call | solution.py:24
  24.5 0.1 collective-permute-start.5
  24.5 2.2 %collective-permute-done.5.got = bf16[4,648,128]{2,1,0:T(8,128)(2,1)S(1)} collective-permute-done((bf16[4,648,128]{2,1,0:T(8,128)(2,1)}, bf16[4,648,128]{2,1,0:T(8,128)(2,1)S(1)}, u32[]{:S(2)}, u32[]{:S(2)}) %collective-permute-start.5) | collective-permute-done | bytes 663584 | tf_op jit(solution)/shard_map/ppermute | solution.py:266
  26.8 0.8 %copy-done = bf16[4,648,128]{2,1,0:T(8,128)(2,1)} copy-done((bf16[4,648,128]{2,1,0:T(8,128)(2,1)}, bf16[4,648,128]{2,1,0:T(8,128)(2,1)S(1)}, u32[]{:S(2)}) %copy-start) | copy-done | bytes 663576
  27.6 2.5 %shard_map.90 = (f32[648,128]{1,0:T(8,128)}, bf16[648,128]{1,0:T(8,128)(2,1)}, bf16[648,128]{1,0:T(8,128)(2,1)}, bf16[648,128]{1,0:T(8,128)(2,1)}) custom-call(f32[4,648,128]{2,1,0:T(8,128)} %get-tuple-element.22.keep, bf16[4,648,128]{2,1,0:T(8,128)(2,1)} %copy-done), custom_call_target="tpu_custom_call" | custom-call | bytes 2820096 | tf_op jit(solution)/shard_map/pallas_call | solution.py:24
  30.1 1.5 %collective-permute-start.6 = (bf16[648,128]{1,0:T(8,128)(2,1)}, bf16[648,128]{1,0:T(8,128)(2,1)S(1)}, u32[]{:S(2)}, u32[]{:S(2)}) collective-permute-start(bf16[648,128]{1,0:T(8,128)(2,1)} %get-tuple-element.25), channel_id=1, source_target_pairs={{0,1},{1,0},{2,3},{3,2},{4,5},{5,4},{6,7},{7,6},{8,9},{9,8},{10,11... | collective-permute-start | bytes 497672 | tf_op jit(solution)/shard_map/ppermute | solution.py:282
  31.6 0.0 collective-permute-start.7
  31.6 1.9 %collective-permute-start.8 = (bf16[648,128]{1,0:T(8,128)(2,1)}, bf16[648,128]{1,0:T(8,128)(2,1)S(1)}, u32[]{:S(2)}, u32[]{:S(2)}) collective-permute-start(bf16[648,128]{1,0:T(8,128)(2,1)} %get-tuple-element.27), channel_id=1, source_target_pairs={{0,5},{1,4},{2,7},{3,6},{4,1},{5,0},{6,3},{7,2},{8,13},{9,12},{10,... | collective-permute-start | bytes 497672 | tf_op jit(solution)/shard_map/ppermute | solution.py:282
  33.6 1.5 %collective-permute-start = (bf16[4,32,384]{2,1,0:T(8,128)(2,1)S(1)}, bf16[4,32,384]{2,1,0:T(8,128)(2,1)S(1)}, u32[]{:S(2)}, u32[]{:S(2)}) collective-permute-start(bf16[4,32,384]{2,1,0:T(8,128)(2,1)S(1)} %copy-done.15), channel_id=1, source_target_pairs={{0,1},{1,0},{2,3},{3,2},{4,5},{5,4},{6,7},{7,6},{8,9},{9,8},{10,11... | collective-permute-start | bytes 294920 | tf_op jit(solution)/shard_map/ppermute | solution.py:313
  35.1 7.1 %collective-permute-done.rest_1_ = bf16[4,32,384]{2,1,0:T(8,128)(2,1)S(1)} collective-permute-done((bf16[4,32,384]{2,1,0:T(8,128)(2,1)S(1)}, bf16[4,32,384]{2,1,0:T(8,128)(2,1)S(1)}, u32[]{:S(2)}, u32[]{:S(2)}) %collective-permute-start) | collective-permute-done | bytes 98336 | tf_op jit(solution)/shard_map/ppermute | solution.py:313
  42.2 0.6 copy-done.6
  42.9 1.7 %shard_map.87 = (bf16[2,128,384]{2,1,0:T(8,128)(2,1)}, bf16[2,64,384]{2,1,0:T(8,128)(2,1)}) custom-call(s32[8]{0:T(128)} %bitcast.19, bf16[4,32,384]{2,1,0:T(8,128)(2,1)} %get-tuple-element.17.rest_0_, bf16[4,32,384]{2,1,0:T(8,128)(2,1)} %copy-done.6), custom_call_target="tpu_custom_call" | custom-call | bytes 491552 | tf_op jit(solution)/shard_map/pallas_call | solution.py:24
  44.6 1.3 %collective-permute-start.1 = (bf16[2,64,384]{2,1,0:T(8,128)(2,1)}, bf16[2,64,384]{2,1,0:T(8,128)(2,1)S(1)}, u32[]{:S(2)}, u32[]{:S(2)}) collective-permute-start(bf16[2,64,384]{2,1,0:T(8,128)(2,1)} %get-tuple-element.20), channel_id=1, source_target_pairs={{2,0},{4,2},{6,4},{3,1},{5,3},{7,5},{10,8},{12,10},{14,12},{11,9},... | collective-permute-start | bytes 294920 | tf_op jit(solution)/shard_map/ppermute | solution.py:322
  45.9 0.0 collective-permute-done.6.rest_0_
  45.9 0.6 copy-done.1
  46.6 0.1 copy-done.2
  46.6 0.1 copy-done.3
  46.7 1.9 %shard_map.91 = (f32[168,128]{1,0:T(8,128)}, bf16[168,128]{1,0:T(8,128)(2,1)}, bf16[168,128]{1,0:T(8,128)(2,1)}, bf16[168,128]{1,0:T(8,128)(2,1)}) custom-call(f32[648,128]{1,0:T(8,128)} %get-tuple-element.24.keep, bf16[648,128]{1,0:T(8,128)(2,1)} %copy-done.1, bf16[648,128]{1,0:T(8,128)(2,1)} %copy-done.2, bf16[648,128]{1,0:T(8,128)(2,1)} %copy-done.3), custom_call_target="tpu_custom_call" | custom-call | bytes 1044480 | tf_op jit(solution)/shard_map/pallas_call | solution.py:24
  48.6 1.6 %collective-permute-start.9 = (bf16[168,128]{1,0:T(8,128)(2,1)}, bf16[168,128]{1,0:T(8,128)(2,1)S(1)}, u32[]{:S(2)}, u32[]{:S(2)}) collective-permute-start(bf16[168,128]{1,0:T(8,128)(2,1)} %get-tuple-element.29), channel_id=1, source_target_pairs={{0,8},{8,16},{16,24},{24,0},{1,9},{9,17},{17,25},{25,1},{2,10},{10... | collective-permute-start | bytes 129032 | tf_op jit(solution)/shard_map/ppermute | solution.py:295
  50.2 2.6 %collective-permute-start.10 = (bf16[168,128]{1,0:T(8,128)(2,1)}, bf16[168,128]{1,0:T(8,128)(2,1)S(1)}, u32[]{:S(2)}, u32[]{:S(2)}) collective-permute-start(bf16[168,128]{1,0:T(8,128)(2,1)} %get-tuple-element.30), channel_id=1, source_target_pairs={{0,16},{8,24},{16,0},{24,8},{1,17},{9,25},{17,1},{25,9},{2,18},{10... | collective-permute-start | bytes 129032 | tf_op jit(solution)/shard_map/ppermute | solution.py:295
  52.8 1.4 %collective-permute-start.11 = (bf16[168,128]{1,0:T(8,128)(2,1)}, bf16[168,128]{1,0:T(8,128)(2,1)S(1)}, u32[]{:S(2)}, u32[]{:S(2)}) collective-permute-start(bf16[168,128]{1,0:T(8,128)(2,1)} %get-tuple-element.31), channel_id=1, source_target_pairs={{0,24},{8,0},{16,8},{24,16},{1,25},{9,1},{17,9},{25,17},{2,26},{10... | collective-permute-start | bytes 129032 | tf_op jit(solution)/shard_map/ppermute | solution.py:295
  54.2 0.8 %collective-permute-done.9.rest_0_ = bf16[168,128]{1,0:T(8,128)(2,1)S(1)} collective-permute-done((bf16[168,128]{1,0:T(8,128)(2,1)}, bf16[168,128]{1,0:T(8,128)(2,1)S(1)}, u32[]{:S(2)}, u32[]{:S(2)}) %collective-permute-start.9) | collective-permute-done | bytes 43040 | tf_op jit(solution)/shard_map/ppermute | solution.py:295
  54.9 2.2 %collective-permute-done.10.rest_1_ = bf16[168,128]{1,0:T(8,128)(2,1)S(1)} collective-permute-done((bf16[168,128]{1,0:T(8,128)(2,1)}, bf16[168,128]{1,0:T(8,128)(2,1)S(1)}, u32[]{:S(2)}, u32[]{:S(2)}) %collective-permute-start.10) | collective-permute-done | bytes 43040 | tf_op jit(solution)/shard_map/ppermute | solution.py:295
  57.1 0.2 collective-permute-done.11.rest_2_
  57.3 0.4 copy-done.10
  57.7 0.2 copy-done.11
  57.9 1.6 %shard_map.92.mine = bf16[168,128]{1,0:T(8,128)(2,1)} custom-call(f32[168,128]{1,0:T(8,128)} %get-tuple-element.28.mine, bf16[168,128]{1,0:T(8,128)(2,1)} %copy-done.9, bf16[168,128]{1,0:T(8,128)(2,1)} %copy-done.10, bf16[168,128]{1,0:T(8,128)(2,1)} %copy-done.11), custom_call_target="tpu_custom_call" | custom-call | bytes 258048 | tf_op jit(solution)/shard_map/pallas_call | solution.py:24
  59.4 3.0 %collective-permute-start.14 = (bf16[168,128]{1,0:T(8,128)(2,1)}, bf16[168,128]{1,0:T(8,128)(2,1)S(1)}, u32[]{:S(2)}, u32[]{:S(2)}) collective-permute-start(bf16[168,128]{1,0:T(8,128)(2,1)} %shard_map.92.mine), channel_id=1, source_target_pairs={{0,24},{8,0},{16,8},{24,16},{1,25},{9,1},{17,9},{25,17},{2,26},{10... | collective-permute-start | bytes 129032 | tf_op jit(solution)/shard_map/ppermute | solution.py:299
  62.4 0.6 collective-permute-start.12
  63.0 0.6 copy-done.4
  63.6 3.0 %shard_map.88 = bf16[128,384]{1,0:T(8,128)(2,1)} custom-call(bf16[2,128,384]{2,1,0:T(8,128)(2,1)} %get-tuple-element.19.natural, bf16[2,64,384]{2,1,0:T(8,128)(2,1)} %copy-done.4, bf16[3,384,768]{2,1,0:T(8,128)(2,1)} %time_weight.3), custom_call_target="tpu_custom_call" | custom-call | flops 226492416 | bytes 2162688 | tf_op jit(solution)/shard_map/pallas_call | solution.py:24
  66.7 0.9 %collective-permute-done.13.rest_1_ = bf16[168,128]{1,0:T(8,128)(2,1)S(1)} collective-permute-done((bf16[168,128]{1,0:T(8,128)(2,1)}, bf16[168,128]{1,0:T(8,128)(2,1)S(1)}, u32[]{:S(2)}, u32[]{:S(2)}) %collective-permute-start.13) | collective-permute-done | bytes 43040 | tf_op jit(solution)/shard_map/ppermute | solution.py:299
  67.6 0.9 %collective-permute-done.12.rest_0_ = bf16[168,128]{1,0:T(8,128)(2,1)S(1)} collective-permute-done((bf16[168,128]{1,0:T(8,128)(2,1)}, bf16[168,128]{1,0:T(8,128)(2,1)S(1)}, u32[]{:S(2)}, u32[]{:S(2)}) %collective-permute-start.12) | collective-permute-done | bytes 43040 | tf_op jit(solution)/shard_map/ppermute | solution.py:299
  68.5 0.6 copy-done.14
  69.1 1.8 %shard_map.93 = f32[648,128]{1,0:T(8,128)} custom-call(bf16[168,128]{1,0:T(8,128)(2,1)} %shard_map.92.mine, bf16[168,128]{1,0:T(8,128)(2,1)} %copy-done.14, bf16[168,128]{1,0:T(8,128)(2,1)} %copy-done.13, bf16[168,128]{1,0:T(8,128)(2,1)} %copy-done.12), custom_call_target="tpu_custom_call" | custom-call | bytes 503808 | tf_op jit(solution)/shard_map/pallas_call | solution.py:24
  (25 shorter events, 0.1 us)
Async XLA Ops:
  0.6 17.7 %collective-permute-start.2 = (bf16[4,32,384]{2,1,0:T(8,128)(2,1)}, bf16[4,32,384]{2,1,0:T(8,128)(2,1)S(1)}, u32[]{:S(2)}, u32[]{:S(2)}) collective-permute-start(bf16[4,32,384]{2,1,0:T(8,128)(2,1)} %bitcast.14), channel_id=1, source_target_pairs={{0,1},{1,0},{2,3},{3,2},{4,5},{5,4},{6,7},{7,6},{8,9},{9,8},{10,11... | collective-permute-start | bytes 294920 | tf_op jit(solution)/shard_map/ppermute | solution.py:213
  4.5 13.7 %collective-permute-start.4 = (bf16[2,32,384]{2,1,0:T(8,128)(2,1)S(1)}, bf16[2,32,384]{2,1,0:T(8,128)(2,1)S(1)}, u32[]{:S(2)}, u32[]{:S(2)}) collective-permute-start(bf16[2,32,384]{2,1,0:T(8,128)(2,1)S(1)} %slice_bitcast_fusion), channel_id=1, source_target_pairs={{0,3},{1,2},{2,5},{3,4},{4,7},{5,6},{8,11},{9,10},{10,13},{11,12},... | collective-permute-start | bytes 147464 | tf_op jit(solution)/shard_map/ppermute | solution.py:220
  5.9 12.4 %collective-permute-start.3 = (bf16[2,32,384]{2,1,0:T(8,128)(2,1)S(1)}, bf16[2,32,384]{2,1,0:T(8,128)(2,1)S(1)}, u32[]{:S(2)}, u32[]{:S(2)}) collective-permute-start(bf16[2,32,384]{2,1,0:T(8,128)(2,1)S(1)} %slice_bitcast_fusion), channel_id=1, source_target_pairs={{0,2},{1,3},{2,4},{3,5},{4,6},{5,7},{8,10},{9,11},{10,12},{11,13},... | collective-permute-start | bytes 147464 | tf_op jit(solution)/shard_map/ppermute | solution.py:220
  18.3 0.6 copy-start.7
  18.3 0.6 copy-start.8
  18.3 0.6 copy-start.5
  24.4 9.1 %copy-start.15 = (bf16[4,32,384]{2,1,0:T(8,128)(2,1)S(1)}, bf16[4,32,384]{2,1,0:T(8,128)(2,1)}, u32[]{:S(2)}) copy-start(bf16[4,32,384]{2,1,0:T(8,128)(2,1)} %get-tuple-element.18) | copy-start | bytes 294916
  24.5 2.3 %collective-permute-start.5 = (bf16[4,648,128]{2,1,0:T(8,128)(2,1)}, bf16[4,648,128]{2,1,0:T(8,128)(2,1)S(1)}, u32[]{:S(2)}, u32[]{:S(2)}) collective-permute-start(bf16[4,648,128]{2,1,0:T(8,128)(2,1)} %get-tuple-element.23), channel_id=1, source_target_pairs={{0,2},{1,3},{2,0},{3,1},{4,6},{5,7},{6,4},{7,5},{8,10},{9,11},{10,... | collective-permute-start | bytes 1990664 | tf_op jit(solution)/shard_map/ppermute | solution.py:266
  26.8 0.8 %copy-start = (bf16[4,648,128]{2,1,0:T(8,128)(2,1)}, bf16[4,648,128]{2,1,0:T(8,128)(2,1)S(1)}, u32[]{:S(2)}) copy-start(bf16[4,648,128]{2,1,0:T(8,128)(2,1)S(1)} %collective-permute-done.5.got) | copy-start | bytes 1990660
  30.1 15.8 %collective-permute-start.6 = (bf16[648,128]{1,0:T(8,128)(2,1)}, bf16[648,128]{1,0:T(8,128)(2,1)S(1)}, u32[]{:S(2)}, u32[]{:S(2)}) collective-permute-start(bf16[648,128]{1,0:T(8,128)(2,1)} %get-tuple-element.25), channel_id=1, source_target_pairs={{0,1},{1,0},{2,3},{3,2},{4,5},{5,4},{6,7},{7,6},{8,9},{9,8},{10,11... | collective-permute-start | bytes 497672 | tf_op jit(solution)/shard_map/ppermute | solution.py:282
  31.6 14.3 %collective-permute-start.7 = (bf16[648,128]{1,0:T(8,128)(2,1)}, bf16[648,128]{1,0:T(8,128)(2,1)S(1)}, u32[]{:S(2)}, u32[]{:S(2)}) collective-permute-start(bf16[648,128]{1,0:T(8,128)(2,1)} %get-tuple-element.26), channel_id=1, source_target_pairs={{0,4},{1,5},{2,6},{3,7},{4,0},{5,1},{6,2},{7,3},{8,12},{9,13},{10,... | collective-permute-start | bytes 497672 | tf_op jit(solution)/shard_map/ppermute | solution.py:282
  31.6 14.3 %collective-permute-start.8 = (bf16[648,128]{1,0:T(8,128)(2,1)}, bf16[648,128]{1,0:T(8,128)(2,1)S(1)}, u32[]{:S(2)}, u32[]{:S(2)}) collective-permute-start(bf16[648,128]{1,0:T(8,128)(2,1)} %get-tuple-element.27), channel_id=1, source_target_pairs={{0,5},{1,4},{2,7},{3,6},{4,1},{5,0},{6,3},{7,2},{8,13},{9,12},{10,... | collective-permute-start | bytes 497672 | tf_op jit(solution)/shard_map/ppermute | solution.py:282
  33.6 8.7 %collective-permute-start = (bf16[4,32,384]{2,1,0:T(8,128)(2,1)S(1)}, bf16[4,32,384]{2,1,0:T(8,128)(2,1)S(1)}, u32[]{:S(2)}, u32[]{:S(2)}) collective-permute-start(bf16[4,32,384]{2,1,0:T(8,128)(2,1)S(1)} %copy-done.15), channel_id=1, source_target_pairs={{0,1},{1,0},{2,3},{3,2},{4,5},{5,4},{6,7},{7,6},{8,9},{9,8},{10,11... | collective-permute-start | bytes 294920 | tf_op jit(solution)/shard_map/ppermute | solution.py:313
  42.2 0.6 copy-start.6
  44.6 18.4 %collective-permute-start.1 = (bf16[2,64,384]{2,1,0:T(8,128)(2,1)}, bf16[2,64,384]{2,1,0:T(8,128)(2,1)S(1)}, u32[]{:S(2)}, u32[]{:S(2)}) collective-permute-start(bf16[2,64,384]{2,1,0:T(8,128)(2,1)} %get-tuple-element.20), channel_id=1, source_target_pairs={{2,0},{4,2},{6,4},{3,1},{5,3},{7,5},{10,8},{12,10},{14,12},{11,9},... | collective-permute-start | bytes 294920 | tf_op jit(solution)/shard_map/ppermute | solution.py:322
  45.9 0.7 copy-start.1
  45.9 0.7 %copy-start.2 = (bf16[648,128]{1,0:T(8,128)(2,1)}, bf16[648,128]{1,0:T(8,128)(2,1)S(1)}, u32[]{:S(2)}) copy-start(bf16[648,128]{1,0:T(8,128)(2,1)S(1)} %collective-permute-done.7.rest_1_) | copy-start | bytes 497668
  45.9 0.8 %copy-start.3 = (bf16[648,128]{1,0:T(8,128)(2,1)}, bf16[648,128]{1,0:T(8,128)(2,1)S(1)}, u32[]{:S(2)}) copy-start(bf16[648,128]{1,0:T(8,128)(2,1)S(1)} %collective-permute-done.8.rest_2_) | copy-start | bytes 497668
  48.6 6.3 %collective-permute-start.9 = (bf16[168,128]{1,0:T(8,128)(2,1)}, bf16[168,128]{1,0:T(8,128)(2,1)S(1)}, u32[]{:S(2)}, u32[]{:S(2)}) collective-permute-start(bf16[168,128]{1,0:T(8,128)(2,1)} %get-tuple-element.29), channel_id=1, source_target_pairs={{0,8},{8,16},{16,24},{24,0},{1,9},{9,17},{17,25},{25,1},{2,10},{10... | collective-permute-start | bytes 129032 | tf_op jit(solution)/shard_map/ppermute | solution.py:295
  50.2 6.9 %collective-permute-start.10 = (bf16[168,128]{1,0:T(8,128)(2,1)}, bf16[168,128]{1,0:T(8,128)(2,1)S(1)}, u32[]{:S(2)}, u32[]{:S(2)}) collective-permute-start(bf16[168,128]{1,0:T(8,128)(2,1)} %get-tuple-element.30), channel_id=1, source_target_pairs={{0,16},{8,24},{16,0},{24,8},{1,17},{9,25},{17,1},{25,9},{2,18},{10... | collective-permute-start | bytes 129032 | tf_op jit(solution)/shard_map/ppermute | solution.py:295
  52.8 4.5 %collective-permute-start.11 = (bf16[168,128]{1,0:T(8,128)(2,1)}, bf16[168,128]{1,0:T(8,128)(2,1)S(1)}, u32[]{:S(2)}, u32[]{:S(2)}) collective-permute-start(bf16[168,128]{1,0:T(8,128)(2,1)} %get-tuple-element.31), channel_id=1, source_target_pairs={{0,24},{8,0},{16,8},{24,16},{1,25},{9,1},{17,9},{25,17},{2,26},{10... | collective-permute-start | bytes 129032 | tf_op jit(solution)/shard_map/ppermute | solution.py:295
  54.9 2.4 %copy-start.9 = (bf16[168,128]{1,0:T(8,128)(2,1)}, bf16[168,128]{1,0:T(8,128)(2,1)S(1)}, u32[]{:S(2)}) copy-start(bf16[168,128]{1,0:T(8,128)(2,1)S(1)} %collective-permute-done.9.rest_0_) | copy-start | bytes 129028
  57.1 0.6 copy-start.10
  57.3 0.6 copy-start.11
  59.4 7.2 %collective-permute-start.14 = (bf16[168,128]{1,0:T(8,128)(2,1)}, bf16[168,128]{1,0:T(8,128)(2,1)S(1)}, u32[]{:S(2)}, u32[]{:S(2)}) collective-permute-start(bf16[168,128]{1,0:T(8,128)(2,1)} %shard_map.92.mine), channel_id=1, source_target_pairs={{0,24},{8,0},{16,8},{24,16},{1,25},{9,1},{17,9},{25,17},{2,26},{10... | collective-permute-start | bytes 129032 | tf_op jit(solution)/shard_map/ppermute | solution.py:299
  62.4 5.1 %collective-permute-start.13 = (bf16[168,128]{1,0:T(8,128)(2,1)}, bf16[168,128]{1,0:T(8,128)(2,1)S(1)}, u32[]{:S(2)}, u32[]{:S(2)}) collective-permute-start(bf16[168,128]{1,0:T(8,128)(2,1)} %shard_map.92.mine), channel_id=1, source_target_pairs={{0,16},{8,24},{16,0},{24,8},{1,17},{9,25},{17,1},{25,9},{2,18},{10... | collective-permute-start | bytes 129032 | tf_op jit(solution)/shard_map/ppermute | solution.py:299
  62.4 6.0 %collective-permute-start.12 = (bf16[168,128]{1,0:T(8,128)(2,1)}, bf16[168,128]{1,0:T(8,128)(2,1)S(1)}, u32[]{:S(2)}, u32[]{:S(2)}) collective-permute-start(bf16[168,128]{1,0:T(8,128)(2,1)} %shard_map.92.mine), channel_id=1, source_target_pairs={{0,8},{8,16},{16,24},{24,0},{1,9},{9,17},{17,25},{25,1},{2,10},{10... | collective-permute-start | bytes 129032 | tf_op jit(solution)/shard_map/ppermute | solution.py:299
  63.0 0.6 copy-start.4
  66.7 1.8 %copy-start.12 = (bf16[168,128]{1,0:T(8,128)(2,1)}, bf16[168,128]{1,0:T(8,128)(2,1)S(1)}, u32[]{:S(2)}) copy-start(bf16[168,128]{1,0:T(8,128)(2,1)S(1)} %collective-permute-done.14.rest_2_) | copy-start | bytes 129028
  67.6 0.9 %copy-start.13 = (bf16[168,128]{1,0:T(8,128)(2,1)}, bf16[168,128]{1,0:T(8,128)(2,1)S(1)}, u32[]{:S(2)}) copy-start(bf16[168,128]{1,0:T(8,128)(2,1)S(1)} %collective-permute-done.13.rest_1_) | copy-start | bytes 129028
  68.5 0.6 copy-start.14

commit v2 on v1

--- a/solution.py
+++ b/solution.py
@@ -9,6 +9,7 @@
 from jax.experimental.pallas import tpu as pltpu
 from jax.sharding import PartitionSpec as P
 
+
 F32 = jnp.float32
 BF16 = jnp.bfloat16
 VMEM = pl.BlockSpec(memory_space=pltpu.VMEM)
@@ -19,14 +20,18 @@
     return jax.ShapeDtypeStruct(shape, dtype)
 
 
-def kernel_call(body, outs, n_smem, args, scratch=(), flops=0):
+def kernel_call(body, outs, n_smem, args, scratch=(), flops=0, far=()):
     moved = sum(math.prod(a.shape) * a.dtype.itemsize for a in list(args) + list(outs))
+    specs = [SMEM] * n_smem + [VMEM] * (len(args) - n_smem)
+    for i in far:
+        specs[i] = pl.BlockSpec(memory_space=pltpu.HBM)
     return pl.pallas_call(
         body,
         out_shape=outs,
-        in_specs=[SMEM] * n_smem + [VMEM] * (len(args) - n_smem),
+        in_specs=specs,
         out_specs=[VMEM] * len(outs),
         scratch_shapes=list(scratch),
+        compiler_params=pltpu.CompilerParams(vmem_limit_bytes=16 * 2**20),
         cost_estimate=pl.CostEstimate(flops=flops, bytes_accessed=moved, transcendentals=0),
     )(*args)
 
@@ -40,15 +45,19 @@
     return ((dr >= 0) & (dr <= 1) & (dc >= 0) & (dc <= 1)).astype(np.float32)
 
 
-def box_kernel(sizes, grads, weight, box, g_out, *rest):
+def box_kernel(sizes, grads, weight_far, box, g_out, *rest):
     S, HR, W, C, CO, r, n_row = sizes
-    bands, padded = rest[: n_row], rest[n_row]
-    acts = rest[n_row + 1]
+    bands, (padded, acts, weight, grads_in, weight_in) = rest[:n_row], rest[n_row:]
     line = 2 * W
+    end = line * (2 * HR + 1)
+    load_grads = pltpu.make_async_copy(grads, padded.at[:, line:end, :], grads_in)
+    load_weight = pltpu.make_async_copy(weight_far, weight, weight_in)
+    load_grads.start()
+    load_weight.start()
     for s in range(S):
         padded[s, 0:line, :] = jnp.zeros((line, CO), BF16)
-        padded[s, line : line * (2 * HR + 1), :] = grads[s]
-        padded[s, line * (2 * HR + 1) :, :] = jnp.zeros((line, CO), BF16)
+        padded[s, end:, :] = jnp.zeros((line, CO), BF16)
+    load_grads.wait()
     matrix = box[...]
     for s in range(S):
         for R in range(HR):
@@ -57,11 +66,10 @@
             at = (s * HR + R) * W
             for t in range(9):
                 g_out[t, at : at + W, :] = sums[t * W : (t + 1) * W]
+    load_weight.wait()
     total = jnp.zeros((S * HR * W, C), F32)
     for t in range(9):
-        total = total + lax.dot_general(
-            g_out[t], weight[t], (((1,), (1,)), ((), ())), preferred_element_type=F32
-        )
+        total = total + jnp.dot(g_out[t], weight[t], preferred_element_type=F32)
     acts[...] = total.astype(BF16).reshape(S, HR * W, C)
     me = lax.axis_index("row")
     for d in range(n_row):
@@ -70,7 +78,7 @@
 
 
 def wgrad_kernel(sizes, plan, order, bias, time_weight, g, *rest):
-    S, HR, W, C, CO, r, n_row, F = sizes
+    S, HR, W, C, _, r, n_row, F = sizes
     own, prior = rest[:n_row], rest[n_row : 2 * n_row]
     n_out = 2 if plan else 1
     outs = rest[2 * n_row : 2 * n_row + n_out]
@@ -79,11 +87,12 @@
     for d in range(n_row):
         source = lax.rem(me - d + n_row, n_row)
         for f in range(F + 2):
-            block = prior[d][f] if f < 2 else own[d][f - 2]
+            block = prior[d][F - 2 + f] if f < 2 else own[d][f - 2]
             start = pl.multiple_of((f * HR + source * r) * W, W)
             ext[pl.ds(start, r * W), :] = block
     step = HR * W
-    total = jnp.broadcast_to(bias[...], (F * step, 2 * C))
+    row = jnp.concatenate([bias[i : i + 1, :] for i in range(bias.shape[0])], axis=1)
+    total = jnp.broadcast_to(row, (F * step, 2 * C))
     for k in range(3):
         total = total + jnp.dot(
             ext[k * step : (k + F) * step, :], time_weight[k], preferred_element_type=F32
@@ -103,7 +112,7 @@
         n_q, chunk = plan
         core = lax.rem(lax.axis_index("frame"), 2)
         keep, send = outs
-        half, low = chunk // 2, CO - 128
+        half = chunk // 2
         for q in range(n_q):
             for which, out in ((core, keep), (1 - core, send)):
                 index = ((q // n_row) * 2 + which) * n_row + q % n_row
@@ -144,7 +153,7 @@
     rest[-1][...] = (value * scale).astype(BF16)
 
 
-def final_kernel(n_clip, base, size, chunk, CO, mine, *rest):
+def final_kernel(n_clip, base, chunk, CO, mine, *rest):
     got, out, total, even = rest[: n_clip - 1], rest[n_clip - 1], rest[n_clip], rest[n_clip + 1]
     z = lax.axis_index("clip")
     for d in range(n_clip):
@@ -169,7 +178,7 @@
 
 
 def order_kernel(sizes, order, *rest):
-    S, rW, n_row, F = sizes
+    S, rW, n_row, _ = sizes
     bands, natural, first = rest[:n_row], rest[n_row], rest[n_row + 1]
     me = lax.axis_index("row")
     for d in range(n_row):
@@ -197,6 +206,11 @@
     out[...] = total.astype(BF16)
 
 
+def direct(n_frame, n_row, n_clip):
+    n_q = n_frame * n_row // 2
+    return n_frame % 2 == 0 and 1 < n_q <= 8 and n_q & (n_q - 1) == 0 and n_clip > 1
+
+
 def local(features, time_weight, time_bias, space_weight, pixel_grads, frame_order):
     _, F, r, W, C = features.shape
     _, S, UR, UW, CO = pixel_grads.shape
@@ -207,7 +221,6 @@
     both = ("frame", "row")
 
     feats = features.reshape(F, rW, C)
-    last = feats[F - 2 :]
     own, prior = [feats], []
     for d in range(1, n_row):
         own.append(lax.ppermute(feats, "row", [(i, (i + d) % n_row) for i in range(n_row)]))
@@ -217,15 +230,22 @@
             for f in range(n_frame - 1)
             for i in range(n_row)
         ]
-        prior.append(lax.ppermute(last, both, route))
+        prior.append(lax.ppermute(feats, both, route))
 
     box = jnp.asarray(box_matrix(W), BF16)
     g, *bands = kernel_call(
         functools.partial(box_kernel, (S, HR, W, C, CO, r, n_row)),
         [struct((9, pixels, CO), BF16)] + [struct((S, rW, C), BF16)] * n_row,
         0,
-        [pixel_grads.reshape(S, UR * UW, CO), space_weight.reshape(9, C, CO), box],
-        [pltpu.VMEM((S, (UR + 2) * UW, CO), BF16), pltpu.VMEM((S, HR * W, C), BF16)],
+        [pixel_grads.reshape(S, UR * UW, CO), space_weight.transpose(0, 1, 3, 2).reshape(9, CO, C), box],
+        [
+            pltpu.VMEM((S, (UR + 2) * UW, CO), BF16),
+            pltpu.VMEM((S, HR * W, C), BF16),
+            pltpu.VMEM((9, CO, C), BF16),
+            pltpu.SemaphoreType.DMA,
+            pltpu.SemaphoreType.DMA,
+        ],
+        far=(0, 1),
         flops=2 * pixels * 9 * C * CO,
     )
 
@@ -234,13 +254,10 @@
     n_q = n_dev // 2
     chunk = n_total // n_dev
     fast = (
-        n_frame % 2 == 0
+        direct(n_frame, n_row, n_clip)
         and n_total % n_dev == 0
         and chunk % 16 == 0
-        and 1 < n_q <= 8
-        and n_q & (n_q - 1) == 0
-        and n_clip > 1
-        and 128 < CO == 192
+        and CO == 192
     )
     wg_sizes = (S, HR, W, C, CO, r, n_row, F)
     packed = chunk * CO // 128
@@ -250,7 +267,7 @@
         if fast
         else [struct((n_total, CO), F32)],
         1,
-        [order, time_bias.reshape(1, -1), time_weight, g] + own + prior,
+        [order, time_bias.reshape(-1, 128), time_weight, g] + own + prior,
         [
             pltpu.VMEM(((F + 2) * HR * W, C), BF16),
             pltpu.VMEM((2, F * HR * W, C), BF16),
@@ -298,7 +315,7 @@
         )
         got = [lax.ppermute(mine, "clip", route) for route in shift]
         (flat,) = kernel_call(
-            functools.partial(final_kernel, n_clip, base, size, chunk, CO),
+            functools.partial(final_kernel, n_clip, base, chunk, CO),
             [struct((packed, 128), F32)],
             0,
             [mine] + got,
@@ -332,7 +349,7 @@
 
 
 def solution(mesh):
-    return jax.shard_map(
+    step = jax.shard_map(
         local,
         mesh=mesh,
         in_specs=(
@@ -346,3 +363,6 @@
         out_specs=(P("clip", "frame", "row", None, None), P(("frame", "row"))),
         check_vma=False,
     )
+    if not direct(mesh.shape["frame"], mesh.shape["row"], mesh.shape["clip"]):
+        return step
+    return step

time: 71.4 us -> 51.9 us (0.73)
  Pallas kernels: 21.4 us -> 7.56 us
  local copies, waits for them, and re-layouts: 10.5 us -> 3.29 us
  waiting for transfers between devices: 14.3 us -> 15.8 us
    pallas_call x8, Pallas kernels: 21.4 us -> 7.56 us  [kernel_call(): pl.pallas_call(body, out_shape=outs, in_specs=specs, out_specs=[VMEM] * l...]
    unnamed x33 -> x14, local copies, waits for them, and re-layouts: 8.38 us -> 3.29 us
    ppermute x2, starting transfers between devices: 5.35 us -> 7.99 us  [local(): prior.append(lax.ppermute(feats, both, route))]
    ppermute x1, starting transfers between devices: 3.06 us -> 0.57 us  [local(): lax.ppermute(feats, 'row', [(i, (i + d) % n_row) for i in range(n_row)])]
    ppermute x3, waiting for transfers between devices: 1.79 us -> 3.8 us  [local(): got = [lax.ppermute(mine, 'clip', route) for route in shift]]
    reshape x1 -> x0, local copies, waits for them, and re-layouts: 1.29 us -> none  [local(): time_bias.reshape(1, -1)]
    slice x1 -> x0, local copies, waits for them, and re-layouts: 0.84 us -> none  [local(): last = feats[F - 2:]]
  transfers between devices with their start and end apart: 15 -> 15, of which waited for: 7 -> 7; matrix products, arithmetic and copies ran while one was open for 8% -> 0% of each run, Pallas kernels for 16% -> 7%
where the time goes in v2:
time: 51.9 us; the launch traced here: 51.6 us
  starting transfers between devices  24.2 us (47%)
  waiting for transfers between devices  15.8 us (30%)
  Pallas kernels  7.56 us (15%)
  local copies, waits for them, and re-layouts  3.29 us (6%)
  between operations  0.79 us (2%)
    ppermute x2, starting transfers between devices, local(): prior.append(lax.ppermute(feats, both, route))  7.99 us
    pallas_call x8, Pallas kernels, kernel_call(): pl.pallas_call(body, out_shape=outs, in_specs=specs, out_specs=[VMEM] * l...  7.56 us
    ppermute x1, waiting for transfers between devices, local(): lax.ppermute(bands[d], 'row', [(i, (i + d) % n_row) for i in range(n_row)])  6.94 us
    ppermute x3, starting transfers between devices, local(): got = [lax.ppermute(x, 'clip', route) for x, route in zip(sends, shift)]  5.56 us
    ppermute x3, waiting for transfers between devices, local(): got = [lax.ppermute(mine, 'clip', route) for route in shift]  3.8 us
    ppermute x3, starting transfers between devices, local(): got = [lax.ppermute(mine, 'clip', route) for route in shift]  3.66 us
    ppermute x3, starting transfers between devices, local(): lax.ppermute(sends[d - 1], both, [(i, square(i, d)) for i in range(n_dev)])  3.55 us
    unnamed x14, local copies, waits for them, and re-layouts  3.29 us
  transfers between devices with their start and end apart: 15, of which 7 were waited for; matrix products, arithmetic and copies ran while one was open for 0% of the time, Pallas kernels for 7%

profile of v2, /device:TPU:0, one launch (start us, length us, event | category | flops | bytes accessed | tf_op | source)
XLA Modules:
  0.0 51.6 jit_solution(16352657880420733476)
XLA Ops:
  0.6 0.0 copy-start
  0.6 4.5 %collective-permute-start.4 = (bf16[4,32,384]{2,1,0:T(8,128)(2,1)}, bf16[4,32,384]{2,1,0:T(8,128)(2,1)S(1)}, u32[]{:S(2)}, u32[]{:S(2)}) collective-permute-start(bf16[4,32,384]{2,1,0:T(8,128)(2,1)} %bitcast.13), channel_id=1, source_target_pairs={{0,3},{1,2},{2,5},{3,4},{4,7},{5,6},{8,11},{9,10},{10,13},{11,12},... | collective-permute-start | bytes 294920 | tf_op jit(solution)/shard_map/ppermute | solution.py:233
  5.1 3.5 %collective-permute-start.3 = (bf16[4,32,384]{2,1,0:T(8,128)(2,1)}, bf16[4,32,384]{2,1,0:T(8,128)(2,1)S(1)}, u32[]{:S(2)}, u32[]{:S(2)}) collective-permute-start(bf16[4,32,384]{2,1,0:T(8,128)(2,1)} %bitcast.14), channel_id=1, source_target_pairs={{0,2},{1,3},{2,4},{3,5},{4,6},{5,7},{8,10},{9,11},{10,12},{11,13},... | collective-permute-start | bytes 294920 | tf_op jit(solution)/shard_map/ppermute | solution.py:233
  8.6 0.6 %collective-permute-start.2 = (bf16[4,32,384]{2,1,0:T(8,128)(2,1)}, bf16[4,32,384]{2,1,0:T(8,128)(2,1)S(1)}, u32[]{:S(2)}, u32[]{:S(2)}) collective-permute-start(bf16[4,32,384]{2,1,0:T(8,128)(2,1)} %bitcast.15), channel_id=1, source_target_pairs={{0,1},{1,0},{2,3},{3,2},{4,5},{5,4},{6,7},{7,6},{8,9},{9,8},{10,11... | collective-permute-start | bytes 294920 | tf_op jit(solution)/shard_map/ppermute | solution.py:226
  9.2 0.0 copy-start.1
  9.2 1.3 %copy-done.1 = bf16[3,3,384,192]{2,3,1,0:T(8,128)(2,1)S(1)} copy-done((bf16[3,3,384,192]{2,3,1,0:T(8,128)(2,1)S(1)}, bf16[3,3,384,192]{2,3,1,0:T(8,128)(2,1)}, u32[]{:S(2)}) %copy-start.1) | copy-done | bytes 1327128
  10.5 0.0 copy-start.2
  10.5 1.0 %copy-done.2 = bf16[1,4,4,64,192]{4,3,2,1,0:T(8,128)(2,1)S(1)} copy-done((bf16[1,4,4,64,192]{4,3,2,1,0:T(8,128)(2,1)S(1)}, bf16[1,4,4,64,192]{4,3,2,1,0:T(8,128)(2,1)}, u32[]{:S(2)}) %copy-start.2) | copy-done | bytes 393240
  11.6 0.0 copy-start.3
  11.6 0.9 %copy-done.3 = bf16[288,256]{1,0:T(8,128)(2,1)S(1)} copy-done((bf16[288,256]{1,0:T(8,128)(2,1)S(1)}, bf16[288,256]{1,0:T(8,128)(2,1)}, u32[]{:S(2)}) %copy-start.3) | copy-done | bytes 147480
  12.5 1.5 %shard_map.86 = (bf16[9,256,192]{2,1,0:T(8,128)(2,1)S(1)}, bf16[4,32,384]{2,1,0:T(8,128)(2,1)S(1)}, bf16[4,32,384]{2,1,0:T(8,128)(2,1)S(1)}) custom-call(bf16[4,256,192]{2,1,0:T(8,128)(2,1)S(1)} %bitcast.12, bf16[9,192,384]{2,1,0:T(8,128)(2,1)S(1)} %bitcast.11, bf16[288,256]{1,0:T(8,128)(2,1)S(1)} %copy-done.3), custom_call_target="tpu_custom_call" | custom-call | flops 339738624 | bytes 2949120 | tf_op jit(solution)/shard_map/pallas_call | solution.py:28
  14.0 0.0 collective-permute-done.4.rest_3_
  14.0 0.0 collective-permute-done.3.rest_2_
  14.0 0.0 collective-permute-done.2.rest_1_
  14.0 0.0 copy-done
  14.0 0.0 copy-done.4
  14.0 0.0 copy-done.5
  14.0 0.0 copy-done.6
  14.0 2.9 %shard_map.89 = (f32[4,648,128]{2,1,0:T(8,128)S(1)}, bf16[4,648,128]{2,1,0:T(8,128)(2,1)S(1)}) custom-call(s32[8]{0:T(128)S(1)} %bitcast.18, f32[6,128]{1,0:T(8,128)S(1)} %bitcast.17, bf16[3,384,768]{2,1,0:T(8,128)(2,1)S(1)} %copy-done, bf16[9,256,192]{2,1,0:T(8,128)(2,1)S(1)} %get-tuple-element.21.g, bf16[4,32,384]{2,1,0:T(8,128)(2,1)S(1)} %bitcast.16, ...), custom_call_target="tpu_custom_call" | custom-call | flops 792723456 | bytes 5041184 | tf_op jit(solution)/shard_map/pallas_call | solution.py:28
  16.9 0.1 collective-permute-start.5
  17.0 2.1 %collective-permute-done.5.got = bf16[4,648,128]{2,1,0:T(8,128)(2,1)S(1)} collective-permute-done((bf16[4,648,128]{2,1,0:T(8,128)(2,1)S(1)}, bf16[4,648,128]{2,1,0:T(8,128)(2,1)S(1)}, u32[]{:S(2)}, u32[]{:S(2)}) %collective-permute-start.5) | collective-permute-done | bytes 663584 | tf_op jit(solution)/shard_map/ppermute | solution.py:283
  19.1 0.1 shard_map.90
  19.2 1.6 %collective-permute-start.6 = (bf16[648,128]{1,0:T(8,128)(2,1)S(1)}, bf16[648,128]{1,0:T(8,128)(2,1)S(1)}, u32[]{:S(2)}, u32[]{:S(2)}) collective-permute-start(bf16[648,128]{1,0:T(8,128)(2,1)S(1)} %get-tuple-element.25), channel_id=1, source_target_pairs={{0,1},{1,0},{2,3},{3,2},{4,5},{5,4},{6,7},{7,6},{8,9},{9,8},{10,11... | collective-permute-start | bytes 497672 | tf_op jit(solution)/shard_map/ppermute | solution.py:299
  20.8 0.0 collective-permute-start.7
  20.8 2.0 %collective-permute-start.8 = (bf16[648,128]{1,0:T(8,128)(2,1)S(1)}, bf16[648,128]{1,0:T(8,128)(2,1)S(1)}, u32[]{:S(2)}, u32[]{:S(2)}) collective-permute-start(bf16[648,128]{1,0:T(8,128)(2,1)S(1)} %get-tuple-element.27), channel_id=1, source_target_pairs={{0,5},{1,4},{2,7},{3,6},{4,1},{5,0},{6,3},{7,2},{8,13},{9,12},{10,... | collective-permute-start | bytes 497672 | tf_op jit(solution)/shard_map/ppermute | solution.py:299
  22.8 1.5 %collective-permute-start = (bf16[4,32,384]{2,1,0:T(8,128)(2,1)S(1)}, bf16[4,32,384]{2,1,0:T(8,128)(2,1)S(1)}, u32[]{:S(2)}, u32[]{:S(2)}) collective-permute-start(bf16[4,32,384]{2,1,0:T(8,128)(2,1)S(1)} %get-tuple-element.18), channel_id=1, source_target_pairs={{0,1},{1,0},{2,3},{3,2},{4,5},{5,4},{6,7},{7,6},{8,9},{9,8},{10,11... | collective-permute-start | bytes 294920 | tf_op jit(solution)/shard_map/ppermute | solution.py:330
  24.3 6.9 %collective-permute-done.rest_1_ = bf16[4,32,384]{2,1,0:T(8,128)(2,1)S(1)} collective-permute-done((bf16[4,32,384]{2,1,0:T(8,128)(2,1)S(1)}, bf16[4,32,384]{2,1,0:T(8,128)(2,1)S(1)}, u32[]{:S(2)}, u32[]{:S(2)}) %collective-permute-start) | collective-permute-done | bytes 98336 | tf_op jit(solution)/shard_map/ppermute | solution.py:330
  31.2 0.6 %shard_map.87 = (bf16[2,128,384]{2,1,0:T(8,128)(2,1)S(1)}, bf16[2,64,384]{2,1,0:T(8,128)(2,1)S(1)}) custom-call(s32[8]{0:T(128)S(1)} %bitcast.19, bf16[4,32,384]{2,1,0:T(8,128)(2,1)S(1)} %get-tuple-element.17.rest_0_, bf16[4,32,384]{2,1,0:T(8,128)(2,1)S(1)} %collective-permute-done.rest_1_), custom_call_target="tpu_custom_call" | custom-call | bytes 491552 | tf_op jit(solution)/shard_map/pallas_call | solution.py:28
  31.9 1.3 %collective-permute-start.1 = (bf16[2,64,384]{2,1,0:T(8,128)(2,1)S(1)}, bf16[2,64,384]{2,1,0:T(8,128)(2,1)S(1)}, u32[]{:S(2)}, u32[]{:S(2)}) collective-permute-start(bf16[2,64,384]{2,1,0:T(8,128)(2,1)S(1)} %get-tuple-element.20), channel_id=1, source_target_pairs={{2,0},{4,2},{6,4},{3,1},{5,3},{7,5},{10,8},{12,10},{14,12},{11,9},... | collective-permute-start | bytes 294920 | tf_op jit(solution)/shard_map/ppermute | solution.py:339
  33.2 0.0 collective-permute-done.6.rest_0_
  33.2 0.0 collective-permute-done.7.rest_1_
  33.2 0.0 collective-permute-done.8.rest_2_
  33.2 0.1 shard_map.91
  33.3 1.6 %collective-permute-start.9 = (bf16[168,128]{1,0:T(8,128)(2,1)S(1)}, bf16[168,128]{1,0:T(8,128)(2,1)S(1)}, u32[]{:S(2)}, u32[]{:S(2)}) collective-permute-start(bf16[168,128]{1,0:T(8,128)(2,1)S(1)} %get-tuple-element.29), channel_id=1, source_target_pairs={{0,8},{8,16},{16,24},{24,0},{1,9},{9,17},{17,25},{25,1},{2,10},{10... | collective-permute-start | bytes 129032 | tf_op jit(solution)/shard_map/ppermute | solution.py:312
  34.9 2.6 %collective-permute-start.10 = (bf16[168,128]{1,0:T(8,128)(2,1)S(1)}, bf16[168,128]{1,0:T(8,128)(2,1)S(1)}, u32[]{:S(2)}, u32[]{:S(2)}) collective-permute-start(bf16[168,128]{1,0:T(8,128)(2,1)S(1)} %get-tuple-element.30), channel_id=1, source_target_pairs={{0,16},{8,24},{16,0},{24,8},{1,17},{9,25},{17,1},{25,9},{2,18},{10... | collective-permute-start | bytes 129032 | tf_op jit(solution)/shard_map/ppermute | solution.py:312
  37.5 1.3 %collective-permute-start.11 = (bf16[168,128]{1,0:T(8,128)(2,1)S(1)}, bf16[168,128]{1,0:T(8,128)(2,1)S(1)}, u32[]{:S(2)}, u32[]{:S(2)}) collective-permute-start(bf16[168,128]{1,0:T(8,128)(2,1)S(1)} %get-tuple-element.31), channel_id=1, source_target_pairs={{0,24},{8,0},{16,8},{24,16},{1,25},{9,1},{17,9},{25,17},{2,26},{10... | collective-permute-start | bytes 129032 | tf_op jit(solution)/shard_map/ppermute | solution.py:312
  38.9 0.6 %collective-permute-done.9.rest_0_ = bf16[168,128]{1,0:T(8,128)(2,1)S(1)} collective-permute-done((bf16[168,128]{1,0:T(8,128)(2,1)S(1)}, bf16[168,128]{1,0:T(8,128)(2,1)S(1)}, u32[]{:S(2)}, u32[]{:S(2)}) %collective-permute-start.9) | collective-permute-done | bytes 43040 | tf_op jit(solution)/shard_map/ppermute | solution.py:312
  39.4 2.2 %collective-permute-done.10.rest_1_ = bf16[168,128]{1,0:T(8,128)(2,1)S(1)} collective-permute-done((bf16[168,128]{1,0:T(8,128)(2,1)S(1)}, bf16[168,128]{1,0:T(8,128)(2,1)S(1)}, u32[]{:S(2)}, u32[]{:S(2)}) %collective-permute-start.10) | collective-permute-done | bytes 43040 | tf_op jit(solution)/shard_map/ppermute | solution.py:312
  41.6 0.2 collective-permute-done.11.rest_2_
  41.8 3.0 %collective-permute-start.14 = (bf16[168,128]{1,0:T(8,128)(2,1)S(1)}, bf16[168,128]{1,0:T(8,128)(2,1)S(1)}, u32[]{:S(2)}, u32[]{:S(2)}) collective-permute-start(bf16[168,128]{1,0:T(8,128)(2,1)S(1)} %shard_map.92.mine), channel_id=1, source_target_pairs={{0,24},{8,0},{16,8},{24,16},{1,25},{9,1},{17,9},{25,17},{2,26},{10... | collective-permute-start | bytes 129032 | tf_op jit(solution)/shard_map/ppermute | solution.py:316
  44.8 0.0 collective-permute-start.13
  44.8 0.6 %collective-permute-start.12 = (bf16[168,128]{1,0:T(8,128)(2,1)S(1)}, bf16[168,128]{1,0:T(8,128)(2,1)S(1)}, u32[]{:S(2)}, u32[]{:S(2)}) collective-permute-start(bf16[168,128]{1,0:T(8,128)(2,1)S(1)} %shard_map.92.mine), channel_id=1, source_target_pairs={{0,8},{8,16},{16,24},{24,0},{1,9},{9,17},{17,25},{25,1},{2,10},{10... | collective-permute-start | bytes 129032 | tf_op jit(solution)/shard_map/ppermute | solution.py:316
  45.5 0.0 collective-permute-done.1.later
  45.5 1.4 %shard_map.88 = bf16[128,384]{1,0:T(8,128)(2,1)} custom-call(bf16[2,128,384]{2,1,0:T(8,128)(2,1)S(1)} %get-tuple-element.19.natural, bf16[2,64,384]{2,1,0:T(8,128)(2,1)S(1)} %collective-permute-done.1.later, bf16[3,384,768]{2,1,0:T(8,128)(2,1)S(1)} %copy-done), custom_call_target="tpu_custom_call" | custom-call | flops 226492416 | bytes 2162688 | tf_op jit(solution)/shard_map/pallas_call | solution.py:28
  46.9 0.0 collective-permute-done.14.rest_2_
  46.9 2.9 %collective-permute-done.13.rest_1_ = bf16[168,128]{1,0:T(8,128)(2,1)S(1)} collective-permute-done((bf16[168,128]{1,0:T(8,128)(2,1)S(1)}, bf16[168,128]{1,0:T(8,128)(2,1)S(1)}, u32[]{:S(2)}, u32[]{:S(2)}) %collective-permute-start.13) | collective-permute-done | bytes 43040 | tf_op jit(solution)/shard_map/ppermute | solution.py:316
  49.8 0.9 %collective-permute-done.12.rest_0_ = bf16[168,128]{1,0:T(8,128)(2,1)S(1)} collective-permute-done((bf16[168,128]{1,0:T(8,128)(2,1)S(1)}, bf16[168,128]{1,0:T(8,128)(2,1)S(1)}, u32[]{:S(2)}, u32[]{:S(2)}) %collective-permute-start.12) | collective-permute-done | bytes 43040 | tf_op jit(solution)/shard_map/ppermute | solution.py:316
  50.7 0.9 %shard_map.93 = f32[648,128]{1,0:T(8,128)} custom-call(bf16[168,128]{1,0:T(8,128)(2,1)S(1)} %shard_map.92.mine, bf16[168,128]{1,0:T(8,128)(2,1)S(1)} %collective-permute-done.12.rest_0_, bf16[168,128]{1,0:T(8,128)(2,1)S(1)} %collective-permute-done.13.rest_1_, bf16[168,128]{1,0:T(8,128)(2,1)S(1)} %collective-permute-done.14.rest_2_), custom_call_target="tpu_custom_call" | custom-call | bytes 503808 | tf_op jit(solution)/shard_map/pallas_call | solution.py:28
  (4 shorter events, 0.0 us)
Async XLA Ops:
  0.6 13.4 %copy-start = (bf16[3,384,768]{2,1,0:T(8,128)(2,1)S(1)}, bf16[3,384,768]{2,1,0:T(8,128)(2,1)}, u32[]{:S(2)}) copy-start(bf16[3,384,768]{2,1,0:T(8,128)(2,1)} %time_weight.3) | copy-start | bytes 5308420
  0.6 13.3 %collective-permute-start.4 = (bf16[4,32,384]{2,1,0:T(8,128)(2,1)}, bf16[4,32,384]{2,1,0:T(8,128)(2,1)S(1)}, u32[]{:S(2)}, u32[]{:S(2)}) collective-permute-start(bf16[4,32,384]{2,1,0:T(8,128)(2,1)} %bitcast.13), channel_id=1, source_target_pairs={{0,3},{1,2},{2,5},{3,4},{4,7},{5,6},{8,11},{9,10},{10,13},{11,12},... | collective-permute-start | bytes 294920 | tf_op jit(solution)/shard_map/ppermute | solution.py:233
  5.1 8.9 %collective-permute-start.3 = (bf16[4,32,384]{2,1,0:T(8,128)(2,1)}, bf16[4,32,384]{2,1,0:T(8,128)(2,1)S(1)}, u32[]{:S(2)}, u32[]{:S(2)}) collective-permute-start(bf16[4,32,384]{2,1,0:T(8,128)(2,1)} %bitcast.14), channel_id=1, source_target_pairs={{0,2},{1,3},{2,4},{3,5},{4,6},{5,7},{8,10},{9,11},{10,12},{11,13},... | collective-permute-start | bytes 294920 | tf_op jit(solution)/shard_map/ppermute | solution.py:233
  8.6 5.3 %collective-permute-start.2 = (bf16[4,32,384]{2,1,0:T(8,128)(2,1)}, bf16[4,32,384]{2,1,0:T(8,128)(2,1)S(1)}, u32[]{:S(2)}, u32[]{:S(2)}) collective-permute-start(bf16[4,32,384]{2,1,0:T(8,128)(2,1)} %bitcast.15), channel_id=1, source_target_pairs={{0,1},{1,0},{2,3},{3,2},{4,5},{5,4},{6,7},{7,6},{8,9},{9,8},{10,11... | collective-permute-start | bytes 294920 | tf_op jit(solution)/shard_map/ppermute | solution.py:226
  9.2 1.3 %copy-start.1 = (bf16[3,3,384,192]{2,3,1,0:T(8,128)(2,1)S(1)}, bf16[3,3,384,192]{2,3,1,0:T(8,128)(2,1)}, u32[]{:S(2)}) copy-start(bf16[3,3,384,192]{2,3,1,0:T(8,128)(2,1)} %param.10) | copy-start | bytes 3981316
  10.5 1.0 %copy-start.2 = (bf16[1,4,4,64,192]{4,3,2,1,0:T(8,128)(2,1)S(1)}, bf16[1,4,4,64,192]{4,3,2,1,0:T(8,128)(2,1)}, u32[]{:S(2)}) copy-start(bf16[1,4,4,64,192]{4,3,2,1,0:T(8,128)(2,1)} %param.11) | copy-start | bytes 1179652
  11.6 0.9 %copy-start.3 = (bf16[288,256]{1,0:T(8,128)(2,1)S(1)}, bf16[288,256]{1,0:T(8,128)(2,1)}, u32[]{:S(2)}) copy-start(bf16[288,256]{1,0:T(8,128)(2,1)} %constant.2.clone.box) | copy-start | bytes 442372
  12.5 1.5 %copy-start.4 = (bf16[1,4,1,32,384]{4,3,2,1,0:T(8,128)(2,1)S(1)}, bf16[1,4,1,32,384]{4,3,2,1,0:T(8,128)(2,1)}, u32[]{:S(2)}) copy-start(bf16[1,4,1,32,384]{4,3,2,1,0:T(8,128)(2,1)} %param.7) | copy-start | bytes 294916
  12.5 1.5 %copy-start.5 = (f32[768]{0:T(1024)S(1)}, f32[768]{0:T(1024)}, u32[]{:S(2)}) copy-start(f32[768]{0:T(1024)} %param.9) | copy-start | bytes 9220
  12.5 1.5 %copy-start.6 = (s32[1,1,8]{2,1,0:T(1,128)S(1)}, s32[1,1,8]{2,1,0:T(1,128)}, u32[]{:S(2)}) copy-start(s32[1,1,8]{2,1,0:T(1,128)} %param.12) | copy-start | bytes 100
  16.9 2.2 %collective-permute-start.5 = (bf16[4,648,128]{2,1,0:T(8,128)(2,1)S(1)}, bf16[4,648,128]{2,1,0:T(8,128)(2,1)S(1)}, u32[]{:S(2)}, u32[]{:S(2)}) collective-permute-start(bf16[4,648,128]{2,1,0:T(8,128)(2,1)S(1)} %get-tuple-element.23), channel_id=1, source_target_pairs={{0,2},{1,3},{2,0},{3,1},{4,6},{5,7},{6,4},{7,5},{8,10},{9,11},{10,... | collective-permute-start | bytes 1990664 | tf_op jit(solution)/shard_map/ppermute | solution.py:283
  19.2 13.9 %collective-permute-start.6 = (bf16[648,128]{1,0:T(8,128)(2,1)S(1)}, bf16[648,128]{1,0:T(8,128)(2,1)S(1)}, u32[]{:S(2)}, u32[]{:S(2)}) collective-permute-start(bf16[648,128]{1,0:T(8,128)(2,1)S(1)} %get-tuple-element.25), channel_id=1, source_target_pairs={{0,1},{1,0},{2,3},{3,2},{4,5},{5,4},{6,7},{7,6},{8,9},{9,8},{10,11... | collective-permute-start | bytes 497672 | tf_op jit(solution)/shard_map/ppermute | solution.py:299
  20.8 12.4 %collective-permute-start.7 = (bf16[648,128]{1,0:T(8,128)(2,1)S(1)}, bf16[648,128]{1,0:T(8,128)(2,1)S(1)}, u32[]{:S(2)}, u32[]{:S(2)}) collective-permute-start(bf16[648,128]{1,0:T(8,128)(2,1)S(1)} %get-tuple-element.26), channel_id=1, source_target_pairs={{0,4},{1,5},{2,6},{3,7},{4,0},{5,1},{6,2},{7,3},{8,12},{9,13},{10,... | collective-permute-start | bytes 497672 | tf_op jit(solution)/shard_map/ppermute | solution.py:299
  20.8 12.4 %collective-permute-start.8 = (bf16[648,128]{1,0:T(8,128)(2,1)S(1)}, bf16[648,128]{1,0:T(8,128)(2,1)S(1)}, u32[]{:S(2)}, u32[]{:S(2)}) collective-permute-start(bf16[648,128]{1,0:T(8,128)(2,1)S(1)} %get-tuple-element.27), channel_id=1, source_target_pairs={{0,5},{1,4},{2,7},{3,6},{4,1},{5,0},{6,3},{7,2},{8,13},{9,12},{10,... | collective-permute-start | bytes 497672 | tf_op jit(solution)/shard_map/ppermute | solution.py:299
  22.8 8.5 %collective-permute-start = (bf16[4,32,384]{2,1,0:T(8,128)(2,1)S(1)}, bf16[4,32,384]{2,1,0:T(8,128)(2,1)S(1)}, u32[]{:S(2)}, u32[]{:S(2)}) collective-permute-start(bf16[4,32,384]{2,1,0:T(8,128)(2,1)S(1)} %get-tuple-element.18), channel_id=1, source_target_pairs={{0,1},{1,0},{2,3},{3,2},{4,5},{5,4},{6,7},{7,6},{8,9},{9,8},{10,11... | collective-permute-start | bytes 294920 | tf_op jit(solution)/shard_map/ppermute | solution.py:330
  31.9 13.6 %collective-permute-start.1 = (bf16[2,64,384]{2,1,0:T(8,128)(2,1)S(1)}, bf16[2,64,384]{2,1,0:T(8,128)(2,1)S(1)}, u32[]{:S(2)}, u32[]{:S(2)}) collective-permute-start(bf16[2,64,384]{2,1,0:T(8,128)(2,1)S(1)} %get-tuple-element.20), channel_id=1, source_target_pairs={{2,0},{4,2},{6,4},{3,1},{5,3},{7,5},{10,8},{12,10},{14,12},{11,9},... | collective-permute-start | bytes 294920 | tf_op jit(solution)/shard_map/ppermute | solution.py:339
  33.3 6.1 %collective-permute-start.9 = (bf16[168,128]{1,0:T(8,128)(2,1)S(1)}, bf16[168,128]{1,0:T(8,128)(2,1)S(1)}, u32[]{:S(2)}, u32[]{:S(2)}) collective-permute-start(bf16[168,128]{1,0:T(8,128)(2,1)S(1)} %get-tuple-element.29), channel_id=1, source_target_pairs={{0,8},{8,16},{16,24},{24,0},{1,9},{9,17},{17,25},{25,1},{2,10},{10... | collective-permute-start | bytes 129032 | tf_op jit(solution)/shard_map/ppermute | solution.py:312
  34.9 6.7 %collective-permute-start.10 = (bf16[168,128]{1,0:T(8,128)(2,1)S(1)}, bf16[168,128]{1,0:T(8,128)(2,1)S(1)}, u32[]{:S(2)}, u32[]{:S(2)}) collective-permute-start(bf16[168,128]{1,0:T(8,128)(2,1)S(1)} %get-tuple-element.30), channel_id=1, source_target_pairs={{0,16},{8,24},{16,0},{24,8},{1,17},{9,25},{17,1},{25,9},{2,18},{10... | collective-permute-start | bytes 129032 | tf_op jit(solution)/shard_map/ppermute | solution.py:312
  37.5 4.3 %collective-permute-start.11 = (bf16[168,128]{1,0:T(8,128)(2,1)S(1)}, bf16[168,128]{1,0:T(8,128)(2,1)S(1)}, u32[]{:S(2)}, u32[]{:S(2)}) collective-permute-start(bf16[168,128]{1,0:T(8,128)(2,1)S(1)} %get-tuple-element.31), channel_id=1, source_target_pairs={{0,24},{8,0},{16,8},{24,16},{1,25},{9,1},{17,9},{25,17},{2,26},{10... | collective-permute-start | bytes 129032 | tf_op jit(solution)/shard_map/ppermute | solution.py:312
  41.8 5.1 %collective-permute-start.14 = (bf16[168,128]{1,0:T(8,128)(2,1)S(1)}, bf16[168,128]{1,0:T(8,128)(2,1)S(1)}, u32[]{:S(2)}, u32[]{:S(2)}) collective-permute-start(bf16[168,128]{1,0:T(8,128)(2,1)S(1)} %shard_map.92.mine), channel_id=1, source_target_pairs={{0,24},{8,0},{16,8},{24,16},{1,25},{9,1},{17,9},{25,17},{2,26},{10... | collective-permute-start | bytes 129032 | tf_op jit(solution)/shard_map/ppermute | solution.py:316
  44.8 4.9 %collective-permute-start.13 = (bf16[168,128]{1,0:T(8,128)(2,1)S(1)}, bf16[168,128]{1,0:T(8,128)(2,1)S(1)}, u32[]{:S(2)}, u32[]{:S(2)}) collective-permute-start(bf16[168,128]{1,0:T(8,128)(2,1)S(1)} %shard_map.92.mine), channel_id=1, source_target_pairs={{0,16},{8,24},{16,0},{24,8},{1,17},{9,25},{17,1},{25,9},{2,18},{10... | collective-permute-start | bytes 129032 | tf_op jit(solution)/shard_map/ppermute | solution.py:316
  44.8 5.8 %collective-permute-start.12 = (bf16[168,128]{1,0:T(8,128)(2,1)S(1)}, bf16[168,128]{1,0:T(8,128)(2,1)S(1)}, u32[]{:S(2)}, u32[]{:S(2)}) collective-permute-start(bf16[168,128]{1,0:T(8,128)(2,1)S(1)} %shard_map.92.mine), channel_id=1, source_target_pairs={{0,8},{8,16},{16,24},{24,0},{1,9},{9,17},{17,25},{25,1},{2,10},{10... | collective-permute-start | bytes 129032 | tf_op jit(solution)/shard_map/ppermute | solution.py:316

commit v3 on v2

--- a/solution.py
+++ b/solution.py
@@ -3,7 +3,6 @@
 
 import jax
 import jax.numpy as jnp
-import numpy as np
 from jax import lax
 from jax.experimental import pallas as pl
 from jax.experimental.pallas import tpu as pltpu
@@ -36,13 +35,16 @@
     )(*args)
 
 
-def box_matrix(width):
-    a, b, s = np.meshgrid(np.arange(3), np.arange(3), np.arange(width), indexing="ij")
-    a, b, s = (x.reshape(-1, 1) for x in (a, b, s))
-    row, col = np.meshgrid(np.arange(4), np.arange(2 * width), indexing="ij")
-    row, col = (x.reshape(1, -1) for x in (row, col))
-    dr, dc = row - (2 - a), col - (2 * s + 1 - b)
-    return ((dr >= 0) & (dr <= 1) & (dc >= 0) & (dc <= 1)).astype(np.float32)
+def matrix_kernel(width, out):
+    column = lax.broadcasted_iota(jnp.int32, (width, 8 * width), 1)
+    line, col = column // (2 * width), column % (2 * width)
+    first = 2 * lax.broadcasted_iota(jnp.int32, (width, 8 * width), 0) + 1
+    for a in range(3):
+        rows = (line == 2 - a) | (line == 3 - a)
+        for b in range(3):
+            inside = rows & ((col == first - b) | (col == first + 1 - b))
+            t = 3 * a + b
+            out[t * width : (t + 1) * width, :] = jnp.where(inside, 1.0, 0.0).astype(BF16)
 
 
 def box_kernel(sizes, grads, weight_far, box, g_out, *rest):
@@ -129,43 +131,19 @@
         sends[d - 1][...] = (keep[p] + got[p].astype(F32)).astype(BF16)
 
 
-def square_kernel(n_q, n_clip, base, size, keep, *rest):
-    got, mine, sends = rest[: n_q - 1], rest[n_q - 1], rest[n_q : n_q + n_clip - 1]
-    total = rest[-1]
+def square_kernel(scale, keep, *rest):
     value = keep[...]
-    for block in got:
-        value = value + block[...].astype(F32)
-    total[...] = value
-    z = lax.axis_index("clip")
-    for d in range(n_clip):
-        to = lax.rem(z + d, n_clip)
-        piece = total[pl.ds(pl.multiple_of(to * base, 8), size), :]
-        if d == 0:
-            mine[...] = piece
-        else:
-            sends[d - 1][...] = piece.astype(BF16)
-
-
-def piece_kernel(scale, mine, *rest):
-    value = mine[...]
     for block in rest[:-1]:
         value = value + block[...].astype(F32)
     rest[-1][...] = (value * scale).astype(BF16)
 
 
-def final_kernel(n_clip, base, chunk, CO, mine, *rest):
-    got, out, total, even = rest[: n_clip - 1], rest[n_clip - 1], rest[n_clip], rest[n_clip + 1]
-    z = lax.axis_index("clip")
-    for d in range(n_clip):
-        source = lax.rem(z - d + n_clip, n_clip)
-        block = mine if d == 0 else got[d - 1]
-        start = pl.multiple_of(source * base, 8)
-        total[pl.ds(start, base), :] = block[:base].astype(F32)
-
-        @pl.when(source == n_clip - 1)
-        def _():
-            total[n_clip * base :, :] = block[base:].astype(F32)
-
+def pair_kernel(mine, got, out):
+    out[...] = (mine[...].astype(F32) + got[...].astype(F32)).astype(BF16)
+
+
+def final_kernel(chunk, CO, mine, got, out, total, even):
+    total[...] = mine[...].astype(F32) + got[...].astype(F32)
     half, low = chunk // 2, CO - 128
     side = total[chunk:]
     even[:half, :low] = side[:, :low]
@@ -208,7 +186,7 @@
 
 def direct(n_frame, n_row, n_clip):
     n_q = n_frame * n_row // 2
-    return n_frame % 2 == 0 and 1 < n_q <= 8 and n_q & (n_q - 1) == 0 and n_clip > 1
+    return n_frame % 2 == 0 and 1 < n_q <= 8 and n_q & (n_q - 1) == 0 and n_clip > 1 and n_clip & (n_clip - 1) == 0
 
 
 def local(features, time_weight, time_bias, space_weight, pixel_grads, frame_order):
@@ -220,6 +198,9 @@
     order = frame_order.reshape(-1)
     both = ("frame", "row")
 
+    (box,) = kernel_call(
+        functools.partial(matrix_kernel, W), [struct((9 * W, 8 * W), BF16)], 0, [], flops=10**10
+    )
     feats = features.reshape(F, rW, C)
     own, prior = [feats], []
     for d in range(1, n_row):
@@ -232,7 +213,6 @@
         ]
         prior.append(lax.ppermute(feats, both, route))
 
-    box = jnp.asarray(box_matrix(W), BF16)
     g, *bands = kernel_call(
         functools.partial(box_kernel, (S, HR, W, C, CO, r, n_row)),
         [struct((9, pixels, CO), BF16)] + [struct((S, rW, C), BF16)] * n_row,
@@ -299,26 +279,20 @@
             lax.ppermute(sends[d - 1], both, [(i, square(i, d)) for i in range(n_dev)])
             for d in range(1, n_q)
         ]
-        base = packed // n_clip // 8 * 8
-        size = packed - base * (n_clip - 1)
-        mine, *sends = kernel_call(
-            functools.partial(square_kernel, n_q, n_clip, base, size),
-            [struct((size, 128), F32)] + [struct((size, 128), BF16)] * (n_clip - 1),
-            0,
-            [mine] + got,
-            [pltpu.VMEM((packed, 128), F32)],
-        )
-        shift = [[(i, (i + d) % n_clip) for i in range(n_clip)] for d in range(1, n_clip)]
-        got = [lax.ppermute(x, "clip", route) for x, route in zip(sends, shift)]
         (mine,) = kernel_call(
-            functools.partial(piece_kernel, scale), [struct((size, 128), BF16)], 0, [mine] + got
-        )
-        got = [lax.ppermute(mine, "clip", route) for route in shift]
+            functools.partial(square_kernel, scale), [struct((packed, 128), BF16)], 0, [mine] + got
+        )
+        mask = n_clip - 1
+        while mask:
+            got = lax.ppermute(mine, "clip", [(i, i ^ mask) for i in range(n_clip)])
+            if mask > 1:
+                (mine,) = kernel_call(pair_kernel, [struct((packed, 128), BF16)], 0, [mine, got])
+            mask //= 2
         (flat,) = kernel_call(
-            functools.partial(final_kernel, n_clip, base, chunk, CO),
+            functools.partial(final_kernel, chunk, CO),
             [struct((packed, 128), F32)],
             0,
-            [mine] + got,
+            [mine, got],
             [pltpu.VMEM((packed, 128), F32), pltpu.VMEM((chunk, 128), F32)],
         )
         weight_grad = flat.reshape(-1)

time: 51.9 us -> 48 us (0.925)
  the two profiles are of different devices: /device:TPU:0 before, /device:TPU:1 now
where the time goes in v3:
time: 48 us; the launch traced here: 47.8 us
  starting transfers between devices  23.2 us (48%)
  waiting for transfers between devices  16.2 us (34%)
  Pallas kernels  7.59 us (16%)
  between operations  0.78 us (2%)
    pallas_call x9, Pallas kernels, kernel_call(): pl.pallas_call(body, out_shape=outs, in_specs=specs, out_specs=[VMEM] * l...  7.59 us
    ppermute x2, starting transfers between devices, local(): prior.append(lax.ppermute(feats, both, route))  7.51 us
    ppermute x2, starting transfers between devices, local(): got = lax.ppermute(mine, 'clip', [(i, i ^ mask) for i in range(n_clip)])  7.46 us
    ppermute x3, waiting for transfers between devices, local(): lax.ppermute(sends[d - 1], both, [(i, square(i, d)) for i in range(n_dev)])  7.23 us
    ppermute x1, starting transfers between devices, local(): lax.ppermute(first, 'frame', [(i + 1, i) for i in range(n_frame - 1)])  3.53 us
    ppermute x3, starting transfers between devices, local(): lax.ppermute(sends[d - 1], both, [(i, square(i, d)) for i in range(n_dev)])  2.71 us
    ppermute x2, waiting for transfers between devices, local(): got = lax.ppermute(mine, 'clip', [(i, i ^ mask) for i in range(n_clip)])  2.56 us
    ppermute x1, waiting for transfers between devices, local(): lax.ppermute(first, 'frame', [(i + 1, i) for i in range(n_frame - 1)])  2.46 us
  transfers between devices with their start and end apart: 11, of which 6 were waited for; matrix products, arithmetic and copies ran while one was open for 0% of the time, Pallas kernels for 7%

profile of v3, /device:TPU:1, one launch (start us, length us, event | category | flops | bytes accessed | tf_op | source)
XLA Modules:
  0.0 47.8 jit_solution(16961553576130041127)
XLA Ops:
  0.6 0.0 copy-start.1
  0.6 0.0 copy-start.2
  0.6 5.6 %collective-permute-start.4 = (bf16[4,32,384]{2,1,0:T(8,128)(2,1)}, bf16[4,32,384]{2,1,0:T(8,128)(2,1)S(1)}, u32[]{:S(2)}, u32[]{:S(2)}) collective-permute-start(bf16[4,32,384]{2,1,0:T(8,128)(2,1)} %bitcast.13), channel_id=1, source_target_pairs={{0,3},{1,2},{2,5},{3,4},{4,7},{5,6},{8,11},{9,10},{10,13},{11,12},... | collective-permute-start | bytes 294920 | tf_op jit(solution)/shard_map/ppermute | solution.py:214
  6.2 1.9 %collective-permute-start.3 = (bf16[4,32,384]{2,1,0:T(8,128)(2,1)}, bf16[4,32,384]{2,1,0:T(8,128)(2,1)S(1)}, u32[]{:S(2)}, u32[]{:S(2)}) collective-permute-start(bf16[4,32,384]{2,1,0:T(8,128)(2,1)} %bitcast.14), channel_id=1, source_target_pairs={{0,2},{1,3},{2,4},{3,5},{4,6},{5,7},{8,10},{9,11},{10,12},{11,13},... | collective-permute-start | bytes 294920 | tf_op jit(solution)/shard_map/ppermute | solution.py:214
  8.2 0.3 collective-permute-start.2
  8.6 0.0 copy-start
  8.6 0.0 copy-start.3
  8.6 0.0 copy-start.4
  8.6 0.0 copy-start.5
  8.6 0.0 copy-done.1
  8.6 0.0 copy-done.2
  8.6 1.5 %shard_map.78 = (bf16[9,256,192]{2,1,0:T(8,128)(2,1)S(1)}, bf16[4,32,384]{2,1,0:T(8,128)(2,1)S(1)}, bf16[4,32,384]{2,1,0:T(8,128)(2,1)S(1)}) custom-call(bf16[4,256,192]{2,1,0:T(8,128)(2,1)S(1)} %bitcast.12, bf16[9,192,384]{2,1,0:T(8,128)(2,1)S(1)} %bitcast.11, bf16[288,256]{1,0:T(8,128)(2,1)S(1)} %shard_map.77.box), custom_call_target="tpu_custom_call" | custom-call | flops 339738624 | bytes 2949120 | tf_op jit(solution)/shard_map/pallas_call | solution.py:27
  10.1 0.0 collective-permute-done.4.rest_3_
  10.1 0.0 collective-permute-done.3.rest_2_
  10.1 2.2 %collective-permute-done.2.rest_1_ = bf16[4,32,384]{2,1,0:T(8,128)(2,1)S(1)} collective-permute-done((bf16[4,32,384]{2,1,0:T(8,128)(2,1)}, bf16[4,32,384]{2,1,0:T(8,128)(2,1)S(1)}, u32[]{:S(2)}, u32[]{:S(2)}) %collective-permute-start.2) | collective-permute-done | bytes 98336 | tf_op jit(solution)/shard_map/ppermute | solution.py:207
  12.3 0.0 copy-done
  12.3 0.0 copy-done.3
  12.3 0.0 copy-done.4
  12.3 0.0 copy-done.5
  12.3 2.9 %shard_map.81 = (f32[4,648,128]{2,1,0:T(8,128)S(1)}, bf16[4,648,128]{2,1,0:T(8,128)(2,1)S(1)}) custom-call(s32[8]{0:T(128)S(1)} %bitcast.18, f32[6,128]{1,0:T(8,128)S(1)} %bitcast.17, bf16[3,384,768]{2,1,0:T(8,128)(2,1)S(1)} %copy-done, bf16[9,256,192]{2,1,0:T(8,128)(2,1)S(1)} %get-tuple-element.17.g, bf16[4,32,384]{2,1,0:T(8,128)(2,1)S(1)} %bitcast.16, ...), custom_call_target="tpu_custom_call" | custom-call | flops 792723456 | bytes 5041184 | tf_op jit(solution)/shard_map/pallas_call | solution.py:27
  15.2 1.4 %collective-permute-start.5 = (bf16[4,648,128]{2,1,0:T(8,128)(2,1)S(1)}, bf16[4,648,128]{2,1,0:T(8,128)(2,1)S(1)}, u32[]{:S(2)}, u32[]{:S(2)}) collective-permute-start(bf16[4,648,128]{2,1,0:T(8,128)(2,1)S(1)} %get-tuple-element.19), channel_id=1, source_target_pairs={{0,2},{1,3},{2,0},{3,1},{4,6},{5,7},{6,4},{7,5},{8,10},{9,11},{10,... | collective-permute-start | bytes 1990664 | tf_op jit(solution)/shard_map/ppermute | solution.py:263
  16.6 1.7 %collective-permute-done.5.got = bf16[4,648,128]{2,1,0:T(8,128)(2,1)S(1)} collective-permute-done((bf16[4,648,128]{2,1,0:T(8,128)(2,1)S(1)}, bf16[4,648,128]{2,1,0:T(8,128)(2,1)S(1)}, u32[]{:S(2)}, u32[]{:S(2)}) %collective-permute-start.5) | collective-permute-done | bytes 663584 | tf_op jit(solution)/shard_map/ppermute | solution.py:263
  18.3 0.1 shard_map.82
  18.5 0.3 collective-permute-start.6
  18.8 0.1 collective-permute-start.7
  19.0 2.3 %collective-permute-start.8 = (bf16[648,128]{1,0:T(8,128)(2,1)S(1)}, bf16[648,128]{1,0:T(8,128)(2,1)S(1)}, u32[]{:S(2)}, u32[]{:S(2)}) collective-permute-start(bf16[648,128]{1,0:T(8,128)(2,1)S(1)} %get-tuple-element.23), channel_id=1, source_target_pairs={{0,5},{1,4},{2,7},{3,6},{4,1},{5,0},{6,3},{7,2},{8,13},{9,12},{10,... | collective-permute-start | bytes 497672 | tf_op jit(solution)/shard_map/ppermute | solution.py:279
  21.2 2.8 %collective-permute-done.6.rest_0_ = bf16[648,128]{1,0:T(8,128)(2,1)S(1)} collective-permute-done((bf16[648,128]{1,0:T(8,128)(2,1)S(1)}, bf16[648,128]{1,0:T(8,128)(2,1)S(1)}, u32[]{:S(2)}, u32[]{:S(2)}) %collective-permute-start.6) | collective-permute-done | bytes 165920 | tf_op jit(solution)/shard_map/ppermute | solution.py:279
  24.0 0.0 collective-permute-done.7.rest_1_
  24.0 4.4 %collective-permute-done.8.rest_2_ = bf16[648,128]{1,0:T(8,128)(2,1)S(1)} collective-permute-done((bf16[648,128]{1,0:T(8,128)(2,1)S(1)}, bf16[648,128]{1,0:T(8,128)(2,1)S(1)}, u32[]{:S(2)}, u32[]{:S(2)}) %collective-permute-start.8) | collective-permute-done | bytes 165920 | tf_op jit(solution)/shard_map/ppermute | solution.py:279
  28.4 0.1 shard_map.83.mine
  28.5 3.4 %collective-permute-start.9 = (bf16[648,128]{1,0:T(8,128)(2,1)S(1)}, bf16[648,128]{1,0:T(8,128)(2,1)S(1)}, u32[]{:S(2)}, u32[]{:S(2)}) collective-permute-start(bf16[648,128]{1,0:T(8,128)(2,1)S(1)} %shard_map.83.mine), channel_id=1, source_target_pairs={{0,24},{8,16},{16,8},{24,0},{1,25},{9,17},{17,9},{25,1},{2,26},{10... | collective-permute-start | bytes 497672 | tf_op jit(solution)/shard_map/ppermute | solution.py:287
  31.9 0.3 collective-permute-start
  32.2 2.6 %collective-permute-done.9.got = bf16[648,128]{1,0:T(8,128)(2,1)S(1)} collective-permute-done((bf16[648,128]{1,0:T(8,128)(2,1)S(1)}, bf16[648,128]{1,0:T(8,128)(2,1)S(1)}, u32[]{:S(2)}, u32[]{:S(2)}) %collective-permute-start.9) | collective-permute-done | bytes 165920 | tf_op jit(solution)/shard_map/ppermute | solution.py:287
  34.8 4.1 %collective-permute-start.10 = (bf16[648,128]{1,0:T(8,128)(2,1)S(1)}, bf16[648,128]{1,0:T(8,128)(2,1)S(1)}, u32[]{:S(2)}, u32[]{:S(2)}) collective-permute-start(bf16[648,128]{1,0:T(8,128)(2,1)S(1)} %shard_map.84.mine), channel_id=1, source_target_pairs={{0,8},{8,0},{16,24},{24,16},{1,9},{9,1},{17,25},{25,17},{2,10},{10... | collective-permute-start | bytes 497672 | tf_op jit(solution)/shard_map/ppermute | solution.py:287
  38.9 0.0 collective-permute-done.rest_1_
  38.9 0.6 %shard_map.79 = (bf16[2,128,384]{2,1,0:T(8,128)(2,1)S(1)}, bf16[2,64,384]{2,1,0:T(8,128)(2,1)S(1)}) custom-call(s32[8]{0:T(128)S(1)} %bitcast.19, bf16[4,32,384]{2,1,0:T(8,128)(2,1)S(1)} %get-tuple-element.13.rest_0_, bf16[4,32,384]{2,1,0:T(8,128)(2,1)S(1)} %collective-permute-done.rest_1_), custom_call_target="tpu_custom_call" | custom-call | bytes 491552 | tf_op jit(solution)/shard_map/pallas_call | solution.py:27
  39.5 3.5 %collective-permute-start.1 = (bf16[2,64,384]{2,1,0:T(8,128)(2,1)S(1)}, bf16[2,64,384]{2,1,0:T(8,128)(2,1)S(1)}, u32[]{:S(2)}, u32[]{:S(2)}) collective-permute-start(bf16[2,64,384]{2,1,0:T(8,128)(2,1)S(1)} %get-tuple-element.16), channel_id=1, source_target_pairs={{2,0},{4,2},{6,4},{3,1},{5,3},{7,5},{10,8},{12,10},{14,12},{11,9},... | collective-permute-start | bytes 294920 | tf_op jit(solution)/shard_map/ppermute | solution.py:313
  43.1 2.5 %collective-permute-done.1.later = bf16[2,64,384]{2,1,0:T(8,128)(2,1)S(1)} collective-permute-done((bf16[2,64,384]{2,1,0:T(8,128)(2,1)S(1)}, bf16[2,64,384]{2,1,0:T(8,128)(2,1)S(1)}, u32[]{:S(2)}, u32[]{:S(2)}) %collective-permute-start.1) | collective-permute-done | bytes 98336 | tf_op jit(solution)/shard_map/ppermute | solution.py:313
  45.5 1.4 %shard_map.80 = bf16[128,384]{1,0:T(8,128)(2,1)} custom-call(bf16[2,128,384]{2,1,0:T(8,128)(2,1)S(1)} %get-tuple-element.15.natural, bf16[2,64,384]{2,1,0:T(8,128)(2,1)S(1)} %collective-permute-done.1.later, bf16[3,384,768]{2,1,0:T(8,128)(2,1)S(1)} %copy-done), custom_call_target="tpu_custom_call" | custom-call | flops 226492416 | bytes 2162688 | tf_op jit(solution)/shard_map/pallas_call | solution.py:27
  46.9 0.0 collective-permute-done.10.got
  46.9 0.9 %shard_map.85 = f32[648,128]{1,0:T(8,128)} custom-call(bf16[648,128]{1,0:T(8,128)(2,1)S(1)} %shard_map.84.mine, bf16[648,128]{1,0:T(8,128)(2,1)S(1)} %collective-permute-done.10.got), custom_call_target="tpu_custom_call" | custom-call | bytes 663552 | tf_op jit(solution)/shard_map/pallas_call | solution.py:27
  (2 shorter events, 0.1 us)
Async XLA Ops:
  0.6 8.0 %copy-start.1 = (bf16[3,3,384,192]{2,3,1,0:T(8,128)(2,1)S(1)}, bf16[3,3,384,192]{2,3,1,0:T(8,128)(2,1)}, u32[]{:S(2)}) copy-start(bf16[3,3,384,192]{2,3,1,0:T(8,128)(2,1)} %param.9) | copy-start | bytes 3981316
  0.6 8.0 %copy-start.2 = (bf16[1,4,4,64,192]{4,3,2,1,0:T(8,128)(2,1)S(1)}, bf16[1,4,4,64,192]{4,3,2,1,0:T(8,128)(2,1)}, u32[]{:S(2)}) copy-start(bf16[1,4,4,64,192]{4,3,2,1,0:T(8,128)(2,1)} %param.10) | copy-start | bytes 1179652
  0.6 9.5 %collective-permute-start.4 = (bf16[4,32,384]{2,1,0:T(8,128)(2,1)}, bf16[4,32,384]{2,1,0:T(8,128)(2,1)S(1)}, u32[]{:S(2)}, u32[]{:S(2)}) collective-permute-start(bf16[4,32,384]{2,1,0:T(8,128)(2,1)} %bitcast.13), channel_id=1, source_target_pairs={{0,3},{1,2},{2,5},{3,4},{4,7},{5,6},{8,11},{9,10},{10,13},{11,12},... | collective-permute-start | bytes 294920 | tf_op jit(solution)/shard_map/ppermute | solution.py:214
  6.2 3.9 %collective-permute-start.3 = (bf16[4,32,384]{2,1,0:T(8,128)(2,1)}, bf16[4,32,384]{2,1,0:T(8,128)(2,1)S(1)}, u32[]{:S(2)}, u32[]{:S(2)}) collective-permute-start(bf16[4,32,384]{2,1,0:T(8,128)(2,1)} %bitcast.14), channel_id=1, source_target_pairs={{0,2},{1,3},{2,4},{3,5},{4,6},{5,7},{8,10},{9,11},{10,12},{11,13},... | collective-permute-start | bytes 294920 | tf_op jit(solution)/shard_map/ppermute | solution.py:214
  8.2 4.1 %collective-permute-start.2 = (bf16[4,32,384]{2,1,0:T(8,128)(2,1)}, bf16[4,32,384]{2,1,0:T(8,128)(2,1)S(1)}, u32[]{:S(2)}, u32[]{:S(2)}) collective-permute-start(bf16[4,32,384]{2,1,0:T(8,128)(2,1)} %bitcast.15), channel_id=1, source_target_pairs={{0,1},{1,0},{2,3},{3,2},{4,5},{5,4},{6,7},{7,6},{8,9},{9,8},{10,11... | collective-permute-start | bytes 294920 | tf_op jit(solution)/shard_map/ppermute | solution.py:207
  8.6 3.7 %copy-start = (bf16[3,384,768]{2,1,0:T(8,128)(2,1)S(1)}, bf16[3,384,768]{2,1,0:T(8,128)(2,1)}, u32[]{:S(2)}) copy-start(bf16[3,384,768]{2,1,0:T(8,128)(2,1)} %time_weight.3) | copy-start | bytes 5308420
  8.6 3.7 %copy-start.3 = (bf16[1,4,1,32,384]{4,3,2,1,0:T(8,128)(2,1)S(1)}, bf16[1,4,1,32,384]{4,3,2,1,0:T(8,128)(2,1)}, u32[]{:S(2)}) copy-start(bf16[1,4,1,32,384]{4,3,2,1,0:T(8,128)(2,1)} %param.6) | copy-start | bytes 294916
  8.6 3.7 %copy-start.4 = (f32[768]{0:T(1024)S(1)}, f32[768]{0:T(1024)}, u32[]{:S(2)}) copy-start(f32[768]{0:T(1024)} %param.8) | copy-start | bytes 9220
  8.6 3.7 %copy-start.5 = (s32[1,1,8]{2,1,0:T(1,128)S(1)}, s32[1,1,8]{2,1,0:T(1,128)}, u32[]{:S(2)}) copy-start(s32[1,1,8]{2,1,0:T(1,128)} %param.11) | copy-start | bytes 100
  15.2 3.1 %collective-permute-start.5 = (bf16[4,648,128]{2,1,0:T(8,128)(2,1)S(1)}, bf16[4,648,128]{2,1,0:T(8,128)(2,1)S(1)}, u32[]{:S(2)}, u32[]{:S(2)}) collective-permute-start(bf16[4,648,128]{2,1,0:T(8,128)(2,1)S(1)} %get-tuple-element.19), channel_id=1, source_target_pairs={{0,2},{1,3},{2,0},{3,1},{4,6},{5,7},{6,4},{7,5},{8,10},{9,11},{10,... | collective-permute-start | bytes 1990664 | tf_op jit(solution)/shard_map/ppermute | solution.py:263
  18.5 5.5 %collective-permute-start.6 = (bf16[648,128]{1,0:T(8,128)(2,1)S(1)}, bf16[648,128]{1,0:T(8,128)(2,1)S(1)}, u32[]{:S(2)}, u32[]{:S(2)}) collective-permute-start(bf16[648,128]{1,0:T(8,128)(2,1)S(1)} %get-tuple-element.21), channel_id=1, source_target_pairs={{0,1},{1,0},{2,3},{3,2},{4,5},{5,4},{6,7},{7,6},{8,9},{9,8},{10,11... | collective-permute-start | bytes 497672 | tf_op jit(solution)/shard_map/ppermute | solution.py:279
  18.8 5.2 %collective-permute-start.7 = (bf16[648,128]{1,0:T(8,128)(2,1)S(1)}, bf16[648,128]{1,0:T(8,128)(2,1)S(1)}, u32[]{:S(2)}, u32[]{:S(2)}) collective-permute-start(bf16[648,128]{1,0:T(8,128)(2,1)S(1)} %get-tuple-element.22), channel_id=1, source_target_pairs={{0,4},{1,5},{2,6},{3,7},{4,0},{5,1},{6,2},{7,3},{8,12},{9,13},{10,... | collective-permute-start | bytes 497672 | tf_op jit(solution)/shard_map/ppermute | solution.py:279
  19.0 9.5 %collective-permute-start.8 = (bf16[648,128]{1,0:T(8,128)(2,1)S(1)}, bf16[648,128]{1,0:T(8,128)(2,1)S(1)}, u32[]{:S(2)}, u32[]{:S(2)}) collective-permute-start(bf16[648,128]{1,0:T(8,128)(2,1)S(1)} %get-tuple-element.23), channel_id=1, source_target_pairs={{0,5},{1,4},{2,7},{3,6},{4,1},{5,0},{6,3},{7,2},{8,13},{9,12},{10,... | collective-permute-start | bytes 497672 | tf_op jit(solution)/shard_map/ppermute | solution.py:279
  28.5 6.2 %collective-permute-start.9 = (bf16[648,128]{1,0:T(8,128)(2,1)S(1)}, bf16[648,128]{1,0:T(8,128)(2,1)S(1)}, u32[]{:S(2)}, u32[]{:S(2)}) collective-permute-start(bf16[648,128]{1,0:T(8,128)(2,1)S(1)} %shard_map.83.mine), channel_id=1, source_target_pairs={{0,24},{8,16},{16,8},{24,0},{1,25},{9,17},{17,9},{25,1},{2,26},{10... | collective-permute-start | bytes 497672 | tf_op jit(solution)/shard_map/ppermute | solution.py:287
  31.9 7.0 %collective-permute-start = (bf16[4,32,384]{2,1,0:T(8,128)(2,1)S(1)}, bf16[4,32,384]{2,1,0:T(8,128)(2,1)S(1)}, u32[]{:S(2)}, u32[]{:S(2)}) collective-permute-start(bf16[4,32,384]{2,1,0:T(8,128)(2,1)S(1)} %get-tuple-element.14), channel_id=1, source_target_pairs={{0,1},{1,0},{2,3},{3,2},{4,5},{5,4},{6,7},{7,6},{8,9},{9,8},{10,11... | collective-permute-start | bytes 294920 | tf_op jit(solution)/shard_map/ppermute | solution.py:304
  34.8 12.1 %collective-permute-start.10 = (bf16[648,128]{1,0:T(8,128)(2,1)S(1)}, bf16[648,128]{1,0:T(8,128)(2,1)S(1)}, u32[]{:S(2)}, u32[]{:S(2)}) collective-permute-start(bf16[648,128]{1,0:T(8,128)(2,1)S(1)} %shard_map.84.mine), channel_id=1, source_target_pairs={{0,8},{8,0},{16,24},{24,16},{1,9},{9,1},{17,25},{25,17},{2,10},{10... | collective-permute-start | bytes 497672 | tf_op jit(solution)/shard_map/ppermute | solution.py:287
  39.5 6.0 %collective-permute-start.1 = (bf16[2,64,384]{2,1,0:T(8,128)(2,1)S(1)}, bf16[2,64,384]{2,1,0:T(8,128)(2,1)S(1)}, u32[]{:S(2)}, u32[]{:S(2)}) collective-permute-start(bf16[2,64,384]{2,1,0:T(8,128)(2,1)S(1)} %get-tuple-element.16), channel_id=1, source_target_pairs={{2,0},{4,2},{6,4},{3,1},{5,3},{7,5},{10,8},{12,10},{14,12},{11,9},... | collective-permute-start | bytes 294920 | tf_op jit(solution)/shard_map/ppermute | solution.py:313

commit v4 on v3

--- a/solution.py
+++ b/solution.py
@@ -79,56 +79,92 @@
         bands[d][...] = acts[:, pl.ds(start, r * W), :]
 
 
-def wgrad_kernel(sizes, plan, order, bias, time_weight, g, *rest):
-    S, HR, W, C, _, r, n_row, F = sizes
-    own, prior = rest[:n_row], rest[n_row : 2 * n_row]
-    n_out = 2 if plan else 1
-    outs = rest[2 * n_row : 2 * n_row + n_out]
-    ext, acts, picked, terms = rest[2 * n_row + n_out :]
+def act_kernel(sizes, order, bias, time_weight, feats, prior, *rest):
+    S, rW, n_row, F, C = sizes
+    outs, (ext, acts) = rest[:n_row], rest[n_row:]
+    for f in range(2, F + 2):
+        ext[f * rW : (f + 1) * rW, :] = feats[f - 2]
+    whole = jnp.where(lax.axis_index("frame") > 0, 1.0, 0.0)
+    for f in range(2):
+        ext[f * rW : (f + 1) * rW, :] = (prior[F - 2 + f].astype(F32) * whole).astype(BF16)
+    row = jnp.concatenate([bias[i : i + 1, :] for i in range(bias.shape[0])], axis=1)
+    total = jnp.broadcast_to(row, (F * rW, 2 * C))
+    for k in range(3):
+        total = total + jnp.dot(
+            ext[k * rW : (k + F) * rW, :], time_weight[k], preferred_element_type=F32
+        )
+    rounded = total.astype(BF16)
+    acts[0] = rounded[:, :C].reshape(F, rW, C)
+    acts[1] = rounded[:, C:].reshape(F, rW, C)
+    me = lax.axis_index("row")
+    for d in range(n_row):
+        holder = lax.rem(me + d, n_row)
+        for s in range(S):
+            o = order[holder * S + s]
+            outs[d][s] = acts[o % 2, o // 2]
+
+
+def transposed_acts(sizes, bands, picked):
+    S, rW, n_row = sizes
     me = lax.axis_index("row")
     for d in range(n_row):
         source = lax.rem(me - d + n_row, n_row)
-        for f in range(F + 2):
-            block = prior[d][F - 2 + f] if f < 2 else own[d][f - 2]
-            start = pl.multiple_of((f * HR + source * r) * W, W)
-            ext[pl.ds(start, r * W), :] = block
-    step = HR * W
-    row = jnp.concatenate([bias[i : i + 1, :] for i in range(bias.shape[0])], axis=1)
-    total = jnp.broadcast_to(row, (F * step, 2 * C))
-    for k in range(3):
-        total = total + jnp.dot(
-            ext[k * step : (k + F) * step, :], time_weight[k], preferred_element_type=F32
-        )
-    rounded = total.astype(BF16)
-    acts[0] = rounded[:, :C]
-    acts[1] = rounded[:, C:]
-    for s in range(S):
-        o = order[me * S + s]
-        start = pl.multiple_of((o // 2) * step, step)
-        picked[s * step : (s + 1) * step, :] = acts[o % 2, pl.ds(start, step), :]
-    left = picked[...].astype(F32).T.astype(BF16)
-    target = terms if plan else outs[0]
+        for s in range(S):
+            start = pl.multiple_of((s * n_row + source) * rW, rW)
+            picked[pl.ds(start, rW), :] = bands[d][s]
+    return picked[...].astype(F32).T.astype(BF16)
+
+
+def all_kernel(sizes, g, *rest):
+    n_row, C = sizes[2], rest[0].shape[-1]
+    out, picked = rest[n_row:]
+    left = transposed_acts(sizes, rest[:n_row], picked)
     for t in range(9):
-        target[t * C : (t + 1) * C, :] = jnp.dot(left, g[t], preferred_element_type=F32)
-    if plan:
-        n_q, chunk = plan
-        core = lax.rem(lax.axis_index("frame"), 2)
-        keep, send = outs
-        half = chunk // 2
-        for q in range(n_q):
-            for which, out in ((core, keep), (1 - core, send)):
-                index = ((q // n_row) * 2 + which) * n_row + q % n_row
-                rows = terms[pl.ds(pl.multiple_of(index * chunk, chunk), chunk), :].astype(out.dtype)
-                out[q, :chunk, :] = rows[:, :128]
-                out[q, chunk:, :] = jnp.concatenate([rows[:half, 128:], rows[half:, 128:]], axis=1)
-
-
-def join_kernel(n_q, n_row, keep, got, own, *sends):
-    q = (lax.axis_index("frame") // 2) * n_row + lax.axis_index("row")
-    own[...] = keep[q] + got[q].astype(F32)
-    for d in range(1, n_q):
-        p = jnp.bitwise_xor(q, d)
-        sends[d - 1][...] = (keep[p] + got[p].astype(F32)).astype(BF16)
+        out[t * C : (t + 1) * C, :] = jnp.dot(left, g[t], preferred_element_type=F32)
+
+
+def packed_chunk(plan, index, left, g, terms):
+    n_dev, chunk, C, _ = plan
+    for value in range(n_dev):
+
+        @pl.when(index == value)
+        def _():
+            begin, end = value * chunk, (value + 1) * chunk
+            for t in range(begin // C, (end + C - 1) // C):
+                lo, hi = max(begin, t * C), min(end, (t + 1) * C)
+                terms[lo - begin : hi - begin, :] = jnp.dot(
+                    left[lo - t * C : hi - t * C, :], g[t], preferred_element_type=F32
+                )
+
+    half = chunk // 2
+    side = jnp.concatenate([terms[:half, 128:], terms[half:, 128:]], axis=1)
+    return jnp.concatenate([terms[:, :128], side], axis=0)
+
+
+def chunk_index(d, other):
+    n_row = lax.axis_size("row")
+    frame = lax.axis_index("frame")
+    q = jnp.bitwise_xor((frame // 2) * n_row + lax.axis_index("row"), d)
+    core = lax.rem(frame, 2)
+    return ((q // n_row) * 2 + (1 - core if other else core)) * n_row + lax.rem(q, n_row)
+
+
+def send_kernel(sizes, plan, group, g, *rest):
+    if sizes:
+        n_row = sizes[2]
+        left, out, picked, terms = rest[n_row:]
+        left[...] = transposed_acts(sizes, rest[:n_row], picked)
+    else:
+        left, out, terms = rest
+    for j, d in enumerate(group):
+        out[j] = packed_chunk(plan, chunk_index(d, True), left, g, terms).astype(BF16)
+
+
+def keep_kernel(plan, group, g, left, got, *rest):
+    outs, terms = rest[:-1], rest[-1]
+    for j, d in enumerate(group):
+        value = packed_chunk(plan, chunk_index(d, False), left, g, terms) + got[j].astype(F32)
+        outs[j][...] = value.astype(outs[j].dtype)
 
 
 def square_kernel(scale, keep, *rest):
@@ -171,7 +207,9 @@
 def input_kernel(sizes, natural, later, time_weight, out, tail):
     rW, F, C = sizes
     tail[:, : F * rW, :] = natural[...]
-    tail[:, F * rW :, :] = later[...]
+    n_frame = lax.axis_size("frame")
+    whole = jnp.where(lax.axis_index("frame") < n_frame - 1, 1.0, 0.0)
+    tail[:, F * rW :, :] = (later[...].astype(F32) * whole).astype(BF16)
     total = jnp.zeros((F * rW, C), F32)
     for k in range(3):
         for p in range(2):
@@ -198,21 +236,12 @@
     order = frame_order.reshape(-1)
     both = ("frame", "row")
 
+    feats = features.reshape(F, rW, C)
+    forward = [(i, (i + 1) % n_frame) for i in range(n_frame)]
+    prior = lax.ppermute(feats, "frame", forward)
     (box,) = kernel_call(
         functools.partial(matrix_kernel, W), [struct((9 * W, 8 * W), BF16)], 0, [], flops=10**10
     )
-    feats = features.reshape(F, rW, C)
-    own, prior = [feats], []
-    for d in range(1, n_row):
-        own.append(lax.ppermute(feats, "row", [(i, (i + d) % n_row) for i in range(n_row)]))
-    for d in range(n_row):
-        route = [
-            (f * n_row + i, (f + 1) * n_row + (i + d) % n_row)
-            for f in range(n_frame - 1)
-            for i in range(n_row)
-        ]
-        prior.append(lax.ppermute(feats, both, route))
-
     g, *bands = kernel_call(
         functools.partial(box_kernel, (S, HR, W, C, CO, r, n_row)),
         [struct((9, pixels, CO), BF16)] + [struct((S, rW, C), BF16)] * n_row,
@@ -239,46 +268,62 @@
         and chunk % 16 == 0
         and CO == 192
     )
-    wg_sizes = (S, HR, W, C, CO, r, n_row, F)
     packed = chunk * CO // 128
-    wg = kernel_call(
-        functools.partial(wgrad_kernel, wg_sizes, (n_q, chunk) if fast else None),
-        [struct((n_q, packed, 128), F32), struct((n_q, packed, 128), BF16)]
-        if fast
-        else [struct((n_total, CO), F32)],
+    own, *others = kernel_call(
+        functools.partial(act_kernel, (S, rW, n_row, F, C)),
+        [struct((S, rW, C), BF16)] * n_row,
         1,
-        [order, time_bias.reshape(-1, 128), time_weight, g] + own + prior,
-        [
-            pltpu.VMEM(((F + 2) * HR * W, C), BF16),
-            pltpu.VMEM((2, F * HR * W, C), BF16),
-            pltpu.VMEM((pixels, C), BF16),
-            pltpu.VMEM((n_total if fast else 8, CO), F32),
-        ],
-        flops=2 * pixels * 9 * C * CO + 2 * F * HR * W * 6 * C * C,
-    )
+        [order, time_bias.reshape(-1, 128), time_weight, feats, prior],
+        [pltpu.VMEM(((F + 2) * rW, C), BF16), pltpu.VMEM((2, F, rW, C), BF16)],
+        flops=2 * F * rW * 6 * C * C,
+    )
+    acts = [own] + [
+        lax.ppermute(others[d - 1], "row", [(i, (i + d) % n_row) for i in range(n_row)])
+        for d in range(1, n_row)
+    ]
+    picked = pltpu.VMEM((pixels, C), BF16)
+    flops = 2 * pixels * 9 * C * CO
 
     scale = 1.0 / math.sqrt(2 * F * UR * UW * n_clip * n_frame)
     if fast:
-        keep, send = wg
-        got = lax.ppermute(
-            send, both, [(i, ((i // n_row) ^ 1) * n_row + i % n_row) for i in range(n_dev)]
-        )
-        mine, *sends = kernel_call(
-            functools.partial(join_kernel, n_q, n_row),
-            [struct((packed, 128), F32)] + [struct((packed, 128), BF16)] * (n_q - 1),
-            0,
-            [keep, got],
-        )
+        plan = (n_dev, chunk, C, CO)
+        terms = pltpu.VMEM((chunk, CO), F32)
+        groups = [[n_q - 1], list(range(1, n_q - 1)), [0]]
+        groups = [group for group in groups if group]
+        swap = [(i, ((i // n_row) ^ 1) * n_row + i % n_row) for i in range(n_dev)]
 
         def square(i, d):
             f, j = i // n_row, i % n_row
             p = ((f // 2) * n_row + j) ^ d
             return ((p // n_row) * 2 + f % 2) * n_row + p % n_row
 
-        got = [
-            lax.ppermute(sends[d - 1], both, [(i, square(i, d)) for i in range(n_dev)])
-            for d in range(1, n_q)
-        ]
+        got = []
+        for k, group in enumerate(groups):
+            left_out = [] if k else [struct((C, pixels), BF16)]
+            *first, send = kernel_call(
+                functools.partial(send_kernel, None if k else (S, rW, n_row), plan, group),
+                left_out + [struct((len(group), packed, 128), BF16)],
+                0,
+                [g] + ([left] if k else acts),
+                [terms] if k else [picked, terms],
+                flops=flops * len(group) // n_dev,
+            )
+            left = left if k else first[0]
+            swapped = lax.ppermute(send, both, swap)
+            shares = kernel_call(
+                functools.partial(keep_kernel, plan, group),
+                [struct((packed, 128), BF16 if d else F32) for d in group],
+                0,
+                [g, left, swapped],
+                [terms],
+                flops=flops * len(group) // n_dev,
+            )
+            for d, share in zip(group, shares):
+                if d:
+                    route = [(i, square(i, d)) for i in range(n_dev)]
+                    got.append(lax.ppermute(share, both, route))
+                else:
+                    mine = share
         (mine,) = kernel_call(
             functools.partial(square_kernel, scale), [struct((packed, 128), BF16)], 0, [mine] + got
         )
@@ -297,7 +342,15 @@
         )
         weight_grad = flat.reshape(-1)
     else:
-        shard = lax.psum_scatter(wg[0].reshape(-1), both, scatter_dimension=0, tiled=True)
+        (wg,) = kernel_call(
+            functools.partial(all_kernel, (S, rW, n_row)),
+            [struct((n_total, CO), F32)],
+            0,
+            [g] + acts,
+            [picked],
+            flops=flops,
+        )
+        shard = lax.psum_scatter(wg.reshape(-1), both, scatter_dimension=0, tiled=True)
         weight_grad = lax.psum(shard, "clip") * scale
 
     bands = [bands[0]] + [
@@ -310,7 +363,7 @@
         1,
         [order] + bands,
     )
-    later = lax.ppermute(first, "frame", [(i + 1, i) for i in range(n_frame - 1)])
+    later = lax.ppermute(first, "frame", [(j, i) for i, j in forward])
     (input_grad,) = kernel_call(
         functools.partial(input_kernel, (rW, F, C)),
         [struct((F * rW, C), BF16)],

time: 48 us -> 48.3 us (level)
  starting transfers between devices: 23.2 us -> 19.1 us
  local copies, waits for them, and re-layouts: 0.03 us -> 3.8 us
  Pallas kernels: 7.59 us -> 8.44 us
    ppermute x8 -> x9, starting transfers between devices: 15.5 us -> 11.3 us  [the longest x3 3.18 us: local(): got.append(lax.ppermute(share, both, route))]
    unnamed x12 -> x16, local copies, waits for them, and re-layouts: 0.03 us -> 3.8 us
    ppermute x1, starting transfers between devices: 0.27 us -> 1.26 us  [local(): lax.ppermute(bands[d], 'row', [(i, (i + d) % n_row) for i in range(n_row)])]
    ppermute x2, starting transfers between devices: 7.46 us -> 6.56 us  [local(): got = lax.ppermute(mine, 'clip', [(i, i ^ mask) for i in range(n_clip)])]
    pallas_call x9 -> x14, Pallas kernels: 7.59 us -> 8.44 us  [kernel_call(): pl.pallas_call(body, out_shape=outs, in_specs=specs, out_specs=[VMEM] * l...]
    ppermute x8 -> x9, waiting for transfers between devices: 13.6 us -> 13.4 us  [the longest x3 6.8 us: local(): got.append(lax.ppermute(share, both, route))]
  transfers between devices with their start and end apart: 11 -> 12, of which waited for: 6 -> 7; matrix products, arithmetic and copies ran while one was open for 0% -> 0% of each run, Pallas kernels for 7% -> 11%
where the time goes in v4:
time: 48.3 us; the launch traced here: 48.1 us
  starting transfers between devices  19.1 us (40%)
  waiting for transfers between devices  16 us (33%)
  Pallas kernels  8.44 us (17%)
  local copies, waits for them, and re-layouts  3.8 us (8%)
  between operations  0.73 us (2%)
    pallas_call x14, Pallas kernels, kernel_call(): pl.pallas_call(body, out_shape=outs, in_specs=specs, out_specs=[VMEM] * l...  8.44 us
    ppermute x3, waiting for transfers between devices, local(): got.append(lax.ppermute(share, both, route))  6.8 us
    ppermute x2, starting transfers between devices, local(): got = lax.ppermute(mine, 'clip', [(i, i ^ mask) for i in range(n_clip)])  6.56 us
    unnamed x16, local copies, waits for them, and re-layouts  3.8 us
    ppermute x1, waiting for transfers between devices, local(): later = lax.ppermute(first, 'frame', [(j, i) for i, j in forward])  3.41 us
    ppermute x3, starting transfers between devices, local(): got.append(lax.ppermute(share, both, route))  3.18 us
    ppermute x1, starting transfers between devices, local(): prior = lax.ppermute(feats, 'frame', forward)  2.64 us
    ppermute x2, waiting for transfers between devices, local(): got = lax.ppermute(mine, 'clip', [(i, i ^ mask) for i in range(n_clip)])  2.63 us
  transfers between devices with their start and end apart: 12, of which 7 were waited for; matrix products, arithmetic and copies ran while one was open for 0% of the time, Pallas kernels for 11%

profile of v4, /device:TPU:1, one launch (start us, length us, event | category | flops | bytes accessed | tf_op | source)
XLA Modules:
  0.0 48.1 jit_solution(17591793343975673009)
XLA Ops:
  0.6 2.6 %collective-permute-start.2 = (bf16[4,32,384]{2,1,0:T(8,128)(2,1)}, bf16[4,32,384]{2,1,0:T(8,128)(2,1)S(1)}, u32[]{:S(2)}, u32[]{:S(2)}) collective-permute-start(bf16[4,32,384]{2,1,0:T(8,128)(2,1)} %bitcast.13), channel_id=1, source_target_pairs={{0,2},{2,4},{4,6},{6,0},{1,3},{3,5},{5,7},{7,1},{8,10},{10,12},{12... | collective-permute-start | bytes 294920 | tf_op jit(solution)/shard_map/ppermute | solution.py:241
  3.3 2.0 %collective-permute-done.2.prior = bf16[4,32,384]{2,1,0:T(8,128)(2,1)S(1)} collective-permute-done((bf16[4,32,384]{2,1,0:T(8,128)(2,1)}, bf16[4,32,384]{2,1,0:T(8,128)(2,1)S(1)}, u32[]{:S(2)}, u32[]{:S(2)}) %collective-permute-start.2) | collective-permute-done | bytes 98336 | tf_op jit(solution)/shard_map/ppermute | solution.py:241
  5.2 0.0 copy-start
  5.2 1.5 %copy-done = bf16[3,384,768]{2,1,0:T(8,128)(2,1)S(1)} copy-done((bf16[3,384,768]{2,1,0:T(8,128)(2,1)S(1)}, bf16[3,384,768]{2,1,0:T(8,128)(2,1)}, u32[]{:S(2)}) %copy-start) | copy-done | bytes 1769496
  6.7 0.0 copy-start.4
  6.7 0.9 %copy-done.4 = bf16[1,4,1,32,384]{4,3,2,1,0:T(8,128)(2,1)S(1)} copy-done((bf16[1,4,1,32,384]{4,3,2,1,0:T(8,128)(2,1)S(1)}, bf16[1,4,1,32,384]{4,3,2,1,0:T(8,128)(2,1)}, u32[]{:S(2)}) %copy-start.4) | copy-done | bytes 98328
  7.6 0.7 %copy-done.5 = f32[768]{0:T(1024)S(1)} copy-done((f32[768]{0:T(1024)S(1)}, f32[768]{0:T(1024)}, u32[]{:S(2)}) %copy-start.5) | copy-done | bytes 3096
  8.3 0.7 %copy-done.6 = s32[1,1,8]{2,1,0:T(1,128)S(1)} copy-done((s32[1,1,8]{2,1,0:T(1,128)S(1)}, s32[1,1,8]{2,1,0:T(1,128)}, u32[]{:S(2)}) %copy-start.6) | copy-done | bytes 56
  8.9 1.0 %shard_map.81 = (bf16[4,32,384]{2,1,0:T(8,128)(2,1)S(1)}, bf16[4,32,384]{2,1,0:T(8,128)(2,1)S(1)}) custom-call(s32[8]{0:T(128)S(1)} %bitcast.16, f32[6,128]{1,0:T(8,128)S(1)} %bitcast.15, bf16[3,384,768]{2,1,0:T(8,128)(2,1)S(1)} %copy-done, bf16[4,32,384]{2,1,0:T(8,128)(2,1)S(1)} %bitcast.14, bf16[4,32,384]{2,1,0:T(8,128)(2,1)S(1)} %collective-permute-done.2.prior), custom_call_target="tpu_custom_call" | custom-call | flops 226492416 | bytes 2165792 | tf_op jit(solution)/shard_map/pallas_call | solution.py:27
  10.0 0.0 copy-start.2
  10.0 0.0 copy-start.3
  10.0 1.3 %collective-permute-start.3 = (bf16[4,32,384]{2,1,0:T(8,128)(2,1)S(1)}, bf16[4,32,384]{2,1,0:T(8,128)(2,1)S(1)}, u32[]{:S(2)}, u32[]{:S(2)}) collective-permute-start(bf16[4,32,384]{2,1,0:T(8,128)(2,1)S(1)} %get-tuple-element.19), channel_id=1, source_target_pairs={{0,1},{1,0},{2,3},{3,2},{4,5},{5,4},{6,7},{7,6},{8,9},{9,8},{10,11... | collective-permute-start | bytes 294920 | tf_op jit(solution)/shard_map/ppermute | solution.py:281
  11.3 0.0 copy-done.2
  11.3 0.1 copy-done.3
  11.4 1.5 %shard_map.78 = (bf16[9,256,192]{2,1,0:T(8,128)(2,1)S(1)}, bf16[4,32,384]{2,1,0:T(8,128)(2,1)S(1)}, bf16[4,32,384]{2,1,0:T(8,128)(2,1)S(1)}) custom-call(bf16[4,256,192]{2,1,0:T(8,128)(2,1)S(1)} %bitcast.12, bf16[9,192,384]{2,1,0:T(8,128)(2,1)S(1)} %bitcast.11, bf16[288,256]{1,0:T(8,128)(2,1)S(1)} %shard_map.77.box), custom_call_target="tpu_custom_call" | custom-call | flops 339738624 | bytes 2949120 | tf_op jit(solution)/shard_map/pallas_call | solution.py:27
  12.9 0.7 %collective-permute-done.3.rest_1_ = bf16[4,32,384]{2,1,0:T(8,128)(2,1)S(1)} collective-permute-done((bf16[4,32,384]{2,1,0:T(8,128)(2,1)S(1)}, bf16[4,32,384]{2,1,0:T(8,128)(2,1)S(1)}, u32[]{:S(2)}, u32[]{:S(2)}) %collective-permute-start.3) | collective-permute-done | bytes 98336 | tf_op jit(solution)/shard_map/ppermute | solution.py:281
  13.5 0.5 %shard_map.82 = (bf16[384,256]{1,0:T(8,128)(2,1)S(1)}, bf16[1,648,128]{2,1,0:T(8,128)(2,1)S(1)}) custom-call(bf16[9,256,192]{2,1,0:T(8,128)(2,1)S(1)} %get-tuple-element.17.g, bf16[4,32,384]{2,1,0:T(8,128)(2,1)S(1)} %get-tuple-element.18.rest_0_, bf16[4,32,384]{2,1,0:T(8,128)(2,1)S(1)} %collective-permute-done.3.rest_1_), custom_call_target="tpu_custom_call" | custom-call | flops 42467328 | bytes 1443840 | tf_op jit(solution)/shard_map/pallas_call | solution.py:27
  14.0 0.7 %shard_map.86 = bf16[2,648,128]{2,1,0:T(8,128)(2,1)S(1)} custom-call(bf16[9,256,192]{2,1,0:T(8,128)(2,1)S(1)} %get-tuple-element.17.g, bf16[384,256]{1,0:T(8,128)(2,1)S(1)} %get-tuple-element.20.rest_0_.left), custom_call_target="tpu_custom_call" | custom-call | flops 84934656 | bytes 1413120 | tf_op jit(solution)/shard_map/pallas_call | solution.py:27
  14.7 1.9 %collective-permute-start.7 = (bf16[2,648,128]{2,1,0:T(8,128)(2,1)S(1)}, bf16[2,648,128]{2,1,0:T(8,128)(2,1)S(1)}, u32[]{:S(2)}, u32[]{:S(2)}) collective-permute-start(bf16[2,648,128]{2,1,0:T(8,128)(2,1)S(1)} %shard_map.86), channel_id=1, source_target_pairs={{0,2},{1,3},{2,0},{3,1},{4,6},{5,7},{6,4},{7,5},{8,10},{9,11},{10,... | collective-permute-start | bytes 995336 | tf_op jit(solution)/shard_map/ppermute | solution.py:312
  16.6 0.1 collective-permute-start.5
  16.7 0.3 shard_map.83
  17.0 0.5 %collective-permute-start.4 = (bf16[1,648,128]{2,1,0:T(8,128)(2,1)S(1)}, bf16[1,648,128]{2,1,0:T(8,128)(2,1)S(1)}, u32[]{:S(2)}, u32[]{:S(2)}) collective-permute-start(bf16[1,648,128]{2,1,0:T(8,128)(2,1)S(1)} %shard_map.83), channel_id=1, source_target_pairs={{0,2},{1,3},{2,0},{3,1},{4,6},{5,7},{6,4},{7,5},{8,10},{9,11},{10,... | collective-permute-start | bytes 497672 | tf_op jit(solution)/shard_map/ppermute | solution.py:312
  17.5 0.6 %collective-permute-done.5.got = bf16[1,648,128]{2,1,0:T(8,128)(2,1)S(1)} collective-permute-done((bf16[1,648,128]{2,1,0:T(8,128)(2,1)S(1)}, bf16[1,648,128]{2,1,0:T(8,128)(2,1)S(1)}, u32[]{:S(2)}, u32[]{:S(2)}) %collective-permute-start.5) | collective-permute-done | bytes 165920 | tf_op jit(solution)/shard_map/ppermute | solution.py:312
  18.1 0.3 shard_map.85
  18.5 2.8 %collective-permute-start.6 = (bf16[648,128]{1,0:T(8,128)(2,1)S(1)}, bf16[648,128]{1,0:T(8,128)(2,1)S(1)}, u32[]{:S(2)}, u32[]{:S(2)}) collective-permute-start(bf16[648,128]{1,0:T(8,128)(2,1)S(1)} %shard_map.85), channel_id=1, source_target_pairs={{0,5},{1,4},{2,7},{3,6},{4,1},{5,0},{6,3},{7,2},{8,13},{9,12},{10,... | collective-permute-start | bytes 497672 | tf_op jit(solution)/shard_map/ppermute | solution.py:324
  21.2 0.0 collective-permute-done.7.got
  21.2 0.7 %shard_map.87 = (bf16[648,128]{1,0:T(8,128)(2,1)S(1)}, bf16[648,128]{1,0:T(8,128)(2,1)S(1)}) custom-call(bf16[9,256,192]{2,1,0:T(8,128)(2,1)S(1)} %get-tuple-element.17.g, bf16[384,256]{1,0:T(8,128)(2,1)S(1)} %get-tuple-element.20.rest_0_.left, bf16[2,648,128]{2,1,0:T(8,128)(2,1)S(1)} %collective-permute-done.7.got), custom_call_target="tpu_custom_call" | custom-call | flops 84934656 | bytes 1744896 | tf_op jit(solution)/shard_map/pallas_call | solution.py:27
  21.9 0.3 collective-permute-start.8
  22.2 0.1 collective-permute-start.9
  22.3 0.0 collective-permute-done.4.got
  22.3 0.4 shard_map.84.keep
  22.7 2.8 %collective-permute-done.6.rest_0_ = bf16[648,128]{1,0:T(8,128)(2,1)S(1)} collective-permute-done((bf16[648,128]{1,0:T(8,128)(2,1)S(1)}, bf16[648,128]{1,0:T(8,128)(2,1)S(1)}, u32[]{:S(2)}, u32[]{:S(2)}) %collective-permute-start.6) | collective-permute-done | bytes 165920 | tf_op jit(solution)/shard_map/ppermute | solution.py:324
  25.5 4.0 %collective-permute-done.8.rest_1_ = bf16[648,128]{1,0:T(8,128)(2,1)S(1)} collective-permute-done((bf16[648,128]{1,0:T(8,128)(2,1)S(1)}, bf16[648,128]{1,0:T(8,128)(2,1)S(1)}, u32[]{:S(2)}, u32[]{:S(2)}) %collective-permute-start.8) | collective-permute-done | bytes 165920 | tf_op jit(solution)/shard_map/ppermute | solution.py:324
  29.5 0.0 collective-permute-done.9.rest_2_
  29.5 0.1 shard_map.88.mine
  29.6 3.5 %collective-permute-start.10 = (bf16[648,128]{1,0:T(8,128)(2,1)S(1)}, bf16[648,128]{1,0:T(8,128)(2,1)S(1)}, u32[]{:S(2)}, u32[]{:S(2)}) collective-permute-start(bf16[648,128]{1,0:T(8,128)(2,1)S(1)} %shard_map.88.mine), channel_id=1, source_target_pairs={{0,24},{8,16},{16,8},{24,0},{1,25},{9,17},{17,9},{25,1},{2,26},{10... | collective-permute-start | bytes 497672 | tf_op jit(solution)/shard_map/ppermute | solution.py:332
  33.1 1.3 %collective-permute-start = (bf16[4,32,384]{2,1,0:T(8,128)(2,1)S(1)}, bf16[4,32,384]{2,1,0:T(8,128)(2,1)S(1)}, u32[]{:S(2)}, u32[]{:S(2)}) collective-permute-start(bf16[4,32,384]{2,1,0:T(8,128)(2,1)S(1)} %get-tuple-element.14), channel_id=1, source_target_pairs={{0,1},{1,0},{2,3},{3,2},{4,5},{5,4},{6,7},{7,6},{8,9},{9,8},{10,11... | collective-permute-start | bytes 294920 | tf_op jit(solution)/shard_map/ppermute | solution.py:357
  34.4 2.6 %collective-permute-done.10.got = bf16[648,128]{1,0:T(8,128)(2,1)S(1)} collective-permute-done((bf16[648,128]{1,0:T(8,128)(2,1)S(1)}, bf16[648,128]{1,0:T(8,128)(2,1)S(1)}, u32[]{:S(2)}, u32[]{:S(2)}) %collective-permute-start.10) | collective-permute-done | bytes 165920 | tf_op jit(solution)/shard_map/ppermute | solution.py:332
  37.1 3.0 %collective-permute-start.11 = (bf16[648,128]{1,0:T(8,128)(2,1)S(1)}, bf16[648,128]{1,0:T(8,128)(2,1)S(1)}, u32[]{:S(2)}, u32[]{:S(2)}) collective-permute-start(bf16[648,128]{1,0:T(8,128)(2,1)S(1)} %shard_map.89.mine), channel_id=1, source_target_pairs={{0,8},{8,0},{16,24},{24,16},{1,9},{9,1},{17,25},{25,17},{2,10},{10... | collective-permute-start | bytes 497672 | tf_op jit(solution)/shard_map/ppermute | solution.py:332
  40.1 0.0 collective-permute-done.rest_1_
  40.1 0.0 copy-done.7
  40.1 0.6 %shard_map.79 = (bf16[2,128,384]{2,1,0:T(8,128)(2,1)S(1)}, bf16[2,64,384]{2,1,0:T(8,128)(2,1)S(1)}) custom-call(s32[8]{0:T(128)S(1)} %bitcast.17, bf16[4,32,384]{2,1,0:T(8,128)(2,1)S(1)} %get-tuple-element.13.rest_0_, bf16[4,32,384]{2,1,0:T(8,128)(2,1)S(1)} %collective-permute-done.rest_1_), custom_call_target="tpu_custom_call" | custom-call | bytes 491552 | tf_op jit(solution)/shard_map/pallas_call | solution.py:27
  40.7 1.7 %collective-permute-start.1 = (bf16[2,64,384]{2,1,0:T(8,128)(2,1)S(1)}, bf16[2,64,384]{2,1,0:T(8,128)(2,1)S(1)}, u32[]{:S(2)}, u32[]{:S(2)}) collective-permute-start(bf16[2,64,384]{2,1,0:T(8,128)(2,1)S(1)} %get-tuple-element.16), channel_id=1, source_target_pairs={{2,0},{4,2},{6,4},{0,6},{3,1},{5,3},{7,5},{1,7},{10,8},{12,10},{14... | collective-permute-start | bytes 294920 | tf_op jit(solution)/shard_map/ppermute | solution.py:366
  42.4 3.4 %collective-permute-done.1.later = bf16[2,64,384]{2,1,0:T(8,128)(2,1)S(1)} collective-permute-done((bf16[2,64,384]{2,1,0:T(8,128)(2,1)S(1)}, bf16[2,64,384]{2,1,0:T(8,128)(2,1)S(1)}, u32[]{:S(2)}, u32[]{:S(2)}) %collective-permute-start.1) | collective-permute-done | bytes 98336 | tf_op jit(solution)/shard_map/ppermute | solution.py:366
  45.8 0.0 copy-done.1
  45.8 1.4 %shard_map.80 = bf16[128,384]{1,0:T(8,128)(2,1)} custom-call(bf16[2,128,384]{2,1,0:T(8,128)(2,1)S(1)} %get-tuple-element.15.natural, bf16[2,64,384]{2,1,0:T(8,128)(2,1)S(1)} %collective-permute-done.1.later, bf16[3,384,768]{2,1,0:T(8,128)(2,1)S(1)} %copy-done.1), custom_call_target="tpu_custom_call" | custom-call | flops 226492416 | bytes 2162688 | tf_op jit(solution)/shard_map/pallas_call | solution.py:27
  47.2 0.0 collective-permute-done.11.got
  47.2 0.9 %shard_map.90 = f32[648,128]{1,0:T(8,128)} custom-call(bf16[648,128]{1,0:T(8,128)(2,1)S(1)} %shard_map.89.mine, bf16[648,128]{1,0:T(8,128)(2,1)S(1)} %collective-permute-done.11.got), custom_call_target="tpu_custom_call" | custom-call | bytes 663552 | tf_op jit(solution)/shard_map/pallas_call | solution.py:27
  (6 shorter events, 0.1 us)
Async XLA Ops:
  0.6 4.6 %collective-permute-start.2 = (bf16[4,32,384]{2,1,0:T(8,128)(2,1)}, bf16[4,32,384]{2,1,0:T(8,128)(2,1)S(1)}, u32[]{:S(2)}, u32[]{:S(2)}) collective-permute-start(bf16[4,32,384]{2,1,0:T(8,128)(2,1)} %bitcast.13), channel_id=1, source_target_pairs={{0,2},{2,4},{4,6},{6,0},{1,3},{3,5},{5,7},{7,1},{8,10},{10,12},{12... | collective-permute-start | bytes 294920 | tf_op jit(solution)/shard_map/ppermute | solution.py:241
  5.2 1.5 %copy-start = (bf16[3,384,768]{2,1,0:T(8,128)(2,1)S(1)}, bf16[3,384,768]{2,1,0:T(8,128)(2,1)}, u32[]{:S(2)}) copy-start(bf16[3,384,768]{2,1,0:T(8,128)(2,1)} %time_weight.3) | copy-start | bytes 5308420
  6.7 0.9 %copy-start.4 = (bf16[1,4,1,32,384]{4,3,2,1,0:T(8,128)(2,1)S(1)}, bf16[1,4,1,32,384]{4,3,2,1,0:T(8,128)(2,1)}, u32[]{:S(2)}) copy-start(bf16[1,4,1,32,384]{4,3,2,1,0:T(8,128)(2,1)} %param.6) | copy-start | bytes 294916
  7.6 0.7 %copy-start.5 = (f32[768]{0:T(1024)S(1)}, f32[768]{0:T(1024)}, u32[]{:S(2)}) copy-start(f32[768]{0:T(1024)} %param.8) | copy-start | bytes 9220
  8.3 0.7 %copy-start.6 = (s32[1,1,8]{2,1,0:T(1,128)S(1)}, s32[1,1,8]{2,1,0:T(1,128)}, u32[]{:S(2)}) copy-start(s32[1,1,8]{2,1,0:T(1,128)} %param.11) | copy-start | bytes 100
  10.0 1.4 %copy-start.2 = (bf16[3,3,384,192]{2,3,1,0:T(8,128)(2,1)S(1)}, bf16[3,3,384,192]{2,3,1,0:T(8,128)(2,1)}, u32[]{:S(2)}) copy-start(bf16[3,3,384,192]{2,3,1,0:T(8,128)(2,1)} %param.9) | copy-start | bytes 3981316
  10.0 1.4 %copy-start.3 = (bf16[1,4,4,64,192]{4,3,2,1,0:T(8,128)(2,1)S(1)}, bf16[1,4,4,64,192]{4,3,2,1,0:T(8,128)(2,1)}, u32[]{:S(2)}) copy-start(bf16[1,4,4,64,192]{4,3,2,1,0:T(8,128)(2,1)} %param.10) | copy-start | bytes 1179652
  10.0 3.5 %collective-permute-start.3 = (bf16[4,32,384]{2,1,0:T(8,128)(2,1)S(1)}, bf16[4,32,384]{2,1,0:T(8,128)(2,1)S(1)}, u32[]{:S(2)}, u32[]{:S(2)}) collective-permute-start(bf16[4,32,384]{2,1,0:T(8,128)(2,1)S(1)} %get-tuple-element.19), channel_id=1, source_target_pairs={{0,1},{1,0},{2,3},{3,2},{4,5},{5,4},{6,7},{7,6},{8,9},{9,8},{10,11... | collective-permute-start | bytes 294920 | tf_op jit(solution)/shard_map/ppermute | solution.py:281
  14.7 6.5 %collective-permute-start.7 = (bf16[2,648,128]{2,1,0:T(8,128)(2,1)S(1)}, bf16[2,648,128]{2,1,0:T(8,128)(2,1)S(1)}, u32[]{:S(2)}, u32[]{:S(2)}) collective-permute-start(bf16[2,648,128]{2,1,0:T(8,128)(2,1)S(1)} %shard_map.86), channel_id=1, source_target_pairs={{0,2},{1,3},{2,0},{3,1},{4,6},{5,7},{6,4},{7,5},{8,10},{9,11},{10,... | collective-permute-start | bytes 995336 | tf_op jit(solution)/shard_map/ppermute | solution.py:312
  16.6 1.5 %collective-permute-start.5 = (bf16[1,648,128]{2,1,0:T(8,128)(2,1)S(1)}, bf16[1,648,128]{2,1,0:T(8,128)(2,1)S(1)}, u32[]{:S(2)}, u32[]{:S(2)}) collective-permute-start(bf16[1,648,128]{2,1,0:T(8,128)(2,1)S(1)} %get-tuple-element.21), channel_id=1, source_target_pairs={{0,2},{1,3},{2,0},{3,1},{4,6},{5,7},{6,4},{7,5},{8,10},{9,11},{10,... | collective-permute-start | bytes 497672 | tf_op jit(solution)/shard_map/ppermute | solution.py:312
  17.0 5.3 %collective-permute-start.4 = (bf16[1,648,128]{2,1,0:T(8,128)(2,1)S(1)}, bf16[1,648,128]{2,1,0:T(8,128)(2,1)S(1)}, u32[]{:S(2)}, u32[]{:S(2)}) collective-permute-start(bf16[1,648,128]{2,1,0:T(8,128)(2,1)S(1)} %shard_map.83), channel_id=1, source_target_pairs={{0,2},{1,3},{2,0},{3,1},{4,6},{5,7},{6,4},{7,5},{8,10},{9,11},{10,... | collective-permute-start | bytes 497672 | tf_op jit(solution)/shard_map/ppermute | solution.py:312
  18.5 7.0 %collective-permute-start.6 = (bf16[648,128]{1,0:T(8,128)(2,1)S(1)}, bf16[648,128]{1,0:T(8,128)(2,1)S(1)}, u32[]{:S(2)}, u32[]{:S(2)}) collective-permute-start(bf16[648,128]{1,0:T(8,128)(2,1)S(1)} %shard_map.85), channel_id=1, source_target_pairs={{0,5},{1,4},{2,7},{3,6},{4,1},{5,0},{6,3},{7,2},{8,13},{9,12},{10,... | collective-permute-start | bytes 497672 | tf_op jit(solution)/shard_map/ppermute | solution.py:324
  21.9 7.6 %collective-permute-start.8 = (bf16[648,128]{1,0:T(8,128)(2,1)S(1)}, bf16[648,128]{1,0:T(8,128)(2,1)S(1)}, u32[]{:S(2)}, u32[]{:S(2)}) collective-permute-start(bf16[648,128]{1,0:T(8,128)(2,1)S(1)} %get-tuple-element.22), channel_id=1, source_target_pairs={{0,1},{1,0},{2,3},{3,2},{4,5},{5,4},{6,7},{7,6},{8,9},{9,8},{10,11... | collective-permute-start | bytes 497672 | tf_op jit(solution)/shard_map/ppermute | solution.py:324
  22.2 17.9 %copy-start.7 = (s32[1,1,8]{2,1,0:T(1,128)S(1)}, s32[1,1,8]{2,1,0:T(1,128)}, u32[]{:S(2)}) copy-start(s32[1,1,8]{2,1,0:T(1,128)} %param.11) | copy-start | bytes 100
  22.2 23.6 %copy-start.1 = (bf16[3,384,768]{2,1,0:T(8,128)(2,1)S(1)}, bf16[3,384,768]{2,1,0:T(8,128)(2,1)}, u32[]{:S(2)}) copy-start(bf16[3,384,768]{2,1,0:T(8,128)(2,1)} %time_weight.3) | copy-start | bytes 5308420
  22.2 7.3 %collective-permute-start.9 = (bf16[648,128]{1,0:T(8,128)(2,1)S(1)}, bf16[648,128]{1,0:T(8,128)(2,1)S(1)}, u32[]{:S(2)}, u32[]{:S(2)}) collective-permute-start(bf16[648,128]{1,0:T(8,128)(2,1)S(1)} %get-tuple-element.23), channel_id=1, source_target_pairs={{0,4},{1,5},{2,6},{3,7},{4,0},{5,1},{6,2},{7,3},{8,12},{9,13},{10,... | collective-permute-start | bytes 497672 | tf_op jit(solution)/shard_map/ppermute | solution.py:324
  29.6 7.4 %collective-permute-start.10 = (bf16[648,128]{1,0:T(8,128)(2,1)S(1)}, bf16[648,128]{1,0:T(8,128)(2,1)S(1)}, u32[]{:S(2)}, u32[]{:S(2)}) collective-permute-start(bf16[648,128]{1,0:T(8,128)(2,1)S(1)} %shard_map.88.mine), channel_id=1, source_target_pairs={{0,24},{8,16},{16,8},{24,0},{1,25},{9,17},{17,9},{25,1},{2,26},{10... | collective-permute-start | bytes 497672 | tf_op jit(solution)/shard_map/ppermute | solution.py:332
  33.1 7.0 %collective-permute-start = (bf16[4,32,384]{2,1,0:T(8,128)(2,1)S(1)}, bf16[4,32,384]{2,1,0:T(8,128)(2,1)S(1)}, u32[]{:S(2)}, u32[]{:S(2)}) collective-permute-start(bf16[4,32,384]{2,1,0:T(8,128)(2,1)S(1)} %get-tuple-element.14), channel_id=1, source_target_pairs={{0,1},{1,0},{2,3},{3,2},{4,5},{5,4},{6,7},{7,6},{8,9},{9,8},{10,11... | collective-permute-start | bytes 294920 | tf_op jit(solution)/shard_map/ppermute | solution.py:357
  37.1 10.1 %collective-permute-start.11 = (bf16[648,128]{1,0:T(8,128)(2,1)S(1)}, bf16[648,128]{1,0:T(8,128)(2,1)S(1)}, u32[]{:S(2)}, u32[]{:S(2)}) collective-permute-start(bf16[648,128]{1,0:T(8,128)(2,1)S(1)} %shard_map.89.mine), channel_id=1, source_target_pairs={{0,8},{8,0},{16,24},{24,16},{1,9},{9,1},{17,25},{25,17},{2,10},{10... | collective-permute-start | bytes 497672 | tf_op jit(solution)/shard_map/ppermute | solution.py:332
  40.7 5.1 %collective-permute-start.1 = (bf16[2,64,384]{2,1,0:T(8,128)(2,1)S(1)}, bf16[2,64,384]{2,1,0:T(8,128)(2,1)S(1)}, u32[]{:S(2)}, u32[]{:S(2)}) collective-permute-start(bf16[2,64,384]{2,1,0:T(8,128)(2,1)S(1)} %get-tuple-element.16), channel_id=1, source_target_pairs={{2,0},{4,2},{6,4},{0,6},{3,1},{5,3},{7,5},{1,7},{10,8},{12,10},{14... | collective-permute-start | bytes 294920 | tf_op jit(solution)/shard_map/ppermute | solution.py:366

commit v5 on v4

--- a/solution.py
+++ b/solution.py
@@ -79,46 +79,41 @@
         bands[d][...] = acts[:, pl.ds(start, r * W), :]
 
 
-def act_kernel(sizes, order, bias, time_weight, feats, prior, *rest):
+def transposed_acts(sizes, order, bias, time_weight, bands, ext, acts, picked):
     S, rW, n_row, F, C = sizes
-    outs, (ext, acts) = rest[:n_row], rest[n_row:]
-    for f in range(2, F + 2):
-        ext[f * rW : (f + 1) * rW, :] = feats[f - 2]
+    step = n_row * rW
+    own, prior = bands[:n_row], bands[n_row:]
+    me = lax.axis_index("row")
     whole = jnp.where(lax.axis_index("frame") > 0, 1.0, 0.0)
-    for f in range(2):
-        ext[f * rW : (f + 1) * rW, :] = (prior[F - 2 + f].astype(F32) * whole).astype(BF16)
+    for d in range(n_row):
+        source = lax.rem(me - d + n_row, n_row)
+        for f in range(F + 2):
+            start = pl.multiple_of(f * step + source * rW, rW)
+            if f < 2:
+                block = (prior[d][F - 2 + f].astype(F32) * whole).astype(BF16)
+            else:
+                block = own[d][f - 2]
+            ext[pl.ds(start, rW), :] = block
     row = jnp.concatenate([bias[i : i + 1, :] for i in range(bias.shape[0])], axis=1)
-    total = jnp.broadcast_to(row, (F * rW, 2 * C))
+    total = jnp.broadcast_to(row, (F * step, 2 * C))
     for k in range(3):
         total = total + jnp.dot(
-            ext[k * rW : (k + F) * rW, :], time_weight[k], preferred_element_type=F32
+            ext[k * step : (k + F) * step, :], time_weight[k], preferred_element_type=F32
         )
     rounded = total.astype(BF16)
-    acts[0] = rounded[:, :C].reshape(F, rW, C)
-    acts[1] = rounded[:, C:].reshape(F, rW, C)
-    me = lax.axis_index("row")
-    for d in range(n_row):
-        holder = lax.rem(me + d, n_row)
-        for s in range(S):
-            o = order[holder * S + s]
-            outs[d][s] = acts[o % 2, o // 2]
-
-
-def transposed_acts(sizes, bands, picked):
-    S, rW, n_row = sizes
-    me = lax.axis_index("row")
-    for d in range(n_row):
-        source = lax.rem(me - d + n_row, n_row)
-        for s in range(S):
-            start = pl.multiple_of((s * n_row + source) * rW, rW)
-            picked[pl.ds(start, rW), :] = bands[d][s]
+    acts[0] = rounded[:, :C]
+    acts[1] = rounded[:, C:]
+    for s in range(S):
+        o = order[me * S + s]
+        start = pl.multiple_of((o // 2) * step, step)
+        picked[s * step : (s + 1) * step, :] = acts[o % 2, pl.ds(start, step), :]
     return picked[...].astype(F32).T.astype(BF16)
 
 
-def all_kernel(sizes, g, *rest):
-    n_row, C = sizes[2], rest[0].shape[-1]
-    out, picked = rest[n_row:]
-    left = transposed_acts(sizes, rest[:n_row], picked)
+def all_kernel(sizes, order, bias, time_weight, g, *rest):
+    n_row, C = sizes[2], sizes[4]
+    out, *scratch = rest[2 * n_row :]
+    left = transposed_acts(sizes, order, bias, time_weight, rest[: 2 * n_row], *scratch)
     for t in range(9):
         out[t * C : (t + 1) * C, :] = jnp.dot(left, g[t], preferred_element_type=F32)
 
@@ -149,13 +144,14 @@
     return ((q // n_row) * 2 + (1 - core if other else core)) * n_row + lax.rem(q, n_row)
 
 
-def send_kernel(sizes, plan, group, g, *rest):
+def send_kernel(sizes, plan, group, *rest):
     if sizes:
+        order, bias, time_weight, g, *rest = rest
         n_row = sizes[2]
-        left, out, picked, terms = rest[n_row:]
-        left[...] = transposed_acts(sizes, rest[:n_row], picked)
+        left, out, *scratch, terms = rest[2 * n_row :]
+        left[...] = transposed_acts(sizes, order, bias, time_weight, rest[: 2 * n_row], *scratch)
     else:
-        left, out, terms = rest
+        g, left, out, terms = rest
     for j, d in enumerate(group):
         out[j] = packed_chunk(plan, chunk_index(d, True), left, g, terms).astype(BF16)
 
@@ -238,7 +234,14 @@
 
     feats = features.reshape(F, rW, C)
     forward = [(i, (i + 1) % n_frame) for i in range(n_frame)]
-    prior = lax.ppermute(feats, "frame", forward)
+    prior = [lax.ppermute(feats, "frame", forward)]
+    own = [feats] + [
+        lax.ppermute(feats, "row", [(i, (i + d) % n_row) for i in range(n_row)])
+        for d in range(1, n_row)
+    ]
+    for d in range(1, n_row):
+        route = [(i * n_row + k, j * n_row + (k + d) % n_row) for i, j in forward for k in range(n_row)]
+        prior.append(lax.ppermute(feats, both, route))
     (box,) = kernel_call(
         functools.partial(matrix_kernel, W), [struct((9 * W, 8 * W), BF16)], 0, [], flops=10**10
     )
@@ -269,19 +272,13 @@
         and CO == 192
     )
     packed = chunk * CO // 128
-    own, *others = kernel_call(
-        functools.partial(act_kernel, (S, rW, n_row, F, C)),
-        [struct((S, rW, C), BF16)] * n_row,
-        1,
-        [order, time_bias.reshape(-1, 128), time_weight, feats, prior],
-        [pltpu.VMEM(((F + 2) * rW, C), BF16), pltpu.VMEM((2, F, rW, C), BF16)],
-        flops=2 * F * rW * 6 * C * C,
-    )
-    acts = [own] + [
-        lax.ppermute(others[d - 1], "row", [(i, (i + d) % n_row) for i in range(n_row)])
-        for d in range(1, n_row)
+    inputs = [order, time_bias.reshape(-1, 128), time_weight, g] + own + prior
+    ext = [
+        pltpu.VMEM(((F + 2) * HR * W, C), BF16),
+        pltpu.VMEM((2, F * HR * W, C), BF16),
+        pltpu.VMEM((pixels, C), BF16),
     ]
-    picked = pltpu.VMEM((pixels, C), BF16)
+    sizes = (S, rW, n_row, F, C)
     flops = 2 * pixels * 9 * C * CO
 
     scale = 1.0 / math.sqrt(2 * F * UR * UW * n_clip * n_frame)
@@ -301,11 +298,11 @@
         for k, group in enumerate(groups):
             left_out = [] if k else [struct((C, pixels), BF16)]
             *first, send = kernel_call(
-                functools.partial(send_kernel, None if k else (S, rW, n_row), plan, group),
+                functools.partial(send_kernel, None if k else sizes, plan, group),
                 left_out + [struct((len(group), packed, 128), BF16)],
-                0,
-                [g] + ([left] if k else acts),
-                [terms] if k else [picked, terms],
+                0 if k else 1,
+                [g, left] if k else inputs,
+                [terms] if k else ext + [terms],
                 flops=flops * len(group) // n_dev,
             )
             left = left if k else first[0]
@@ -343,11 +340,11 @@
         weight_grad = flat.reshape(-1)
     else:
         (wg,) = kernel_call(
-            functools.partial(all_kernel, (S, rW, n_row)),
+            functools.partial(all_kernel, sizes),
             [struct((n_total, CO), F32)],
-            0,
-            [g] + acts,
-            [picked],
+            1,
+            inputs,
+            ext,
             flops=flops,
         )
         shard = lax.psum_scatter(wg.reshape(-1), both, scatter_dimension=0, tiled=True)

time: 48.3 us -> 43.3 us (0.90)
  local copies, waits for them, and re-layouts: 3.8 us -> 0.03 us
  starting transfers between devices: 19.1 us -> 16.7 us
  waiting for transfers between devices: 16 us -> 16.7 us
    unnamed x16 -> x12, local copies, waits for them, and re-layouts: 3.8 us -> 0.03 us
    ppermute x3, starting transfers between devices: 2.49 us -> 0.71 us  [local(): swapped = lax.ppermute(send, both, swap)]
    pallas_call x14 -> x13, Pallas kernels: 8.44 us -> 8.82 us  [kernel_call(): pl.pallas_call(body, out_shape=outs, in_specs=specs, out_specs=[VMEM] * l...]
    ppermute x2 -> x3, starting transfers between devices: 3.94 us -> 4.18 us  [the longest x1 2.12 us: local(): lax.ppermute(feats, 'row', [(i, (i + d) % n_row) for i in range(n_row)])]
    ppermute x2 -> x3, waiting for transfers between devices: 2.61 us -> 2.82 us  [the longest x1 2.47 us: local(): prior.append(lax.ppermute(feats, both, route))]
  transfers between devices with their start and end apart: 12 -> 13, of which waited for: 7 -> 8; matrix products, arithmetic and copies ran while one was open for 0% -> 0% of each run, Pallas kernels for 11% -> 12%
where the time goes in v5:
time: 43.3 us; the launch traced here: 43.1 us
  starting transfers between devices  16.7 us (39%)
  waiting for transfers between devices  16.7 us (39%)
  Pallas kernels  8.82 us (20%)
  between operations  0.79 us (2%)
    pallas_call x13, Pallas kernels, kernel_call(): pl.pallas_call(body, out_shape=outs, in_specs=specs, out_specs=[VMEM] * l...  8.82 us
    ppermute x3, waiting for transfers between devices, local(): got.append(lax.ppermute(share, both, route))  6.78 us
    ppermute x2, starting transfers between devices, local(): got = lax.ppermute(mine, 'clip', [(i, i ^ mask) for i in range(n_clip)])  6.38 us
    ppermute x1, waiting for transfers between devices, local(): later = lax.ppermute(first, 'frame', [(j, i) for i, j in forward])  3.21 us
    ppermute x2, waiting for transfers between devices, local(): got = lax.ppermute(mine, 'clip', [(i, i ^ mask) for i in range(n_clip)])  3.03 us
    ppermute x3, starting transfers between devices, local(): got.append(lax.ppermute(share, both, route))  2.77 us
    ppermute x1, waiting for transfers between devices, local(): prior.append(lax.ppermute(feats, both, route))  2.47 us
    ppermute x1, starting transfers between devices, local(): lax.ppermute(feats, 'row', [(i, (i + d) % n_row) for i in range(n_row)])  2.12 us
  transfers between devices with their start and end apart: 13, of which 8 were waited for; matrix products, arithmetic and copies ran while one was open for 0% of the time, Pallas kernels for 12%

profile of v5, /device:TPU:1, one launch (start us, length us, event | category | flops | bytes accessed | tf_op | source)
XLA Modules:
  0.0 43.1 jit_solution(1115153499783167030)
XLA Ops:
  0.6 0.0 copy-start.1
  0.6 0.0 copy-start.2
  0.6 2.1 %collective-permute-start.2 = (bf16[4,32,384]{2,1,0:T(8,128)(2,1)}, bf16[4,32,384]{2,1,0:T(8,128)(2,1)S(1)}, u32[]{:S(2)}, u32[]{:S(2)}) collective-permute-start(bf16[4,32,384]{2,1,0:T(8,128)(2,1)} %bitcast.13), channel_id=1, source_target_pairs={{0,1},{1,0},{2,3},{3,2},{4,5},{5,4},{6,7},{7,6},{8,9},{9,8},{10,11... | collective-permute-start | bytes 294920 | tf_op jit(solution)/shard_map/ppermute | solution.py:239
  2.8 2.1 %collective-permute-start.3 = (bf16[4,32,384]{2,1,0:T(8,128)(2,1)}, bf16[4,32,384]{2,1,0:T(8,128)(2,1)S(1)}, u32[]{:S(2)}, u32[]{:S(2)}) collective-permute-start(bf16[4,32,384]{2,1,0:T(8,128)(2,1)} %bitcast.14), channel_id=1, source_target_pairs={{0,2},{2,4},{4,6},{6,0},{1,3},{3,5},{5,7},{7,1},{8,10},{10,12},{12... | collective-permute-start | bytes 294920 | tf_op jit(solution)/shard_map/ppermute | solution.py:237
  4.8 0.0 collective-permute-start.4
  4.9 0.0 copy-start
  4.9 0.0 copy-start.3
  4.9 0.0 copy-start.4
  4.9 0.0 copy-start.5
  4.9 0.0 copy-done.1
  4.9 0.0 copy-done.2
  4.9 1.5 %shard_map.78 = (bf16[9,256,192]{2,1,0:T(8,128)(2,1)S(1)}, bf16[4,32,384]{2,1,0:T(8,128)(2,1)S(1)}, bf16[4,32,384]{2,1,0:T(8,128)(2,1)S(1)}) custom-call(bf16[4,256,192]{2,1,0:T(8,128)(2,1)S(1)} %bitcast.12, bf16[9,192,384]{2,1,0:T(8,128)(2,1)S(1)} %bitcast.11, bf16[288,256]{1,0:T(8,128)(2,1)S(1)} %shard_map.77.box), custom_call_target="tpu_custom_call" | custom-call | flops 339738624 | bytes 2949120 | tf_op jit(solution)/shard_map/pallas_call | solution.py:27
  6.4 0.0 collective-permute-done.2.rest_5_
  6.4 0.3 collective-permute-done.3.rest_6_
  6.8 2.5 %collective-permute-done.4.rest_7_ = bf16[4,32,384]{2,1,0:T(8,128)(2,1)S(1)} collective-permute-done((bf16[4,32,384]{2,1,0:T(8,128)(2,1)}, bf16[4,32,384]{2,1,0:T(8,128)(2,1)S(1)}, u32[]{:S(2)}, u32[]{:S(2)}) %collective-permute-start.4) | collective-permute-done | bytes 98336 | tf_op jit(solution)/shard_map/ppermute | solution.py:244
  9.2 0.0 copy-done
  9.2 0.0 copy-done.3
  9.3 0.0 copy-done.4
  9.3 1.8 %shard_map.81 = (bf16[384,256]{1,0:T(8,128)(2,1)S(1)}, bf16[1,648,128]{2,1,0:T(8,128)(2,1)S(1)}) custom-call(s32[8]{0:T(128)S(1)} %bitcast.18, f32[6,128]{1,0:T(8,128)S(1)} %bitcast.17, bf16[3,384,768]{2,1,0:T(8,128)(2,1)S(1)} %copy-done, bf16[9,256,192]{2,1,0:T(8,128)(2,1)S(1)} %get-tuple-element.15.rest_3_.rest_0_.g, bf16[4,32,384]{2,1,0:T(8,128)(2,1)S(1)} %bitcast.16, ...), custom_call_target="tpu_custom_call" | custom-call | flops 42467328 | bytes 3413024 | tf_op jit(solution)/shard_map/pallas_call | solution.py:27
  11.1 0.7 %shard_map.85 = bf16[2,648,128]{2,1,0:T(8,128)(2,1)S(1)} custom-call(bf16[9,256,192]{2,1,0:T(8,128)(2,1)S(1)} %get-tuple-element.15.rest_3_.rest_0_.g, bf16[384,256]{1,0:T(8,128)(2,1)S(1)} %get-tuple-element.16.rest_1_.left), custom_call_target="tpu_custom_call" | custom-call | flops 84934656 | bytes 1413120 | tf_op jit(solution)/shard_map/pallas_call | solution.py:27
  11.8 0.1 collective-permute-start.8
  11.9 0.5 %collective-permute-start.6 = (bf16[1,648,128]{2,1,0:T(8,128)(2,1)S(1)}, bf16[1,648,128]{2,1,0:T(8,128)(2,1)S(1)}, u32[]{:S(2)}, u32[]{:S(2)}) collective-permute-start(bf16[1,648,128]{2,1,0:T(8,128)(2,1)S(1)} %get-tuple-element.17), channel_id=1, source_target_pairs={{0,2},{1,3},{2,0},{3,1},{4,6},{5,7},{6,4},{7,5},{8,10},{9,11},{10,... | collective-permute-start | bytes 497672 | tf_op jit(solution)/shard_map/ppermute | solution.py:309
  12.4 0.3 shard_map.82
  12.7 0.1 collective-permute-start.5
  12.9 0.9 %collective-permute-done.6.got = bf16[1,648,128]{2,1,0:T(8,128)(2,1)S(1)} collective-permute-done((bf16[1,648,128]{2,1,0:T(8,128)(2,1)S(1)}, bf16[1,648,128]{2,1,0:T(8,128)(2,1)S(1)}, u32[]{:S(2)}, u32[]{:S(2)}) %collective-permute-start.6) | collective-permute-done | bytes 165920 | tf_op jit(solution)/shard_map/ppermute | solution.py:309
  13.7 0.3 shard_map.84
  14.1 1.7 %collective-permute-start.7 = (bf16[648,128]{1,0:T(8,128)(2,1)S(1)}, bf16[648,128]{1,0:T(8,128)(2,1)S(1)}, u32[]{:S(2)}, u32[]{:S(2)}) collective-permute-start(bf16[648,128]{1,0:T(8,128)(2,1)S(1)} %shard_map.84), channel_id=1, source_target_pairs={{0,5},{1,4},{2,7},{3,6},{4,1},{5,0},{6,3},{7,2},{8,13},{9,12},{10,... | collective-permute-start | bytes 497672 | tf_op jit(solution)/shard_map/ppermute | solution.py:321
  15.8 0.0 collective-permute-done.8.got
  15.8 0.7 %shard_map.86 = (bf16[648,128]{1,0:T(8,128)(2,1)S(1)}, bf16[648,128]{1,0:T(8,128)(2,1)S(1)}) custom-call(bf16[9,256,192]{2,1,0:T(8,128)(2,1)S(1)} %get-tuple-element.15.rest_3_.rest_0_.g, bf16[384,256]{1,0:T(8,128)(2,1)S(1)} %get-tuple-element.16.rest_1_.left, bf16[2,648,128]{2,1,0:T(8,128)(2,1)S(1)} %collective-permute-done.8.got), custom_call_target="tpu_custom_call" | custom-call | flops 84934656 | bytes 1744896 | tf_op jit(solution)/shard_map/pallas_call | solution.py:27
  16.5 0.7 %collective-permute-start.10 = (bf16[648,128]{1,0:T(8,128)(2,1)S(1)}, bf16[648,128]{1,0:T(8,128)(2,1)S(1)}, u32[]{:S(2)}, u32[]{:S(2)}) collective-permute-start(bf16[648,128]{1,0:T(8,128)(2,1)S(1)} %get-tuple-element.19), channel_id=1, source_target_pairs={{0,4},{1,5},{2,6},{3,7},{4,0},{5,1},{6,2},{7,3},{8,12},{9,13},{10,... | collective-permute-start | bytes 497672 | tf_op jit(solution)/shard_map/ppermute | solution.py:321
  17.2 0.4 collective-permute-start.9
  17.6 0.0 collective-permute-done.5.got
  17.6 0.4 shard_map.83.keep
  17.9 2.8 %collective-permute-done.7.rest_0_ = bf16[648,128]{1,0:T(8,128)(2,1)S(1)} collective-permute-done((bf16[648,128]{1,0:T(8,128)(2,1)S(1)}, bf16[648,128]{1,0:T(8,128)(2,1)S(1)}, u32[]{:S(2)}, u32[]{:S(2)}) %collective-permute-start.7) | collective-permute-done | bytes 165920 | tf_op jit(solution)/shard_map/ppermute | solution.py:321
  20.7 3.5 %collective-permute-done.10.rest_2_ = bf16[648,128]{1,0:T(8,128)(2,1)S(1)} collective-permute-done((bf16[648,128]{1,0:T(8,128)(2,1)S(1)}, bf16[648,128]{1,0:T(8,128)(2,1)S(1)}, u32[]{:S(2)}, u32[]{:S(2)}) %collective-permute-start.10) | collective-permute-done | bytes 165920 | tf_op jit(solution)/shard_map/ppermute | solution.py:321
  24.2 0.5 %collective-permute-done.9.rest_1_ = bf16[648,128]{1,0:T(8,128)(2,1)S(1)} collective-permute-done((bf16[648,128]{1,0:T(8,128)(2,1)S(1)}, bf16[648,128]{1,0:T(8,128)(2,1)S(1)}, u32[]{:S(2)}, u32[]{:S(2)}) %collective-permute-start.9) | collective-permute-done | bytes 165920 | tf_op jit(solution)/shard_map/ppermute | solution.py:321
  24.7 0.1 shard_map.87.mine
  24.8 3.5 %collective-permute-start.11 = (bf16[648,128]{1,0:T(8,128)(2,1)S(1)}, bf16[648,128]{1,0:T(8,128)(2,1)S(1)}, u32[]{:S(2)}, u32[]{:S(2)}) collective-permute-start(bf16[648,128]{1,0:T(8,128)(2,1)S(1)} %shard_map.87.mine), channel_id=1, source_target_pairs={{0,24},{8,16},{16,8},{24,0},{1,25},{9,17},{17,9},{25,1},{2,26},{10... | collective-permute-start | bytes 497672 | tf_op jit(solution)/shard_map/ppermute | solution.py:329
  28.3 1.0 %collective-permute-start = (bf16[4,32,384]{2,1,0:T(8,128)(2,1)S(1)}, bf16[4,32,384]{2,1,0:T(8,128)(2,1)S(1)}, u32[]{:S(2)}, u32[]{:S(2)}) collective-permute-start(bf16[4,32,384]{2,1,0:T(8,128)(2,1)S(1)} %get-tuple-element.12), channel_id=1, source_target_pairs={{0,1},{1,0},{2,3},{3,2},{4,5},{5,4},{6,7},{7,6},{8,9},{9,8},{10,11... | collective-permute-start | bytes 294920 | tf_op jit(solution)/shard_map/ppermute | solution.py:354
  29.3 3.0 %collective-permute-done.11.got = bf16[648,128]{1,0:T(8,128)(2,1)S(1)} collective-permute-done((bf16[648,128]{1,0:T(8,128)(2,1)S(1)}, bf16[648,128]{1,0:T(8,128)(2,1)S(1)}, u32[]{:S(2)}, u32[]{:S(2)}) %collective-permute-start.11) | collective-permute-done | bytes 165920 | tf_op jit(solution)/shard_map/ppermute | solution.py:329
  32.4 2.9 %collective-permute-start.12 = (bf16[648,128]{1,0:T(8,128)(2,1)S(1)}, bf16[648,128]{1,0:T(8,128)(2,1)S(1)}, u32[]{:S(2)}, u32[]{:S(2)}) collective-permute-start(bf16[648,128]{1,0:T(8,128)(2,1)S(1)} %shard_map.88.mine), channel_id=1, source_target_pairs={{0,8},{8,0},{16,24},{24,16},{1,9},{9,1},{17,25},{25,17},{2,10},{10... | collective-permute-start | bytes 497672 | tf_op jit(solution)/shard_map/ppermute | solution.py:329
  35.3 0.0 collective-permute-done.rest_1_
  35.3 0.6 %shard_map.79 = (bf16[2,128,384]{2,1,0:T(8,128)(2,1)S(1)}, bf16[2,64,384]{2,1,0:T(8,128)(2,1)S(1)}) custom-call(s32[8]{0:T(128)S(1)} %bitcast.19, bf16[4,32,384]{2,1,0:T(8,128)(2,1)S(1)} %get-tuple-element.11.rest_0_, bf16[4,32,384]{2,1,0:T(8,128)(2,1)S(1)} %collective-permute-done.rest_1_), custom_call_target="tpu_custom_call" | custom-call | bytes 491552 | tf_op jit(solution)/shard_map/pallas_call | solution.py:27
  35.9 1.7 %collective-permute-start.1 = (bf16[2,64,384]{2,1,0:T(8,128)(2,1)S(1)}, bf16[2,64,384]{2,1,0:T(8,128)(2,1)S(1)}, u32[]{:S(2)}, u32[]{:S(2)}) collective-permute-start(bf16[2,64,384]{2,1,0:T(8,128)(2,1)S(1)} %get-tuple-element.14), channel_id=1, source_target_pairs={{2,0},{4,2},{6,4},{0,6},{3,1},{5,3},{7,5},{1,7},{10,8},{12,10},{14... | collective-permute-start | bytes 294920 | tf_op jit(solution)/shard_map/ppermute | solution.py:363
  37.6 3.2 %collective-permute-done.1.later = bf16[2,64,384]{2,1,0:T(8,128)(2,1)S(1)} collective-permute-done((bf16[2,64,384]{2,1,0:T(8,128)(2,1)S(1)}, bf16[2,64,384]{2,1,0:T(8,128)(2,1)S(1)}, u32[]{:S(2)}, u32[]{:S(2)}) %collective-permute-start.1) | collective-permute-done | bytes 98336 | tf_op jit(solution)/shard_map/ppermute | solution.py:363
  40.8 1.4 %shard_map.80 = bf16[128,384]{1,0:T(8,128)(2,1)} custom-call(bf16[2,128,384]{2,1,0:T(8,128)(2,1)S(1)} %get-tuple-element.13.natural, bf16[2,64,384]{2,1,0:T(8,128)(2,1)S(1)} %collective-permute-done.1.later, bf16[3,384,768]{2,1,0:T(8,128)(2,1)S(1)} %copy-done), custom_call_target="tpu_custom_call" | custom-call | flops 226492416 | bytes 2162688 | tf_op jit(solution)/shard_map/pallas_call | solution.py:27
  42.2 0.0 collective-permute-done.12.got
  42.2 0.9 %shard_map.89 = f32[648,128]{1,0:T(8,128)} custom-call(bf16[648,128]{1,0:T(8,128)(2,1)S(1)} %shard_map.88.mine, bf16[648,128]{1,0:T(8,128)(2,1)S(1)} %collective-permute-done.12.got), custom_call_target="tpu_custom_call" | custom-call | bytes 663552 | tf_op jit(solution)/shard_map/pallas_call | solution.py:27
  (3 shorter events, 0.1 us)
Async XLA Ops:
  0.6 4.3 %copy-start.1 = (bf16[3,3,384,192]{2,3,1,0:T(8,128)(2,1)S(1)}, bf16[3,3,384,192]{2,3,1,0:T(8,128)(2,1)}, u32[]{:S(2)}) copy-start(bf16[3,3,384,192]{2,3,1,0:T(8,128)(2,1)} %param.9) | copy-start | bytes 3981316
  0.6 4.3 %copy-start.2 = (bf16[1,4,4,64,192]{4,3,2,1,0:T(8,128)(2,1)S(1)}, bf16[1,4,4,64,192]{4,3,2,1,0:T(8,128)(2,1)}, u32[]{:S(2)}) copy-start(bf16[1,4,4,64,192]{4,3,2,1,0:T(8,128)(2,1)} %param.10) | copy-start | bytes 1179652
  0.6 5.8 %collective-permute-start.2 = (bf16[4,32,384]{2,1,0:T(8,128)(2,1)}, bf16[4,32,384]{2,1,0:T(8,128)(2,1)S(1)}, u32[]{:S(2)}, u32[]{:S(2)}) collective-permute-start(bf16[4,32,384]{2,1,0:T(8,128)(2,1)} %bitcast.13), channel_id=1, source_target_pairs={{0,1},{1,0},{2,3},{3,2},{4,5},{5,4},{6,7},{7,6},{8,9},{9,8},{10,11... | collective-permute-start | bytes 294920 | tf_op jit(solution)/shard_map/ppermute | solution.py:239
  2.8 4.0 %collective-permute-start.3 = (bf16[4,32,384]{2,1,0:T(8,128)(2,1)}, bf16[4,32,384]{2,1,0:T(8,128)(2,1)S(1)}, u32[]{:S(2)}, u32[]{:S(2)}) collective-permute-start(bf16[4,32,384]{2,1,0:T(8,128)(2,1)} %bitcast.14), channel_id=1, source_target_pairs={{0,2},{2,4},{4,6},{6,0},{1,3},{3,5},{5,7},{7,1},{8,10},{10,12},{12... | collective-permute-start | bytes 294920 | tf_op jit(solution)/shard_map/ppermute | solution.py:237
  4.8 4.4 %collective-permute-start.4 = (bf16[4,32,384]{2,1,0:T(8,128)(2,1)}, bf16[4,32,384]{2,1,0:T(8,128)(2,1)S(1)}, u32[]{:S(2)}, u32[]{:S(2)}) collective-permute-start(bf16[4,32,384]{2,1,0:T(8,128)(2,1)} %bitcast.15), channel_id=1, source_target_pairs={{0,3},{1,2},{2,5},{3,4},{4,7},{5,6},{6,1},{7,0},{8,11},{9,10},{10,... | collective-permute-start | bytes 294920 | tf_op jit(solution)/shard_map/ppermute | solution.py:244
  4.9 4.4 %copy-start = (bf16[3,384,768]{2,1,0:T(8,128)(2,1)S(1)}, bf16[3,384,768]{2,1,0:T(8,128)(2,1)}, u32[]{:S(2)}) copy-start(bf16[3,384,768]{2,1,0:T(8,128)(2,1)} %rest_2_.1) | copy-start | bytes 5308420
  4.9 4.4 %copy-start.3 = (bf16[1,4,1,32,384]{4,3,2,1,0:T(8,128)(2,1)S(1)}, bf16[1,4,1,32,384]{4,3,2,1,0:T(8,128)(2,1)}, u32[]{:S(2)}) copy-start(bf16[1,4,1,32,384]{4,3,2,1,0:T(8,128)(2,1)} %param.6) | copy-start | bytes 294916
  4.9 4.4 %copy-start.4 = (f32[768]{0:T(1024)S(1)}, f32[768]{0:T(1024)}, u32[]{:S(2)}) copy-start(f32[768]{0:T(1024)} %param.8) | copy-start | bytes 9220
  4.9 4.4 %copy-start.5 = (s32[1,1,8]{2,1,0:T(1,128)S(1)}, s32[1,1,8]{2,1,0:T(1,128)}, u32[]{:S(2)}) copy-start(s32[1,1,8]{2,1,0:T(1,128)} %param.11) | copy-start | bytes 100
  11.8 4.0 %collective-permute-start.8 = (bf16[2,648,128]{2,1,0:T(8,128)(2,1)S(1)}, bf16[2,648,128]{2,1,0:T(8,128)(2,1)S(1)}, u32[]{:S(2)}, u32[]{:S(2)}) collective-permute-start(bf16[2,648,128]{2,1,0:T(8,128)(2,1)S(1)} %shard_map.85), channel_id=1, source_target_pairs={{0,2},{1,3},{2,0},{3,1},{4,6},{5,7},{6,4},{7,5},{8,10},{9,11},{10,... | collective-permute-start | bytes 995336 | tf_op jit(solution)/shard_map/ppermute | solution.py:309
  11.9 1.9 %collective-permute-start.6 = (bf16[1,648,128]{2,1,0:T(8,128)(2,1)S(1)}, bf16[1,648,128]{2,1,0:T(8,128)(2,1)S(1)}, u32[]{:S(2)}, u32[]{:S(2)}) collective-permute-start(bf16[1,648,128]{2,1,0:T(8,128)(2,1)S(1)} %get-tuple-element.17), channel_id=1, source_target_pairs={{0,2},{1,3},{2,0},{3,1},{4,6},{5,7},{6,4},{7,5},{8,10},{9,11},{10,... | collective-permute-start | bytes 497672 | tf_op jit(solution)/shard_map/ppermute | solution.py:309
  12.7 4.8 %collective-permute-start.5 = (bf16[1,648,128]{2,1,0:T(8,128)(2,1)S(1)}, bf16[1,648,128]{2,1,0:T(8,128)(2,1)S(1)}, u32[]{:S(2)}, u32[]{:S(2)}) collective-permute-start(bf16[1,648,128]{2,1,0:T(8,128)(2,1)S(1)} %shard_map.82), channel_id=1, source_target_pairs={{0,2},{1,3},{2,0},{3,1},{4,6},{5,7},{6,4},{7,5},{8,10},{9,11},{10,... | collective-permute-start | bytes 497672 | tf_op jit(solution)/shard_map/ppermute | solution.py:309
  14.1 6.6 %collective-permute-start.7 = (bf16[648,128]{1,0:T(8,128)(2,1)S(1)}, bf16[648,128]{1,0:T(8,128)(2,1)S(1)}, u32[]{:S(2)}, u32[]{:S(2)}) collective-permute-start(bf16[648,128]{1,0:T(8,128)(2,1)S(1)} %shard_map.84), channel_id=1, source_target_pairs={{0,5},{1,4},{2,7},{3,6},{4,1},{5,0},{6,3},{7,2},{8,13},{9,12},{10,... | collective-permute-start | bytes 497672 | tf_op jit(solution)/shard_map/ppermute | solution.py:321
  16.5 7.7 %collective-permute-start.10 = (bf16[648,128]{1,0:T(8,128)(2,1)S(1)}, bf16[648,128]{1,0:T(8,128)(2,1)S(1)}, u32[]{:S(2)}, u32[]{:S(2)}) collective-permute-start(bf16[648,128]{1,0:T(8,128)(2,1)S(1)} %get-tuple-element.19), channel_id=1, source_target_pairs={{0,4},{1,5},{2,6},{3,7},{4,0},{5,1},{6,2},{7,3},{8,12},{9,13},{10,... | collective-permute-start | bytes 497672 | tf_op jit(solution)/shard_map/ppermute | solution.py:321
  17.2 7.5 %collective-permute-start.9 = (bf16[648,128]{1,0:T(8,128)(2,1)S(1)}, bf16[648,128]{1,0:T(8,128)(2,1)S(1)}, u32[]{:S(2)}, u32[]{:S(2)}) collective-permute-start(bf16[648,128]{1,0:T(8,128)(2,1)S(1)} %get-tuple-element.18), channel_id=1, source_target_pairs={{0,1},{1,0},{2,3},{3,2},{4,5},{5,4},{6,7},{7,6},{8,9},{9,8},{10,11... | collective-permute-start | bytes 497672 | tf_op jit(solution)/shard_map/ppermute | solution.py:321
  24.8 7.6 %collective-permute-start.11 = (bf16[648,128]{1,0:T(8,128)(2,1)S(1)}, bf16[648,128]{1,0:T(8,128)(2,1)S(1)}, u32[]{:S(2)}, u32[]{:S(2)}) collective-permute-start(bf16[648,128]{1,0:T(8,128)(2,1)S(1)} %shard_map.87.mine), channel_id=1, source_target_pairs={{0,24},{8,16},{16,8},{24,0},{1,25},{9,17},{17,9},{25,1},{2,26},{10... | collective-permute-start | bytes 497672 | tf_op jit(solution)/shard_map/ppermute | solution.py:329
  28.3 6.9 %collective-permute-start = (bf16[4,32,384]{2,1,0:T(8,128)(2,1)S(1)}, bf16[4,32,384]{2,1,0:T(8,128)(2,1)S(1)}, u32[]{:S(2)}, u32[]{:S(2)}) collective-permute-start(bf16[4,32,384]{2,1,0:T(8,128)(2,1)S(1)} %get-tuple-element.12), channel_id=1, source_target_pairs={{0,1},{1,0},{2,3},{3,2},{4,5},{5,4},{6,7},{7,6},{8,9},{9,8},{10,11... | collective-permute-start | bytes 294920 | tf_op jit(solution)/shard_map/ppermute | solution.py:354
  32.4 9.8 %collective-permute-start.12 = (bf16[648,128]{1,0:T(8,128)(2,1)S(1)}, bf16[648,128]{1,0:T(8,128)(2,1)S(1)}, u32[]{:S(2)}, u32[]{:S(2)}) collective-permute-start(bf16[648,128]{1,0:T(8,128)(2,1)S(1)} %shard_map.88.mine), channel_id=1, source_target_pairs={{0,8},{8,0},{16,24},{24,16},{1,9},{9,1},{17,25},{25,17},{2,10},{10... | collective-permute-start | bytes 497672 | tf_op jit(solution)/shard_map/ppermute | solution.py:329
  35.9 4.9 %collective-permute-start.1 = (bf16[2,64,384]{2,1,0:T(8,128)(2,1)S(1)}, bf16[2,64,384]{2,1,0:T(8,128)(2,1)S(1)}, u32[]{:S(2)}, u32[]{:S(2)}) collective-permute-start(bf16[2,64,384]{2,1,0:T(8,128)(2,1)S(1)} %get-tuple-element.14), channel_id=1, source_target_pairs={{2,0},{4,2},{6,4},{0,6},{3,1},{5,3},{7,5},{1,7},{10,8},{12,10},{14... | collective-permute-start | bytes 294920 | tf_op jit(solution)/shard_map/ppermute | solution.py:363

commit v6 on v5

--- a/solution.py
+++ b/solution.py
@@ -324,12 +324,11 @@
         (mine,) = kernel_call(
             functools.partial(square_kernel, scale), [struct((packed, 128), BF16)], 0, [mine] + got
         )
-        mask = n_clip - 1
-        while mask:
+        masks = [(1 << k) - 1 for k in range(1, n_clip.bit_length())]
+        for mask in masks:
             got = lax.ppermute(mine, "clip", [(i, i ^ mask) for i in range(n_clip)])
-            if mask > 1:
+            if mask != masks[-1]:
                 (mine,) = kernel_call(pair_kernel, [struct((packed, 128), BF16)], 0, [mine, got])
-            mask //= 2
         (flat,) = kernel_call(
             functools.partial(final_kernel, chunk, CO),
             [struct((packed, 128), F32)],

time: 43.3 us -> 41.7 us (0.963)
  starting transfers between devices: 16.7 us -> 15.5 us
    ppermute x2, starting transfers between devices: 6.38 us -> 5.08 us  [local(): got = lax.ppermute(mine, 'clip', [(i, i ^ mask) for i in range(n_clip)])]
  transfers between devices with their start and end apart: 13 -> 13, of which waited for: 8 -> 8; matrix products, arithmetic and copies ran while one was open for 0% -> 0% of each run, Pallas kernels for 12% -> 13%
where the time goes in v6:
time: 41.7 us; the launch traced here: 41.6 us
  waiting for transfers between devices  16.5 us (40%)
  starting transfers between devices  15.5 us (37%)
  Pallas kernels  8.82 us (21%)
  between operations  0.79 us (2%)
    pallas_call x13, Pallas kernels, kernel_call(): pl.pallas_call(body, out_shape=outs, in_specs=specs, out_specs=[VMEM] * l...  8.82 us
    ppermute x3, waiting for transfers between devices, local(): got.append(lax.ppermute(share, both, route))  6.78 us
    ppermute x2, starting transfers between devices, local(): got = lax.ppermute(mine, 'clip', [(i, i ^ mask) for i in range(n_clip)])  5.08 us
    ppermute x1, waiting for transfers between devices, local(): later = lax.ppermute(first, 'frame', [(j, i) for i, j in forward])  3.21 us
    ppermute x2, waiting for transfers between devices, local(): got = lax.ppermute(mine, 'clip', [(i, i ^ mask) for i in range(n_clip)])  2.78 us
    ppermute x3, starting transfers between devices, local(): got.append(lax.ppermute(share, both, route))  2.77 us
    ppermute x1, waiting for transfers between devices, local(): prior.append(lax.ppermute(feats, both, route))  2.47 us
    ppermute x1, starting transfers between devices, local(): lax.ppermute(feats, 'row', [(i, (i + d) % n_row) for i in range(n_row)])  2.12 us
  transfers between devices with their start and end apart: 13, of which 8 were waited for; matrix products, arithmetic and copies ran while one was open for 0% of the time, Pallas kernels for 13%

profile of v6, /device:TPU:1, one launch (start us, length us, event | category | flops | bytes accessed | tf_op | source)
XLA Modules:
  0.0 41.6 jit_solution(7513204863540975311)
XLA Ops:
  0.6 0.0 copy-start.1
  0.6 0.0 copy-start.2
  0.6 2.1 %collective-permute-start.2 = (bf16[4,32,384]{2,1,0:T(8,128)(2,1)}, bf16[4,32,384]{2,1,0:T(8,128)(2,1)S(1)}, u32[]{:S(2)}, u32[]{:S(2)}) collective-permute-start(bf16[4,32,384]{2,1,0:T(8,128)(2,1)} %bitcast.13), channel_id=1, source_target_pairs={{0,1},{1,0},{2,3},{3,2},{4,5},{5,4},{6,7},{7,6},{8,9},{9,8},{10,11... | collective-permute-start | bytes 294920 | tf_op jit(solution)/shard_map/ppermute | solution.py:239
  2.8 2.1 %collective-permute-start.3 = (bf16[4,32,384]{2,1,0:T(8,128)(2,1)}, bf16[4,32,384]{2,1,0:T(8,128)(2,1)S(1)}, u32[]{:S(2)}, u32[]{:S(2)}) collective-permute-start(bf16[4,32,384]{2,1,0:T(8,128)(2,1)} %bitcast.14), channel_id=1, source_target_pairs={{0,2},{2,4},{4,6},{6,0},{1,3},{3,5},{5,7},{7,1},{8,10},{10,12},{12... | collective-permute-start | bytes 294920 | tf_op jit(solution)/shard_map/ppermute | solution.py:237
  4.8 0.0 collective-permute-start.4
  4.9 0.0 copy-start
  4.9 0.0 copy-start.3
  4.9 0.0 copy-start.4
  4.9 0.0 copy-start.5
  4.9 0.0 copy-done.1
  4.9 0.0 copy-done.2
  4.9 1.5 %shard_map.78 = (bf16[9,256,192]{2,1,0:T(8,128)(2,1)S(1)}, bf16[4,32,384]{2,1,0:T(8,128)(2,1)S(1)}, bf16[4,32,384]{2,1,0:T(8,128)(2,1)S(1)}) custom-call(bf16[4,256,192]{2,1,0:T(8,128)(2,1)S(1)} %bitcast.12, bf16[9,192,384]{2,1,0:T(8,128)(2,1)S(1)} %bitcast.11, bf16[288,256]{1,0:T(8,128)(2,1)S(1)} %shard_map.77.box), custom_call_target="tpu_custom_call" | custom-call | flops 339738624 | bytes 2949120 | tf_op jit(solution)/shard_map/pallas_call | solution.py:27
  6.4 0.0 collective-permute-done.2.rest_5_
  6.4 0.3 collective-permute-done.3.rest_6_
  6.8 2.5 %collective-permute-done.4.rest_7_ = bf16[4,32,384]{2,1,0:T(8,128)(2,1)S(1)} collective-permute-done((bf16[4,32,384]{2,1,0:T(8,128)(2,1)}, bf16[4,32,384]{2,1,0:T(8,128)(2,1)S(1)}, u32[]{:S(2)}, u32[]{:S(2)}) %collective-permute-start.4) | collective-permute-done | bytes 98336 | tf_op jit(solution)/shard_map/ppermute | solution.py:244
  9.2 0.0 copy-done
  9.2 0.0 copy-done.3
  9.3 0.0 copy-done.4
  9.3 1.8 %shard_map.81 = (bf16[384,256]{1,0:T(8,128)(2,1)S(1)}, bf16[1,648,128]{2,1,0:T(8,128)(2,1)S(1)}) custom-call(s32[8]{0:T(128)S(1)} %bitcast.18, f32[6,128]{1,0:T(8,128)S(1)} %bitcast.17, bf16[3,384,768]{2,1,0:T(8,128)(2,1)S(1)} %copy-done, bf16[9,256,192]{2,1,0:T(8,128)(2,1)S(1)} %get-tuple-element.15.rest_3_.rest_0_.g, bf16[4,32,384]{2,1,0:T(8,128)(2,1)S(1)} %bitcast.16, ...), custom_call_target="tpu_custom_call" | custom-call | flops 42467328 | bytes 3413024 | tf_op jit(solution)/shard_map/pallas_call | solution.py:27
  11.1 0.7 %shard_map.85 = bf16[2,648,128]{2,1,0:T(8,128)(2,1)S(1)} custom-call(bf16[9,256,192]{2,1,0:T(8,128)(2,1)S(1)} %get-tuple-element.15.rest_3_.rest_0_.g, bf16[384,256]{1,0:T(8,128)(2,1)S(1)} %get-tuple-element.16.rest_1_.left), custom_call_target="tpu_custom_call" | custom-call | flops 84934656 | bytes 1413120 | tf_op jit(solution)/shard_map/pallas_call | solution.py:27
  11.8 0.1 collective-permute-start.8
  11.9 0.5 %collective-permute-start.6 = (bf16[1,648,128]{2,1,0:T(8,128)(2,1)S(1)}, bf16[1,648,128]{2,1,0:T(8,128)(2,1)S(1)}, u32[]{:S(2)}, u32[]{:S(2)}) collective-permute-start(bf16[1,648,128]{2,1,0:T(8,128)(2,1)S(1)} %get-tuple-element.17), channel_id=1, source_target_pairs={{0,2},{1,3},{2,0},{3,1},{4,6},{5,7},{6,4},{7,5},{8,10},{9,11},{10,... | collective-permute-start | bytes 497672 | tf_op jit(solution)/shard_map/ppermute | solution.py:309
  12.4 0.3 shard_map.82
  12.7 0.1 collective-permute-start.5
  12.9 0.9 %collective-permute-done.6.got = bf16[1,648,128]{2,1,0:T(8,128)(2,1)S(1)} collective-permute-done((bf16[1,648,128]{2,1,0:T(8,128)(2,1)S(1)}, bf16[1,648,128]{2,1,0:T(8,128)(2,1)S(1)}, u32[]{:S(2)}, u32[]{:S(2)}) %collective-permute-start.6) | collective-permute-done | bytes 165920 | tf_op jit(solution)/shard_map/ppermute | solution.py:309
  13.7 0.3 shard_map.84
  14.1 1.7 %collective-permute-start.7 = (bf16[648,128]{1,0:T(8,128)(2,1)S(1)}, bf16[648,128]{1,0:T(8,128)(2,1)S(1)}, u32[]{:S(2)}, u32[]{:S(2)}) collective-permute-start(bf16[648,128]{1,0:T(8,128)(2,1)S(1)} %shard_map.84), channel_id=1, source_target_pairs={{0,5},{1,4},{2,7},{3,6},{4,1},{5,0},{6,3},{7,2},{8,13},{9,12},{10,... | collective-permute-start | bytes 497672 | tf_op jit(solution)/shard_map/ppermute | solution.py:321
  15.8 0.0 collective-permute-done.8.got
  15.8 0.7 %shard_map.86 = (bf16[648,128]{1,0:T(8,128)(2,1)S(1)}, bf16[648,128]{1,0:T(8,128)(2,1)S(1)}) custom-call(bf16[9,256,192]{2,1,0:T(8,128)(2,1)S(1)} %get-tuple-element.15.rest_3_.rest_0_.g, bf16[384,256]{1,0:T(8,128)(2,1)S(1)} %get-tuple-element.16.rest_1_.left, bf16[2,648,128]{2,1,0:T(8,128)(2,1)S(1)} %collective-permute-done.8.got), custom_call_target="tpu_custom_call" | custom-call | flops 84934656 | bytes 1744896 | tf_op jit(solution)/shard_map/pallas_call | solution.py:27
  16.5 0.7 %collective-permute-start.10 = (bf16[648,128]{1,0:T(8,128)(2,1)S(1)}, bf16[648,128]{1,0:T(8,128)(2,1)S(1)}, u32[]{:S(2)}, u32[]{:S(2)}) collective-permute-start(bf16[648,128]{1,0:T(8,128)(2,1)S(1)} %get-tuple-element.19), channel_id=1, source_target_pairs={{0,4},{1,5},{2,6},{3,7},{4,0},{5,1},{6,2},{7,3},{8,12},{9,13},{10,... | collective-permute-start | bytes 497672 | tf_op jit(solution)/shard_map/ppermute | solution.py:321
  17.2 0.4 collective-permute-start.9
  17.6 0.0 collective-permute-done.5.got
  17.6 0.4 shard_map.83.keep
  17.9 2.8 %collective-permute-done.7.rest_0_ = bf16[648,128]{1,0:T(8,128)(2,1)S(1)} collective-permute-done((bf16[648,128]{1,0:T(8,128)(2,1)S(1)}, bf16[648,128]{1,0:T(8,128)(2,1)S(1)}, u32[]{:S(2)}, u32[]{:S(2)}) %collective-permute-start.7) | collective-permute-done | bytes 165920 | tf_op jit(solution)/shard_map/ppermute | solution.py:321
  20.7 3.5 %collective-permute-done.10.rest_2_ = bf16[648,128]{1,0:T(8,128)(2,1)S(1)} collective-permute-done((bf16[648,128]{1,0:T(8,128)(2,1)S(1)}, bf16[648,128]{1,0:T(8,128)(2,1)S(1)}, u32[]{:S(2)}, u32[]{:S(2)}) %collective-permute-start.10) | collective-permute-done | bytes 165920 | tf_op jit(solution)/shard_map/ppermute | solution.py:321
  24.2 0.5 %collective-permute-done.9.rest_1_ = bf16[648,128]{1,0:T(8,128)(2,1)S(1)} collective-permute-done((bf16[648,128]{1,0:T(8,128)(2,1)S(1)}, bf16[648,128]{1,0:T(8,128)(2,1)S(1)}, u32[]{:S(2)}, u32[]{:S(2)}) %collective-permute-start.9) | collective-permute-done | bytes 165920 | tf_op jit(solution)/shard_map/ppermute | solution.py:321
  24.7 0.1 shard_map.87.mine
  24.8 1.5 %collective-permute-start.11 = (bf16[648,128]{1,0:T(8,128)(2,1)S(1)}, bf16[648,128]{1,0:T(8,128)(2,1)S(1)}, u32[]{:S(2)}, u32[]{:S(2)}) collective-permute-start(bf16[648,128]{1,0:T(8,128)(2,1)S(1)} %shard_map.87.mine), channel_id=1, source_target_pairs={{0,8},{8,0},{16,24},{24,16},{1,9},{9,1},{17,25},{25,17},{2,10},{10... | collective-permute-start | bytes 497672 | tf_op jit(solution)/shard_map/ppermute | solution.py:329
  26.3 1.0 %collective-permute-start = (bf16[4,32,384]{2,1,0:T(8,128)(2,1)S(1)}, bf16[4,32,384]{2,1,0:T(8,128)(2,1)S(1)}, u32[]{:S(2)}, u32[]{:S(2)}) collective-permute-start(bf16[4,32,384]{2,1,0:T(8,128)(2,1)S(1)} %get-tuple-element.12), channel_id=1, source_target_pairs={{0,1},{1,0},{2,3},{3,2},{4,5},{5,4},{6,7},{7,6},{8,9},{9,8},{10,11... | collective-permute-start | bytes 294920 | tf_op jit(solution)/shard_map/ppermute | solution.py:353
  27.3 2.8 %collective-permute-done.11.got = bf16[648,128]{1,0:T(8,128)(2,1)S(1)} collective-permute-done((bf16[648,128]{1,0:T(8,128)(2,1)S(1)}, bf16[648,128]{1,0:T(8,128)(2,1)S(1)}, u32[]{:S(2)}, u32[]{:S(2)}) %collective-permute-start.11) | collective-permute-done | bytes 165920 | tf_op jit(solution)/shard_map/ppermute | solution.py:329
  30.2 3.6 %collective-permute-start.12 = (bf16[648,128]{1,0:T(8,128)(2,1)S(1)}, bf16[648,128]{1,0:T(8,128)(2,1)S(1)}, u32[]{:S(2)}, u32[]{:S(2)}) collective-permute-start(bf16[648,128]{1,0:T(8,128)(2,1)S(1)} %shard_map.88.mine), channel_id=1, source_target_pairs={{0,24},{8,16},{16,8},{24,0},{1,25},{9,17},{17,9},{25,1},{2,26},{10... | collective-permute-start | bytes 497672 | tf_op jit(solution)/shard_map/ppermute | solution.py:329
  33.7 0.0 collective-permute-done.rest_1_
  33.7 0.6 %shard_map.79 = (bf16[2,128,384]{2,1,0:T(8,128)(2,1)S(1)}, bf16[2,64,384]{2,1,0:T(8,128)(2,1)S(1)}) custom-call(s32[8]{0:T(128)S(1)} %bitcast.19, bf16[4,32,384]{2,1,0:T(8,128)(2,1)S(1)} %get-tuple-element.11.rest_0_, bf16[4,32,384]{2,1,0:T(8,128)(2,1)S(1)} %collective-permute-done.rest_1_), custom_call_target="tpu_custom_call" | custom-call | bytes 491552 | tf_op jit(solution)/shard_map/pallas_call | solution.py:27
  34.4 1.7 %collective-permute-start.1 = (bf16[2,64,384]{2,1,0:T(8,128)(2,1)S(1)}, bf16[2,64,384]{2,1,0:T(8,128)(2,1)S(1)}, u32[]{:S(2)}, u32[]{:S(2)}) collective-permute-start(bf16[2,64,384]{2,1,0:T(8,128)(2,1)S(1)} %get-tuple-element.14), channel_id=1, source_target_pairs={{2,0},{4,2},{6,4},{0,6},{3,1},{5,3},{7,5},{1,7},{10,8},{12,10},{14... | collective-permute-start | bytes 294920 | tf_op jit(solution)/shard_map/ppermute | solution.py:362
  36.1 3.2 %collective-permute-done.1.later = bf16[2,64,384]{2,1,0:T(8,128)(2,1)S(1)} collective-permute-done((bf16[2,64,384]{2,1,0:T(8,128)(2,1)S(1)}, bf16[2,64,384]{2,1,0:T(8,128)(2,1)S(1)}, u32[]{:S(2)}, u32[]{:S(2)}) %collective-permute-start.1) | collective-permute-done | bytes 98336 | tf_op jit(solution)/shard_map/ppermute | solution.py:362
  39.3 1.4 %shard_map.80 = bf16[128,384]{1,0:T(8,128)(2,1)} custom-call(bf16[2,128,384]{2,1,0:T(8,128)(2,1)S(1)} %get-tuple-element.13.natural, bf16[2,64,384]{2,1,0:T(8,128)(2,1)S(1)} %collective-permute-done.1.later, bf16[3,384,768]{2,1,0:T(8,128)(2,1)S(1)} %copy-done), custom_call_target="tpu_custom_call" | custom-call | flops 226492416 | bytes 2162688 | tf_op jit(solution)/shard_map/pallas_call | solution.py:27
  40.7 0.0 collective-permute-done.12.got
  40.7 0.9 %shard_map.89 = f32[648,128]{1,0:T(8,128)} custom-call(bf16[648,128]{1,0:T(8,128)(2,1)S(1)} %shard_map.88.mine, bf16[648,128]{1,0:T(8,128)(2,1)S(1)} %collective-permute-done.12.got), custom_call_target="tpu_custom_call" | custom-call | bytes 663552 | tf_op jit(solution)/shard_map/pallas_call | solution.py:27
  (3 shorter events, 0.1 us)
Async XLA Ops:
  0.6 4.3 %copy-start.1 = (bf16[3,3,384,192]{2,3,1,0:T(8,128)(2,1)S(1)}, bf16[3,3,384,192]{2,3,1,0:T(8,128)(2,1)}, u32[]{:S(2)}) copy-start(bf16[3,3,384,192]{2,3,1,0:T(8,128)(2,1)} %param.9) | copy-start | bytes 3981316
  0.6 4.3 %copy-start.2 = (bf16[1,4,4,64,192]{4,3,2,1,0:T(8,128)(2,1)S(1)}, bf16[1,4,4,64,192]{4,3,2,1,0:T(8,128)(2,1)}, u32[]{:S(2)}) copy-start(bf16[1,4,4,64,192]{4,3,2,1,0:T(8,128)(2,1)} %param.10) | copy-start | bytes 1179652
  0.6 5.8 %collective-permute-start.2 = (bf16[4,32,384]{2,1,0:T(8,128)(2,1)}, bf16[4,32,384]{2,1,0:T(8,128)(2,1)S(1)}, u32[]{:S(2)}, u32[]{:S(2)}) collective-permute-start(bf16[4,32,384]{2,1,0:T(8,128)(2,1)} %bitcast.13), channel_id=1, source_target_pairs={{0,1},{1,0},{2,3},{3,2},{4,5},{5,4},{6,7},{7,6},{8,9},{9,8},{10,11... | collective-permute-start | bytes 294920 | tf_op jit(solution)/shard_map/ppermute | solution.py:239
  2.8 4.0 %collective-permute-start.3 = (bf16[4,32,384]{2,1,0:T(8,128)(2,1)}, bf16[4,32,384]{2,1,0:T(8,128)(2,1)S(1)}, u32[]{:S(2)}, u32[]{:S(2)}) collective-permute-start(bf16[4,32,384]{2,1,0:T(8,128)(2,1)} %bitcast.14), channel_id=1, source_target_pairs={{0,2},{2,4},{4,6},{6,0},{1,3},{3,5},{5,7},{7,1},{8,10},{10,12},{12... | collective-permute-start | bytes 294920 | tf_op jit(solution)/shard_map/ppermute | solution.py:237
  4.8 4.4 %collective-permute-start.4 = (bf16[4,32,384]{2,1,0:T(8,128)(2,1)}, bf16[4,32,384]{2,1,0:T(8,128)(2,1)S(1)}, u32[]{:S(2)}, u32[]{:S(2)}) collective-permute-start(bf16[4,32,384]{2,1,0:T(8,128)(2,1)} %bitcast.15), channel_id=1, source_target_pairs={{0,3},{1,2},{2,5},{3,4},{4,7},{5,6},{6,1},{7,0},{8,11},{9,10},{10,... | collective-permute-start | bytes 294920 | tf_op jit(solution)/shard_map/ppermute | solution.py:244
  4.9 4.4 %copy-start = (bf16[3,384,768]{2,1,0:T(8,128)(2,1)S(1)}, bf16[3,384,768]{2,1,0:T(8,128)(2,1)}, u32[]{:S(2)}) copy-start(bf16[3,384,768]{2,1,0:T(8,128)(2,1)} %rest_2_.1) | copy-start | bytes 5308420
  4.9 4.4 %copy-start.3 = (bf16[1,4,1,32,384]{4,3,2,1,0:T(8,128)(2,1)S(1)}, bf16[1,4,1,32,384]{4,3,2,1,0:T(8,128)(2,1)}, u32[]{:S(2)}) copy-start(bf16[1,4,1,32,384]{4,3,2,1,0:T(8,128)(2,1)} %param.6) | copy-start | bytes 294916
  4.9 4.4 %copy-start.4 = (f32[768]{0:T(1024)S(1)}, f32[768]{0:T(1024)}, u32[]{:S(2)}) copy-start(f32[768]{0:T(1024)} %param.8) | copy-start | bytes 9220
  4.9 4.4 %copy-start.5 = (s32[1,1,8]{2,1,0:T(1,128)S(1)}, s32[1,1,8]{2,1,0:T(1,128)}, u32[]{:S(2)}) copy-start(s32[1,1,8]{2,1,0:T(1,128)} %param.11) | copy-start | bytes 100
  11.8 4.0 %collective-permute-start.8 = (bf16[2,648,128]{2,1,0:T(8,128)(2,1)S(1)}, bf16[2,648,128]{2,1,0:T(8,128)(2,1)S(1)}, u32[]{:S(2)}, u32[]{:S(2)}) collective-permute-start(bf16[2,648,128]{2,1,0:T(8,128)(2,1)S(1)} %shard_map.85), channel_id=1, source_target_pairs={{0,2},{1,3},{2,0},{3,1},{4,6},{5,7},{6,4},{7,5},{8,10},{9,11},{10,... | collective-permute-start | bytes 995336 | tf_op jit(solution)/shard_map/ppermute | solution.py:309
  11.9 1.9 %collective-permute-start.6 = (bf16[1,648,128]{2,1,0:T(8,128)(2,1)S(1)}, bf16[1,648,128]{2,1,0:T(8,128)(2,1)S(1)}, u32[]{:S(2)}, u32[]{:S(2)}) collective-permute-start(bf16[1,648,128]{2,1,0:T(8,128)(2,1)S(1)} %get-tuple-element.17), channel_id=1, source_target_pairs={{0,2},{1,3},{2,0},{3,1},{4,6},{5,7},{6,4},{7,5},{8,10},{9,11},{10,... | collective-permute-start | bytes 497672 | tf_op jit(solution)/shard_map/ppermute | solution.py:309
  12.7 4.8 %collective-permute-start.5 = (bf16[1,648,128]{2,1,0:T(8,128)(2,1)S(1)}, bf16[1,648,128]{2,1,0:T(8,128)(2,1)S(1)}, u32[]{:S(2)}, u32[]{:S(2)}) collective-permute-start(bf16[1,648,128]{2,1,0:T(8,128)(2,1)S(1)} %shard_map.82), channel_id=1, source_target_pairs={{0,2},{1,3},{2,0},{3,1},{4,6},{5,7},{6,4},{7,5},{8,10},{9,11},{10,... | collective-permute-start | bytes 497672 | tf_op jit(solution)/shard_map/ppermute | solution.py:309
  14.1 6.6 %collective-permute-start.7 = (bf16[648,128]{1,0:T(8,128)(2,1)S(1)}, bf16[648,128]{1,0:T(8,128)(2,1)S(1)}, u32[]{:S(2)}, u32[]{:S(2)}) collective-permute-start(bf16[648,128]{1,0:T(8,128)(2,1)S(1)} %shard_map.84), channel_id=1, source_target_pairs={{0,5},{1,4},{2,7},{3,6},{4,1},{5,0},{6,3},{7,2},{8,13},{9,12},{10,... | collective-permute-start | bytes 497672 | tf_op jit(solution)/shard_map/ppermute | solution.py:321
  16.5 7.7 %collective-permute-start.10 = (bf16[648,128]{1,0:T(8,128)(2,1)S(1)}, bf16[648,128]{1,0:T(8,128)(2,1)S(1)}, u32[]{:S(2)}, u32[]{:S(2)}) collective-permute-start(bf16[648,128]{1,0:T(8,128)(2,1)S(1)} %get-tuple-element.19), channel_id=1, source_target_pairs={{0,4},{1,5},{2,6},{3,7},{4,0},{5,1},{6,2},{7,3},{8,12},{9,13},{10,... | collective-permute-start | bytes 497672 | tf_op jit(solution)/shard_map/ppermute | solution.py:321
  17.2 7.5 %collective-permute-start.9 = (bf16[648,128]{1,0:T(8,128)(2,1)S(1)}, bf16[648,128]{1,0:T(8,128)(2,1)S(1)}, u32[]{:S(2)}, u32[]{:S(2)}) collective-permute-start(bf16[648,128]{1,0:T(8,128)(2,1)S(1)} %get-tuple-element.18), channel_id=1, source_target_pairs={{0,1},{1,0},{2,3},{3,2},{4,5},{5,4},{6,7},{7,6},{8,9},{9,8},{10,11... | collective-permute-start | bytes 497672 | tf_op jit(solution)/shard_map/ppermute | solution.py:321
  24.8 5.3 %collective-permute-start.11 = (bf16[648,128]{1,0:T(8,128)(2,1)S(1)}, bf16[648,128]{1,0:T(8,128)(2,1)S(1)}, u32[]{:S(2)}, u32[]{:S(2)}) collective-permute-start(bf16[648,128]{1,0:T(8,128)(2,1)S(1)} %shard_map.87.mine), channel_id=1, source_target_pairs={{0,8},{8,0},{16,24},{24,16},{1,9},{9,1},{17,25},{25,17},{2,10},{10... | collective-permute-start | bytes 497672 | tf_op jit(solution)/shard_map/ppermute | solution.py:329
  26.3 7.4 %collective-permute-start = (bf16[4,32,384]{2,1,0:T(8,128)(2,1)S(1)}, bf16[4,32,384]{2,1,0:T(8,128)(2,1)S(1)}, u32[]{:S(2)}, u32[]{:S(2)}) collective-permute-start(bf16[4,32,384]{2,1,0:T(8,128)(2,1)S(1)} %get-tuple-element.12), channel_id=1, source_target_pairs={{0,1},{1,0},{2,3},{3,2},{4,5},{5,4},{6,7},{7,6},{8,9},{9,8},{10,11... | collective-permute-start | bytes 294920 | tf_op jit(solution)/shard_map/ppermute | solution.py:353
  30.2 10.5 %collective-permute-start.12 = (bf16[648,128]{1,0:T(8,128)(2,1)S(1)}, bf16[648,128]{1,0:T(8,128)(2,1)S(1)}, u32[]{:S(2)}, u32[]{:S(2)}) collective-permute-start(bf16[648,128]{1,0:T(8,128)(2,1)S(1)} %shard_map.88.mine), channel_id=1, source_target_pairs={{0,24},{8,16},{16,8},{24,0},{1,25},{9,17},{17,9},{25,1},{2,26},{10... | collective-permute-start | bytes 497672 | tf_op jit(solution)/shard_map/ppermute | solution.py:329
  34.4 4.9 %collective-permute-start.1 = (bf16[2,64,384]{2,1,0:T(8,128)(2,1)S(1)}, bf16[2,64,384]{2,1,0:T(8,128)(2,1)S(1)}, u32[]{:S(2)}, u32[]{:S(2)}) collective-permute-start(bf16[2,64,384]{2,1,0:T(8,128)(2,1)S(1)} %get-tuple-element.14), channel_id=1, source_target_pairs={{2,0},{4,2},{6,4},{0,6},{3,1},{5,3},{7,5},{1,7},{10,8},{12,10},{14... | collective-permute-start | bytes 294920 | tf_op jit(solution)/shard_map/ppermute | solution.py:362

commit v7 on v6

--- a/solution.py
+++ b/solution.py
@@ -79,41 +79,69 @@
         bands[d][...] = acts[:, pl.ds(start, r * W), :]
 
 
-def transposed_acts(sizes, order, bias, time_weight, bands, ext, acts, picked):
-    S, rW, n_row, F, C = sizes
+def extended(sizes, ext, bands):
+    rW, n_row = sizes[1], sizes[2]
+    me = lax.axis_index("row")
+    for d in range(n_row):
+        source = lax.rem(me - d + n_row, n_row)
+        for f, block in enumerate(bands(d)):
+            start = pl.multiple_of(f * n_row * rW + source * rW, rW)
+            ext[pl.ds(start, rW), :] = block
+
+
+def time_conv(sizes, frames, bias, time_weight, ext, acts):
+    _, rW, n_row, _, C = sizes
+    step = n_row * rW
+    row = jnp.concatenate([bias[i : i + 1, :] for i in range(bias.shape[0])], axis=1)
+    total = jnp.broadcast_to(row, (frames * step, 2 * C))
+    for k in range(3):
+        total = total + jnp.dot(
+            ext[k * step : (k + frames) * step, :], time_weight[k], preferred_element_type=F32
+        )
+    rounded = total.astype(BF16).reshape(frames, step, 2 * C)
+    acts[0] = rounded[:, :, :C]
+    acts[1] = rounded[:, :, C:]
+
+
+def late_kernel(sizes, bias, time_weight, *rest):
+    n_row, F = sizes[2], sizes[3]
+    own, (acts, ext) = rest[:n_row], rest[n_row:]
+    extended(sizes, ext, lambda d: [own[d][f] for f in range(F)])
+    time_conv(sizes, F - 2, bias, time_weight, ext, acts)
+
+
+def transposed_acts(sizes, order, bias, time_weight, late, bands, ext, early, picked):
+    S, rW, n_row, F, _ = sizes
     step = n_row * rW
     own, prior = bands[:n_row], bands[n_row:]
+    whole = jnp.where(lax.axis_index("frame") > 0, 1.0, 0.0)
+
+    def frames(d):
+        before = [(prior[d][f].astype(F32) * whole).astype(BF16) for f in range(F - 2, F)]
+        return before + [own[d][f] for f in range(2)]
+
+    extended(sizes, ext, frames)
+    time_conv(sizes, 2, bias, time_weight, ext, early)
     me = lax.axis_index("row")
-    whole = jnp.where(lax.axis_index("frame") > 0, 1.0, 0.0)
-    for d in range(n_row):
-        source = lax.rem(me - d + n_row, n_row)
-        for f in range(F + 2):
-            start = pl.multiple_of(f * step + source * rW, rW)
-            if f < 2:
-                block = (prior[d][F - 2 + f].astype(F32) * whole).astype(BF16)
-            else:
-                block = own[d][f - 2]
-            ext[pl.ds(start, rW), :] = block
-    row = jnp.concatenate([bias[i : i + 1, :] for i in range(bias.shape[0])], axis=1)
-    total = jnp.broadcast_to(row, (F * step, 2 * C))
-    for k in range(3):
-        total = total + jnp.dot(
-            ext[k * step : (k + F) * step, :], time_weight[k], preferred_element_type=F32
-        )
-    rounded = total.astype(BF16)
-    acts[0] = rounded[:, :C]
-    acts[1] = rounded[:, C:]
     for s in range(S):
         o = order[me * S + s]
-        start = pl.multiple_of((o // 2) * step, step)
-        picked[s * step : (s + 1) * step, :] = acts[o % 2, pl.ds(start, step), :]
+        f = o // 2
+
+        @pl.when(f < 2)
+        def _():
+            picked[s * step : (s + 1) * step, :] = early[o % 2, f]
+
+        @pl.when(f >= 2)
+        def _():
+            picked[s * step : (s + 1) * step, :] = late[o % 2, f - 2]
+
     return picked[...].astype(F32).T.astype(BF16)
 
 
-def all_kernel(sizes, order, bias, time_weight, g, *rest):
+def all_kernel(sizes, order, bias, time_weight, late, g, *rest):
     n_row, C = sizes[2], sizes[4]
     out, *scratch = rest[2 * n_row :]
-    left = transposed_acts(sizes, order, bias, time_weight, rest[: 2 * n_row], *scratch)
+    left = transposed_acts(sizes, order, bias, time_weight, late, rest[: 2 * n_row], *scratch)
     for t in range(9):
         out[t * C : (t + 1) * C, :] = jnp.dot(left, g[t], preferred_element_type=F32)
 
@@ -146,10 +174,10 @@
 
 def send_kernel(sizes, plan, group, *rest):
     if sizes:
-        order, bias, time_weight, g, *rest = rest
+        order, bias, time_weight, late, g, *rest = rest
         n_row = sizes[2]
         left, out, *scratch, terms = rest[2 * n_row :]
-        left[...] = transposed_acts(sizes, order, bias, time_weight, rest[: 2 * n_row], *scratch)
+        left[...] = transposed_acts(sizes, order, bias, time_weight, late, rest[: 2 * n_row], *scratch)
     else:
         g, left, out, terms = rest
     for j, d in enumerate(group):
@@ -272,13 +300,22 @@
         and CO == 192
     )
     packed = chunk * CO // 128
-    inputs = [order, time_bias.reshape(-1, 128), time_weight, g] + own + prior
+    sizes = (S, rW, n_row, F, C)
+    bias = time_bias.reshape(-1, 128)
+    (late,) = kernel_call(
+        functools.partial(late_kernel, sizes),
+        [struct((2, F - 2, HR * W, C), BF16)],
+        0,
+        [bias, time_weight] + own,
+        [pltpu.VMEM((F * HR * W, C), BF16)],
+        flops=2 * (F - 2) * HR * W * 6 * C * C,
+    )
+    inputs = [order, bias, time_weight, late, g] + own + prior
     ext = [
-        pltpu.VMEM(((F + 2) * HR * W, C), BF16),
-        pltpu.VMEM((2, F * HR * W, C), BF16),
+        pltpu.VMEM((4 * HR * W, C), BF16),
+        pltpu.VMEM((2, 2, HR * W, C), BF16),
         pltpu.VMEM((pixels, C), BF16),
     ]
-    sizes = (S, rW, n_row, F, C)
     flops = 2 * pixels * 9 * C * CO
 
     scale = 1.0 / math.sqrt(2 * F * UR * UW * n_clip * n_frame)

time: 41.7 us -> 41.5 us (level)
  waiting for transfers between devices: 16.5 us -> 16 us
    pallas_call x13 -> x14, Pallas kernels: 8.82 us -> 9.07 us  [kernel_call(): pl.pallas_call(body, out_shape=outs, in_specs=specs, out_specs=[VMEM] * l...]
  transfers between devices with their start and end apart: 13 -> 13, of which waited for: 8 -> 7; matrix products, arithmetic and copies ran while one was open for 0% -> 0% of each run, Pallas kernels for 13% -> 14%
where the time goes in v7:
time: 41.5 us; the launch traced here: 41.3 us
  waiting for transfers between devices  16 us (39%)
  starting transfers between devices  15.4 us (37%)
  Pallas kernels  9.07 us (22%)
  between operations  0.81 us (2%)
    pallas_call x14, Pallas kernels, kernel_call(): pl.pallas_call(body, out_shape=outs, in_specs=specs, out_specs=[VMEM] * l...  9.07 us
    ppermute x3, waiting for transfers between devices, local(): got.append(lax.ppermute(share, both, route))  6.81 us
    ppermute x2, starting transfers between devices, local(): got = lax.ppermute(mine, 'clip', [(i, i ^ mask) for i in range(n_clip)])  5.07 us
    ppermute x1, waiting for transfers between devices, local(): later = lax.ppermute(first, 'frame', [(j, i) for i, j in forward])  3.21 us
    ppermute x2, waiting for transfers between devices, local(): got = lax.ppermute(mine, 'clip', [(i, i ^ mask) for i in range(n_clip)])  2.81 us
    ppermute x3, starting transfers between devices, local(): got.append(lax.ppermute(share, both, route))  2.77 us
    ppermute x1, waiting for transfers between devices, local(): prior.append(lax.ppermute(feats, both, route))  2.26 us
    ppermute x1, starting transfers between devices, local(): lax.ppermute(feats, 'row', [(i, (i + d) % n_row) for i in range(n_row)])  2.12 us
  transfers between devices with their start and end apart: 13, of which 7 were waited for; matrix products, arithmetic and copies ran while one was open for 0% of the time, Pallas kernels for 14%

profile of v7, /device:TPU:1, one launch (start us, length us, event | category | flops | bytes accessed | tf_op | source)
XLA Modules:
  0.0 41.3 jit_solution(3663451308075829841)
XLA Ops:
  0.6 0.0 copy-start.1
  0.6 0.0 copy-start.2
  0.6 2.1 %collective-permute-start.2 = (bf16[4,32,384]{2,1,0:T(8,128)(2,1)}, bf16[4,32,384]{2,1,0:T(8,128)(2,1)S(1)}, u32[]{:S(2)}, u32[]{:S(2)}) collective-permute-start(bf16[4,32,384]{2,1,0:T(8,128)(2,1)} %bitcast.13), channel_id=1, source_target_pairs={{0,1},{1,0},{2,3},{3,2},{4,5},{5,4},{6,7},{7,6},{8,9},{9,8},{10,11... | collective-permute-start | bytes 294920 | tf_op jit(solution)/shard_map/ppermute | solution.py:267
  2.8 2.1 %collective-permute-start.3 = (bf16[4,32,384]{2,1,0:T(8,128)(2,1)}, bf16[4,32,384]{2,1,0:T(8,128)(2,1)S(1)}, u32[]{:S(2)}, u32[]{:S(2)}) collective-permute-start(bf16[4,32,384]{2,1,0:T(8,128)(2,1)} %bitcast.14), channel_id=1, source_target_pairs={{0,2},{2,4},{4,6},{6,0},{1,3},{3,5},{5,7},{7,1},{8,10},{10,12},{12... | collective-permute-start | bytes 294920 | tf_op jit(solution)/shard_map/ppermute | solution.py:265
  4.8 0.0 collective-permute-start.4
  4.9 0.0 copy-start
  4.9 0.0 copy-start.3
  4.9 0.0 copy-start.4
  4.9 0.0 copy-done.1
  4.9 0.0 copy-done.2
  4.9 1.5 %shard_map.78 = (bf16[9,256,192]{2,1,0:T(8,128)(2,1)S(1)}, bf16[4,32,384]{2,1,0:T(8,128)(2,1)S(1)}, bf16[4,32,384]{2,1,0:T(8,128)(2,1)S(1)}) custom-call(bf16[4,256,192]{2,1,0:T(8,128)(2,1)S(1)} %bitcast.12, bf16[9,192,384]{2,1,0:T(8,128)(2,1)S(1)} %bitcast.11, bf16[288,256]{1,0:T(8,128)(2,1)S(1)} %shard_map.77.box), custom_call_target="tpu_custom_call" | custom-call | flops 339738624 | bytes 2949120 | tf_op jit(solution)/shard_map/pallas_call | solution.py:27
  6.4 0.0 copy-start.5
  6.4 0.0 collective-permute-done.2.rest_1_.rest_6_
  6.4 0.0 copy-done
  6.4 0.0 copy-done.3
  6.5 0.5 %shard_map.81.rest_3_ = bf16[2,2,64,384]{3,2,1,0:T(8,128)(2,1)S(1)} custom-call(f32[6,128]{1,0:T(8,128)S(1)} %bitcast.18, bf16[3,384,768]{2,1,0:T(8,128)(2,1)S(1)} %copy-done, bf16[4,32,384]{2,1,0:T(8,128)(2,1)S(1)} %bitcast.16, bf16[4,32,384]{2,1,0:T(8,128)(2,1)S(1)} %collective-permute-done.2.rest_1_.rest_6_), custom_call_target="tpu_custom_call" | custom-call | flops 226492416 | bytes 2165760 | tf_op jit(solution)/shard_map/pallas_call | solution.py:27
  7.0 0.0 collective-permute-done.3.rest_7_
  7.0 2.3 %collective-permute-done.4.rest_8_ = bf16[4,32,384]{2,1,0:T(8,128)(2,1)S(1)} collective-permute-done((bf16[4,32,384]{2,1,0:T(8,128)(2,1)}, bf16[4,32,384]{2,1,0:T(8,128)(2,1)S(1)}, u32[]{:S(2)}, u32[]{:S(2)}) %collective-permute-start.4) | collective-permute-done | bytes 98336 | tf_op jit(solution)/shard_map/ppermute | solution.py:272
  9.2 1.6 %shard_map.82 = (bf16[384,256]{1,0:T(8,128)(2,1)S(1)}, bf16[1,648,128]{2,1,0:T(8,128)(2,1)S(1)}) custom-call(s32[8]{0:T(128)S(1)} %bitcast.20, f32[6,128]{1,0:T(8,128)S(1)} %bitcast.19, bf16[3,384,768]{2,1,0:T(8,128)(2,1)S(1)} %copy-done, bf16[2,2,64,384]{3,2,1,0:T(8,128)(2,1)S(1)} %shard_map.81.rest_3_, ...), custom_call_target="tpu_custom_call" | custom-call | flops 42467328 | bytes 3609632 | tf_op jit(solution)/shard_map/pallas_call | solution.py:27
  10.8 0.7 %shard_map.86 = bf16[2,648,128]{2,1,0:T(8,128)(2,1)S(1)} custom-call(bf16[9,256,192]{2,1,0:T(8,128)(2,1)S(1)} %get-tuple-element.15.rest_4_.rest_0_.g, bf16[384,256]{1,0:T(8,128)(2,1)S(1)} %get-tuple-element.16.rest_1_.left), custom_call_target="tpu_custom_call" | custom-call | flops 84934656 | bytes 1413120 | tf_op jit(solution)/shard_map/pallas_call | solution.py:27
  11.5 0.1 collective-permute-start.8
  11.6 0.5 %collective-permute-start.6 = (bf16[1,648,128]{2,1,0:T(8,128)(2,1)S(1)}, bf16[1,648,128]{2,1,0:T(8,128)(2,1)S(1)}, u32[]{:S(2)}, u32[]{:S(2)}) collective-permute-start(bf16[1,648,128]{2,1,0:T(8,128)(2,1)S(1)} %get-tuple-element.17), channel_id=1, source_target_pairs={{0,2},{1,3},{2,0},{3,1},{4,6},{5,7},{6,4},{7,5},{8,10},{9,11},{10,... | collective-permute-start | bytes 497672 | tf_op jit(solution)/shard_map/ppermute | solution.py:346
  12.1 0.3 shard_map.83
  12.5 0.1 collective-permute-start.5
  12.6 0.9 %collective-permute-done.6.got = bf16[1,648,128]{2,1,0:T(8,128)(2,1)S(1)} collective-permute-done((bf16[1,648,128]{2,1,0:T(8,128)(2,1)S(1)}, bf16[1,648,128]{2,1,0:T(8,128)(2,1)S(1)}, u32[]{:S(2)}, u32[]{:S(2)}) %collective-permute-start.6) | collective-permute-done | bytes 165920 | tf_op jit(solution)/shard_map/ppermute | solution.py:346
  13.5 0.3 shard_map.85
  13.8 1.7 %collective-permute-start.7 = (bf16[648,128]{1,0:T(8,128)(2,1)S(1)}, bf16[648,128]{1,0:T(8,128)(2,1)S(1)}, u32[]{:S(2)}, u32[]{:S(2)}) collective-permute-start(bf16[648,128]{1,0:T(8,128)(2,1)S(1)} %shard_map.85), channel_id=1, source_target_pairs={{0,5},{1,4},{2,7},{3,6},{4,1},{5,0},{6,3},{7,2},{8,13},{9,12},{10,... | collective-permute-start | bytes 497672 | tf_op jit(solution)/shard_map/ppermute | solution.py:358
  15.5 0.0 collective-permute-done.8.got
  15.5 0.7 %shard_map.87 = (bf16[648,128]{1,0:T(8,128)(2,1)S(1)}, bf16[648,128]{1,0:T(8,128)(2,1)S(1)}) custom-call(bf16[9,256,192]{2,1,0:T(8,128)(2,1)S(1)} %get-tuple-element.15.rest_4_.rest_0_.g, bf16[384,256]{1,0:T(8,128)(2,1)S(1)} %get-tuple-element.16.rest_1_.left, bf16[2,648,128]{2,1,0:T(8,128)(2,1)S(1)} %collective-permute-done.8.got), custom_call_target="tpu_custom_call" | custom-call | flops 84934656 | bytes 1744896 | tf_op jit(solution)/shard_map/pallas_call | solution.py:27
  16.2 0.7 %collective-permute-start.10 = (bf16[648,128]{1,0:T(8,128)(2,1)S(1)}, bf16[648,128]{1,0:T(8,128)(2,1)S(1)}, u32[]{:S(2)}, u32[]{:S(2)}) collective-permute-start(bf16[648,128]{1,0:T(8,128)(2,1)S(1)} %get-tuple-element.19), channel_id=1, source_target_pairs={{0,4},{1,5},{2,6},{3,7},{4,0},{5,1},{6,2},{7,3},{8,12},{9,13},{10,... | collective-permute-start | bytes 497672 | tf_op jit(solution)/shard_map/ppermute | solution.py:358
  16.9 0.4 collective-permute-start.9
  17.3 0.0 collective-permute-done.5.got
  17.3 0.4 shard_map.84.keep
  17.6 2.8 %collective-permute-done.7.rest_0_ = bf16[648,128]{1,0:T(8,128)(2,1)S(1)} collective-permute-done((bf16[648,128]{1,0:T(8,128)(2,1)S(1)}, bf16[648,128]{1,0:T(8,128)(2,1)S(1)}, u32[]{:S(2)}, u32[]{:S(2)}) %collective-permute-start.7) | collective-permute-done | bytes 165920 | tf_op jit(solution)/shard_map/ppermute | solution.py:358
  20.4 3.5 %collective-permute-done.10.rest_2_ = bf16[648,128]{1,0:T(8,128)(2,1)S(1)} collective-permute-done((bf16[648,128]{1,0:T(8,128)(2,1)S(1)}, bf16[648,128]{1,0:T(8,128)(2,1)S(1)}, u32[]{:S(2)}, u32[]{:S(2)}) %collective-permute-start.10) | collective-permute-done | bytes 165920 | tf_op jit(solution)/shard_map/ppermute | solution.py:358
  23.9 0.5 %collective-permute-done.9.rest_1_ = bf16[648,128]{1,0:T(8,128)(2,1)S(1)} collective-permute-done((bf16[648,128]{1,0:T(8,128)(2,1)S(1)}, bf16[648,128]{1,0:T(8,128)(2,1)S(1)}, u32[]{:S(2)}, u32[]{:S(2)}) %collective-permute-start.9) | collective-permute-done | bytes 165920 | tf_op jit(solution)/shard_map/ppermute | solution.py:358
  24.4 0.1 shard_map.88.mine
  24.5 1.5 %collective-permute-start.11 = (bf16[648,128]{1,0:T(8,128)(2,1)S(1)}, bf16[648,128]{1,0:T(8,128)(2,1)S(1)}, u32[]{:S(2)}, u32[]{:S(2)}) collective-permute-start(bf16[648,128]{1,0:T(8,128)(2,1)S(1)} %shard_map.88.mine), channel_id=1, source_target_pairs={{0,8},{8,0},{16,24},{24,16},{1,9},{9,1},{17,25},{25,17},{2,10},{10... | collective-permute-start | bytes 497672 | tf_op jit(solution)/shard_map/ppermute | solution.py:366
  26.0 1.0 %collective-permute-start = (bf16[4,32,384]{2,1,0:T(8,128)(2,1)S(1)}, bf16[4,32,384]{2,1,0:T(8,128)(2,1)S(1)}, u32[]{:S(2)}, u32[]{:S(2)}) collective-permute-start(bf16[4,32,384]{2,1,0:T(8,128)(2,1)S(1)} %get-tuple-element.12), channel_id=1, source_target_pairs={{0,1},{1,0},{2,3},{3,2},{4,5},{5,4},{6,7},{7,6},{8,9},{9,8},{10,11... | collective-permute-start | bytes 294920 | tf_op jit(solution)/shard_map/ppermute | solution.py:390
  27.1 2.8 %collective-permute-done.11.got = bf16[648,128]{1,0:T(8,128)(2,1)S(1)} collective-permute-done((bf16[648,128]{1,0:T(8,128)(2,1)S(1)}, bf16[648,128]{1,0:T(8,128)(2,1)S(1)}, u32[]{:S(2)}, u32[]{:S(2)}) %collective-permute-start.11) | collective-permute-done | bytes 165920 | tf_op jit(solution)/shard_map/ppermute | solution.py:366
  29.9 3.6 %collective-permute-start.12 = (bf16[648,128]{1,0:T(8,128)(2,1)S(1)}, bf16[648,128]{1,0:T(8,128)(2,1)S(1)}, u32[]{:S(2)}, u32[]{:S(2)}) collective-permute-start(bf16[648,128]{1,0:T(8,128)(2,1)S(1)} %shard_map.89.mine), channel_id=1, source_target_pairs={{0,24},{8,16},{16,8},{24,0},{1,25},{9,17},{17,9},{25,1},{2,26},{10... | collective-permute-start | bytes 497672 | tf_op jit(solution)/shard_map/ppermute | solution.py:366
  33.5 0.0 collective-permute-done.rest_1_
  33.5 0.6 %shard_map.79 = (bf16[2,128,384]{2,1,0:T(8,128)(2,1)S(1)}, bf16[2,64,384]{2,1,0:T(8,128)(2,1)S(1)}) custom-call(s32[8]{0:T(128)S(1)} %bitcast.21, bf16[4,32,384]{2,1,0:T(8,128)(2,1)S(1)} %get-tuple-element.11.rest_0_, bf16[4,32,384]{2,1,0:T(8,128)(2,1)S(1)} %collective-permute-done.rest_1_), custom_call_target="tpu_custom_call" | custom-call | bytes 491552 | tf_op jit(solution)/shard_map/pallas_call | solution.py:27
  34.1 1.7 %collective-permute-start.1 = (bf16[2,64,384]{2,1,0:T(8,128)(2,1)S(1)}, bf16[2,64,384]{2,1,0:T(8,128)(2,1)S(1)}, u32[]{:S(2)}, u32[]{:S(2)}) collective-permute-start(bf16[2,64,384]{2,1,0:T(8,128)(2,1)S(1)} %get-tuple-element.14), channel_id=1, source_target_pairs={{2,0},{4,2},{6,4},{0,6},{3,1},{5,3},{7,5},{1,7},{10,8},{12,10},{14... | collective-permute-start | bytes 294920 | tf_op jit(solution)/shard_map/ppermute | solution.py:399
  35.8 3.2 %collective-permute-done.1.later = bf16[2,64,384]{2,1,0:T(8,128)(2,1)S(1)} collective-permute-done((bf16[2,64,384]{2,1,0:T(8,128)(2,1)S(1)}, bf16[2,64,384]{2,1,0:T(8,128)(2,1)S(1)}, u32[]{:S(2)}, u32[]{:S(2)}) %collective-permute-start.1) | collective-permute-done | bytes 98336 | tf_op jit(solution)/shard_map/ppermute | solution.py:399
  39.0 1.4 %shard_map.80 = bf16[128,384]{1,0:T(8,128)(2,1)} custom-call(bf16[2,128,384]{2,1,0:T(8,128)(2,1)S(1)} %get-tuple-element.13.natural, bf16[2,64,384]{2,1,0:T(8,128)(2,1)S(1)} %collective-permute-done.1.later, bf16[3,384,768]{2,1,0:T(8,128)(2,1)S(1)} %copy-done), custom_call_target="tpu_custom_call" | custom-call | flops 226492416 | bytes 2162688 | tf_op jit(solution)/shard_map/pallas_call | solution.py:27
  40.4 0.0 collective-permute-done.12.got
  40.4 0.9 %shard_map.90 = f32[648,128]{1,0:T(8,128)} custom-call(bf16[648,128]{1,0:T(8,128)(2,1)S(1)} %shard_map.89.mine, bf16[648,128]{1,0:T(8,128)(2,1)S(1)} %collective-permute-done.12.got), custom_call_target="tpu_custom_call" | custom-call | bytes 663552 | tf_op jit(solution)/shard_map/pallas_call | solution.py:27
  (4 shorter events, 0.1 us)
Async XLA Ops:
  0.6 4.3 %copy-start.1 = (bf16[3,3,384,192]{2,3,1,0:T(8,128)(2,1)S(1)}, bf16[3,3,384,192]{2,3,1,0:T(8,128)(2,1)}, u32[]{:S(2)}) copy-start(bf16[3,3,384,192]{2,3,1,0:T(8,128)(2,1)} %param.9) | copy-start | bytes 3981316
  0.6 4.3 %copy-start.2 = (bf16[1,4,4,64,192]{4,3,2,1,0:T(8,128)(2,1)S(1)}, bf16[1,4,4,64,192]{4,3,2,1,0:T(8,128)(2,1)}, u32[]{:S(2)}) copy-start(bf16[1,4,4,64,192]{4,3,2,1,0:T(8,128)(2,1)} %param.10) | copy-start | bytes 1179652
  0.6 5.8 %collective-permute-start.2 = (bf16[4,32,384]{2,1,0:T(8,128)(2,1)}, bf16[4,32,384]{2,1,0:T(8,128)(2,1)S(1)}, u32[]{:S(2)}, u32[]{:S(2)}) collective-permute-start(bf16[4,32,384]{2,1,0:T(8,128)(2,1)} %bitcast.13), channel_id=1, source_target_pairs={{0,1},{1,0},{2,3},{3,2},{4,5},{5,4},{6,7},{7,6},{8,9},{9,8},{10,11... | collective-permute-start | bytes 294920 | tf_op jit(solution)/shard_map/ppermute | solution.py:267
  2.8 4.2 %collective-permute-start.3 = (bf16[4,32,384]{2,1,0:T(8,128)(2,1)}, bf16[4,32,384]{2,1,0:T(8,128)(2,1)S(1)}, u32[]{:S(2)}, u32[]{:S(2)}) collective-permute-start(bf16[4,32,384]{2,1,0:T(8,128)(2,1)} %bitcast.14), channel_id=1, source_target_pairs={{0,2},{2,4},{4,6},{6,0},{1,3},{3,5},{5,7},{7,1},{8,10},{10,12},{12... | collective-permute-start | bytes 294920 | tf_op jit(solution)/shard_map/ppermute | solution.py:265
  4.8 4.4 %collective-permute-start.4 = (bf16[4,32,384]{2,1,0:T(8,128)(2,1)}, bf16[4,32,384]{2,1,0:T(8,128)(2,1)S(1)}, u32[]{:S(2)}, u32[]{:S(2)}) collective-permute-start(bf16[4,32,384]{2,1,0:T(8,128)(2,1)} %bitcast.15), channel_id=1, source_target_pairs={{0,3},{1,2},{2,5},{3,4},{4,7},{5,6},{6,1},{7,0},{8,11},{9,10},{10,... | collective-permute-start | bytes 294920 | tf_op jit(solution)/shard_map/ppermute | solution.py:272
  4.9 1.6 %copy-start = (bf16[3,384,768]{2,1,0:T(8,128)(2,1)S(1)}, bf16[3,384,768]{2,1,0:T(8,128)(2,1)}, u32[]{:S(2)}) copy-start(bf16[3,384,768]{2,1,0:T(8,128)(2,1)} %rest_2_.1) | copy-start | bytes 5308420
  4.9 1.6 %copy-start.3 = (bf16[1,4,1,32,384]{4,3,2,1,0:T(8,128)(2,1)S(1)}, bf16[1,4,1,32,384]{4,3,2,1,0:T(8,128)(2,1)}, u32[]{:S(2)}) copy-start(bf16[1,4,1,32,384]{4,3,2,1,0:T(8,128)(2,1)} %param.6) | copy-start | bytes 294916
  4.9 1.6 %copy-start.4 = (f32[768]{0:T(1024)S(1)}, f32[768]{0:T(1024)}, u32[]{:S(2)}) copy-start(f32[768]{0:T(1024)} %param.8) | copy-start | bytes 9220
  6.4 2.8 %copy-start.5 = (s32[1,1,8]{2,1,0:T(1,128)S(1)}, s32[1,1,8]{2,1,0:T(1,128)}, u32[]{:S(2)}) copy-start(s32[1,1,8]{2,1,0:T(1,128)} %param.11) | copy-start | bytes 100
  11.5 4.0 %collective-permute-start.8 = (bf16[2,648,128]{2,1,0:T(8,128)(2,1)S(1)}, bf16[2,648,128]{2,1,0:T(8,128)(2,1)S(1)}, u32[]{:S(2)}, u32[]{:S(2)}) collective-permute-start(bf16[2,648,128]{2,1,0:T(8,128)(2,1)S(1)} %shard_map.86), channel_id=1, source_target_pairs={{0,2},{1,3},{2,0},{3,1},{4,6},{5,7},{6,4},{7,5},{8,10},{9,11},{10,... | collective-permute-start | bytes 995336 | tf_op jit(solution)/shard_map/ppermute | solution.py:346
  11.6 1.9 %collective-permute-start.6 = (bf16[1,648,128]{2,1,0:T(8,128)(2,1)S(1)}, bf16[1,648,128]{2,1,0:T(8,128)(2,1)S(1)}, u32[]{:S(2)}, u32[]{:S(2)}) collective-permute-start(bf16[1,648,128]{2,1,0:T(8,128)(2,1)S(1)} %get-tuple-element.17), channel_id=1, source_target_pairs={{0,2},{1,3},{2,0},{3,1},{4,6},{5,7},{6,4},{7,5},{8,10},{9,11},{10,... | collective-permute-start | bytes 497672 | tf_op jit(solution)/shard_map/ppermute | solution.py:346
  12.5 4.8 %collective-permute-start.5 = (bf16[1,648,128]{2,1,0:T(8,128)(2,1)S(1)}, bf16[1,648,128]{2,1,0:T(8,128)(2,1)S(1)}, u32[]{:S(2)}, u32[]{:S(2)}) collective-permute-start(bf16[1,648,128]{2,1,0:T(8,128)(2,1)S(1)} %shard_map.83), channel_id=1, source_target_pairs={{0,2},{1,3},{2,0},{3,1},{4,6},{5,7},{6,4},{7,5},{8,10},{9,11},{10,... | collective-permute-start | bytes 497672 | tf_op jit(solution)/shard_map/ppermute | solution.py:346
  13.8 6.6 %collective-permute-start.7 = (bf16[648,128]{1,0:T(8,128)(2,1)S(1)}, bf16[648,128]{1,0:T(8,128)(2,1)S(1)}, u32[]{:S(2)}, u32[]{:S(2)}) collective-permute-start(bf16[648,128]{1,0:T(8,128)(2,1)S(1)} %shard_map.85), channel_id=1, source_target_pairs={{0,5},{1,4},{2,7},{3,6},{4,1},{5,0},{6,3},{7,2},{8,13},{9,12},{10,... | collective-permute-start | bytes 497672 | tf_op jit(solution)/shard_map/ppermute | solution.py:358
  16.2 7.7 %collective-permute-start.10 = (bf16[648,128]{1,0:T(8,128)(2,1)S(1)}, bf16[648,128]{1,0:T(8,128)(2,1)S(1)}, u32[]{:S(2)}, u32[]{:S(2)}) collective-permute-start(bf16[648,128]{1,0:T(8,128)(2,1)S(1)} %get-tuple-element.19), channel_id=1, source_target_pairs={{0,4},{1,5},{2,6},{3,7},{4,0},{5,1},{6,2},{7,3},{8,12},{9,13},{10,... | collective-permute-start | bytes 497672 | tf_op jit(solution)/shard_map/ppermute | solution.py:358
  16.9 7.5 %collective-permute-start.9 = (bf16[648,128]{1,0:T(8,128)(2,1)S(1)}, bf16[648,128]{1,0:T(8,128)(2,1)S(1)}, u32[]{:S(2)}, u32[]{:S(2)}) collective-permute-start(bf16[648,128]{1,0:T(8,128)(2,1)S(1)} %get-tuple-element.18), channel_id=1, source_target_pairs={{0,1},{1,0},{2,3},{3,2},{4,5},{5,4},{6,7},{7,6},{8,9},{9,8},{10,11... | collective-permute-start | bytes 497672 | tf_op jit(solution)/shard_map/ppermute | solution.py:358
  24.5 5.3 %collective-permute-start.11 = (bf16[648,128]{1,0:T(8,128)(2,1)S(1)}, bf16[648,128]{1,0:T(8,128)(2,1)S(1)}, u32[]{:S(2)}, u32[]{:S(2)}) collective-permute-start(bf16[648,128]{1,0:T(8,128)(2,1)S(1)} %shard_map.88.mine), channel_id=1, source_target_pairs={{0,8},{8,0},{16,24},{24,16},{1,9},{9,1},{17,25},{25,17},{2,10},{10... | collective-permute-start | bytes 497672 | tf_op jit(solution)/shard_map/ppermute | solution.py:366
  26.0 7.4 %collective-permute-start = (bf16[4,32,384]{2,1,0:T(8,128)(2,1)S(1)}, bf16[4,32,384]{2,1,0:T(8,128)(2,1)S(1)}, u32[]{:S(2)}, u32[]{:S(2)}) collective-permute-start(bf16[4,32,384]{2,1,0:T(8,128)(2,1)S(1)} %get-tuple-element.12), channel_id=1, source_target_pairs={{0,1},{1,0},{2,3},{3,2},{4,5},{5,4},{6,7},{7,6},{8,9},{9,8},{10,11... | collective-permute-start | bytes 294920 | tf_op jit(solution)/shard_map/ppermute | solution.py:390
  29.9 10.5 %collective-permute-start.12 = (bf16[648,128]{1,0:T(8,128)(2,1)S(1)}, bf16[648,128]{1,0:T(8,128)(2,1)S(1)}, u32[]{:S(2)}, u32[]{:S(2)}) collective-permute-start(bf16[648,128]{1,0:T(8,128)(2,1)S(1)} %shard_map.89.mine), channel_id=1, source_target_pairs={{0,24},{8,16},{16,8},{24,0},{1,25},{9,17},{17,9},{25,1},{2,26},{10... | collective-permute-start | bytes 497672 | tf_op jit(solution)/shard_map/ppermute | solution.py:366
  34.1 4.9 %collective-permute-start.1 = (bf16[2,64,384]{2,1,0:T(8,128)(2,1)S(1)}, bf16[2,64,384]{2,1,0:T(8,128)(2,1)S(1)}, u32[]{:S(2)}, u32[]{:S(2)}) collective-permute-start(bf16[2,64,384]{2,1,0:T(8,128)(2,1)S(1)} %get-tuple-element.14), channel_id=1, source_target_pairs={{2,0},{4,2},{6,4},{0,6},{3,1},{5,3},{7,5},{1,7},{10,8},{12,10},{14... | collective-permute-start | bytes 294920 | tf_op jit(solution)/shard_map/ppermute | solution.py:399

commit v8 on v7

--- a/solution.py
+++ b/solution.py
@@ -202,17 +202,22 @@
     out[...] = (mine[...].astype(F32) + got[...].astype(F32)).astype(BF16)
 
 
-def final_kernel(chunk, CO, mine, got, out, total, even):
+def final_kernel(chunk, CO, mine, got, out, total):
     total[...] = mine[...].astype(F32) + got[...].astype(F32)
-    half, low = chunk // 2, CO - 128
-    side = total[chunk:]
-    even[:half, :low] = side[:, :low]
-    even[half:, :low] = side[:, low:]
-    a, b = (total[pl.ds(p, half, stride=2), :] for p in range(2))
-    a_side, b_side = (even[pl.ds(p, half, stride=2), :][:, :low] for p in range(2))
-    out[pl.ds(0, half, stride=3), :] = a
-    out[pl.ds(1, half, stride=3), :] = jnp.concatenate([a_side, b[:, :low]], axis=1)
-    out[pl.ds(2, half, stride=3), :] = jnp.concatenate([b[:, low:], b_side], axis=1)
+    low = CO - 128
+    part = chunk // 4
+
+    def lines(start):
+        return total[pl.ds(start, part, stride=2), :]
+
+    side, side_next = lines(chunk), lines(chunk + 1)
+    for h in range(2):
+        a, b = lines(2 * part * h), lines(2 * part * h + 1)
+        a_side, b_side = (x[:, h * low : (h + 1) * low] for x in (side, side_next))
+        start = 3 * part * h
+        out[pl.ds(start, part, stride=3), :] = a
+        out[pl.ds(start + 1, part, stride=3), :] = jnp.concatenate([a_side, b[:, :low]], axis=1)
+        out[pl.ds(start + 2, part, stride=3), :] = jnp.concatenate([b[:, low:], b_side], axis=1)
 
 
 def order_kernel(sizes, order, *rest):
@@ -371,7 +376,7 @@
             [struct((packed, 128), F32)],
             0,
             [mine, got],
-            [pltpu.VMEM((packed, 128), F32), pltpu.VMEM((chunk, 128), F32)],
+            [pltpu.VMEM((packed, 128), F32)],
         )
         weight_grad = flat.reshape(-1)
     else:

time: 41.5 us -> 41.4 us (level)
  no operation moved by 1% of the time
where the time goes in v8:
time: 41.4 us; the launch traced here: 41.3 us
  waiting for transfers between devices  16 us (39%)
  starting transfers between devices  15.4 us (37%)
  Pallas kernels  9.02 us (22%)
  between operations  0.81 us (2%)
    pallas_call x14, Pallas kernels, kernel_call(): pl.pallas_call(body, out_shape=outs, in_specs=specs, out_specs=[VMEM] * l...  9.02 us
    ppermute x3, waiting for transfers between devices, local(): got.append(lax.ppermute(share, both, route))  6.81 us
    ppermute x2, starting transfers between devices, local(): got = lax.ppermute(mine, 'clip', [(i, i ^ mask) for i in range(n_clip)])  5.07 us
    ppermute x1, waiting for transfers between devices, local(): later = lax.ppermute(first, 'frame', [(j, i) for i, j in forward])  3.21 us
    ppermute x2, waiting for transfers between devices, local(): got = lax.ppermute(mine, 'clip', [(i, i ^ mask) for i in range(n_clip)])  2.81 us
    ppermute x3, starting transfers between devices, local(): got.append(lax.ppermute(share, both, route))  2.77 us
    ppermute x1, waiting for transfers between devices, local(): prior.append(lax.ppermute(feats, both, route))  2.26 us
    ppermute x1, starting transfers between devices, local(): lax.ppermute(feats, 'row', [(i, (i + d) % n_row) for i in range(n_row)])  2.12 us
  transfers between devices with their start and end apart: 13, of which 7 were waited for; matrix products, arithmetic and copies ran while one was open for 0% of the time, Pallas kernels for 14%

profile of v8, /device:TPU:1, one launch (start us, length us, event | category | flops | bytes accessed | tf_op | source)
XLA Modules:
  0.0 41.3 jit_solution(17047858048138222595)
XLA Ops:
  0.6 0.0 copy-start.1
  0.6 0.0 copy-start.2
  0.6 2.1 %collective-permute-start.2 = (bf16[4,32,384]{2,1,0:T(8,128)(2,1)}, bf16[4,32,384]{2,1,0:T(8,128)(2,1)S(1)}, u32[]{:S(2)}, u32[]{:S(2)}) collective-permute-start(bf16[4,32,384]{2,1,0:T(8,128)(2,1)} %bitcast.13), channel_id=1, source_target_pairs={{0,1},{1,0},{2,3},{3,2},{4,5},{5,4},{6,7},{7,6},{8,9},{9,8},{10,11... | collective-permute-start | bytes 294920 | tf_op jit(solution)/shard_map/ppermute | solution.py:272
  2.8 2.1 %collective-permute-start.3 = (bf16[4,32,384]{2,1,0:T(8,128)(2,1)}, bf16[4,32,384]{2,1,0:T(8,128)(2,1)S(1)}, u32[]{:S(2)}, u32[]{:S(2)}) collective-permute-start(bf16[4,32,384]{2,1,0:T(8,128)(2,1)} %bitcast.14), channel_id=1, source_target_pairs={{0,2},{2,4},{4,6},{6,0},{1,3},{3,5},{5,7},{7,1},{8,10},{10,12},{12... | collective-permute-start | bytes 294920 | tf_op jit(solution)/shard_map/ppermute | solution.py:270
  4.8 0.0 collective-permute-start.4
  4.9 0.0 copy-start
  4.9 0.0 copy-start.3
  4.9 0.0 copy-start.4
  4.9 0.0 copy-done.1
  4.9 0.0 copy-done.2
  4.9 1.5 %shard_map.78 = (bf16[9,256,192]{2,1,0:T(8,128)(2,1)S(1)}, bf16[4,32,384]{2,1,0:T(8,128)(2,1)S(1)}, bf16[4,32,384]{2,1,0:T(8,128)(2,1)S(1)}) custom-call(bf16[4,256,192]{2,1,0:T(8,128)(2,1)S(1)} %bitcast.12, bf16[9,192,384]{2,1,0:T(8,128)(2,1)S(1)} %bitcast.11, bf16[288,256]{1,0:T(8,128)(2,1)S(1)} %shard_map.77.box), custom_call_target="tpu_custom_call" | custom-call | flops 339738624 | bytes 2949120 | tf_op jit(solution)/shard_map/pallas_call | solution.py:27
  6.4 0.0 copy-start.5
  6.4 0.0 collective-permute-done.2.rest_1_.rest_6_
  6.4 0.0 copy-done
  6.4 0.0 copy-done.3
  6.5 0.5 %shard_map.81.rest_3_ = bf16[2,2,64,384]{3,2,1,0:T(8,128)(2,1)S(1)} custom-call(f32[6,128]{1,0:T(8,128)S(1)} %bitcast.18, bf16[3,384,768]{2,1,0:T(8,128)(2,1)S(1)} %copy-done, bf16[4,32,384]{2,1,0:T(8,128)(2,1)S(1)} %bitcast.16, bf16[4,32,384]{2,1,0:T(8,128)(2,1)S(1)} %collective-permute-done.2.rest_1_.rest_6_), custom_call_target="tpu_custom_call" | custom-call | flops 226492416 | bytes 2165760 | tf_op jit(solution)/shard_map/pallas_call | solution.py:27
  7.0 0.0 collective-permute-done.3.rest_7_
  7.0 2.3 %collective-permute-done.4.rest_8_ = bf16[4,32,384]{2,1,0:T(8,128)(2,1)S(1)} collective-permute-done((bf16[4,32,384]{2,1,0:T(8,128)(2,1)}, bf16[4,32,384]{2,1,0:T(8,128)(2,1)S(1)}, u32[]{:S(2)}, u32[]{:S(2)}) %collective-permute-start.4) | collective-permute-done | bytes 98336 | tf_op jit(solution)/shard_map/ppermute | solution.py:277
  9.2 1.6 %shard_map.82 = (bf16[384,256]{1,0:T(8,128)(2,1)S(1)}, bf16[1,648,128]{2,1,0:T(8,128)(2,1)S(1)}) custom-call(s32[8]{0:T(128)S(1)} %bitcast.20, f32[6,128]{1,0:T(8,128)S(1)} %bitcast.19, bf16[3,384,768]{2,1,0:T(8,128)(2,1)S(1)} %copy-done, bf16[2,2,64,384]{3,2,1,0:T(8,128)(2,1)S(1)} %shard_map.81.rest_3_, ...), custom_call_target="tpu_custom_call" | custom-call | flops 42467328 | bytes 3609632 | tf_op jit(solution)/shard_map/pallas_call | solution.py:27
  10.8 0.7 %shard_map.86 = bf16[2,648,128]{2,1,0:T(8,128)(2,1)S(1)} custom-call(bf16[9,256,192]{2,1,0:T(8,128)(2,1)S(1)} %get-tuple-element.15.rest_4_.rest_0_.g, bf16[384,256]{1,0:T(8,128)(2,1)S(1)} %get-tuple-element.16.rest_1_.left), custom_call_target="tpu_custom_call" | custom-call | flops 84934656 | bytes 1413120 | tf_op jit(solution)/shard_map/pallas_call | solution.py:27
  11.5 0.1 collective-permute-start.8
  11.6 0.5 %collective-permute-start.6 = (bf16[1,648,128]{2,1,0:T(8,128)(2,1)S(1)}, bf16[1,648,128]{2,1,0:T(8,128)(2,1)S(1)}, u32[]{:S(2)}, u32[]{:S(2)}) collective-permute-start(bf16[1,648,128]{2,1,0:T(8,128)(2,1)S(1)} %get-tuple-element.17), channel_id=1, source_target_pairs={{0,2},{1,3},{2,0},{3,1},{4,6},{5,7},{6,4},{7,5},{8,10},{9,11},{10,... | collective-permute-start | bytes 497672 | tf_op jit(solution)/shard_map/ppermute | solution.py:351
  12.1 0.3 shard_map.83
  12.5 0.1 collective-permute-start.5
  12.6 0.9 %collective-permute-done.6.got = bf16[1,648,128]{2,1,0:T(8,128)(2,1)S(1)} collective-permute-done((bf16[1,648,128]{2,1,0:T(8,128)(2,1)S(1)}, bf16[1,648,128]{2,1,0:T(8,128)(2,1)S(1)}, u32[]{:S(2)}, u32[]{:S(2)}) %collective-permute-start.6) | collective-permute-done | bytes 165920 | tf_op jit(solution)/shard_map/ppermute | solution.py:351
  13.5 0.3 shard_map.85
  13.8 1.7 %collective-permute-start.7 = (bf16[648,128]{1,0:T(8,128)(2,1)S(1)}, bf16[648,128]{1,0:T(8,128)(2,1)S(1)}, u32[]{:S(2)}, u32[]{:S(2)}) collective-permute-start(bf16[648,128]{1,0:T(8,128)(2,1)S(1)} %shard_map.85), channel_id=1, source_target_pairs={{0,5},{1,4},{2,7},{3,6},{4,1},{5,0},{6,3},{7,2},{8,13},{9,12},{10,... | collective-permute-start | bytes 497672 | tf_op jit(solution)/shard_map/ppermute | solution.py:363
  15.5 0.0 collective-permute-done.8.got
  15.5 0.7 %shard_map.87 = (bf16[648,128]{1,0:T(8,128)(2,1)S(1)}, bf16[648,128]{1,0:T(8,128)(2,1)S(1)}) custom-call(bf16[9,256,192]{2,1,0:T(8,128)(2,1)S(1)} %get-tuple-element.15.rest_4_.rest_0_.g, bf16[384,256]{1,0:T(8,128)(2,1)S(1)} %get-tuple-element.16.rest_1_.left, bf16[2,648,128]{2,1,0:T(8,128)(2,1)S(1)} %collective-permute-done.8.got), custom_call_target="tpu_custom_call" | custom-call | flops 84934656 | bytes 1744896 | tf_op jit(solution)/shard_map/pallas_call | solution.py:27
  16.2 0.7 %collective-permute-start.10 = (bf16[648,128]{1,0:T(8,128)(2,1)S(1)}, bf16[648,128]{1,0:T(8,128)(2,1)S(1)}, u32[]{:S(2)}, u32[]{:S(2)}) collective-permute-start(bf16[648,128]{1,0:T(8,128)(2,1)S(1)} %get-tuple-element.19), channel_id=1, source_target_pairs={{0,4},{1,5},{2,6},{3,7},{4,0},{5,1},{6,2},{7,3},{8,12},{9,13},{10,... | collective-permute-start | bytes 497672 | tf_op jit(solution)/shard_map/ppermute | solution.py:363
  16.9 0.4 collective-permute-start.9
  17.3 0.0 collective-permute-done.5.got
  17.3 0.4 shard_map.84.keep
  17.6 2.8 %collective-permute-done.7.rest_0_ = bf16[648,128]{1,0:T(8,128)(2,1)S(1)} collective-permute-done((bf16[648,128]{1,0:T(8,128)(2,1)S(1)}, bf16[648,128]{1,0:T(8,128)(2,1)S(1)}, u32[]{:S(2)}, u32[]{:S(2)}) %collective-permute-start.7) | collective-permute-done | bytes 165920 | tf_op jit(solution)/shard_map/ppermute | solution.py:363
  20.4 3.5 %collective-permute-done.10.rest_2_ = bf16[648,128]{1,0:T(8,128)(2,1)S(1)} collective-permute-done((bf16[648,128]{1,0:T(8,128)(2,1)S(1)}, bf16[648,128]{1,0:T(8,128)(2,1)S(1)}, u32[]{:S(2)}, u32[]{:S(2)}) %collective-permute-start.10) | collective-permute-done | bytes 165920 | tf_op jit(solution)/shard_map/ppermute | solution.py:363
  23.9 0.5 %collective-permute-done.9.rest_1_ = bf16[648,128]{1,0:T(8,128)(2,1)S(1)} collective-permute-done((bf16[648,128]{1,0:T(8,128)(2,1)S(1)}, bf16[648,128]{1,0:T(8,128)(2,1)S(1)}, u32[]{:S(2)}, u32[]{:S(2)}) %collective-permute-start.9) | collective-permute-done | bytes 165920 | tf_op jit(solution)/shard_map/ppermute | solution.py:363
  24.4 0.1 shard_map.88.mine
  24.5 1.5 %collective-permute-start.11 = (bf16[648,128]{1,0:T(8,128)(2,1)S(1)}, bf16[648,128]{1,0:T(8,128)(2,1)S(1)}, u32[]{:S(2)}, u32[]{:S(2)}) collective-permute-start(bf16[648,128]{1,0:T(8,128)(2,1)S(1)} %shard_map.88.mine), channel_id=1, source_target_pairs={{0,8},{8,0},{16,24},{24,16},{1,9},{9,1},{17,25},{25,17},{2,10},{10... | collective-permute-start | bytes 497672 | tf_op jit(solution)/shard_map/ppermute | solution.py:371
  26.0 1.0 %collective-permute-start = (bf16[4,32,384]{2,1,0:T(8,128)(2,1)S(1)}, bf16[4,32,384]{2,1,0:T(8,128)(2,1)S(1)}, u32[]{:S(2)}, u32[]{:S(2)}) collective-permute-start(bf16[4,32,384]{2,1,0:T(8,128)(2,1)S(1)} %get-tuple-element.12), channel_id=1, source_target_pairs={{0,1},{1,0},{2,3},{3,2},{4,5},{5,4},{6,7},{7,6},{8,9},{9,8},{10,11... | collective-permute-start | bytes 294920 | tf_op jit(solution)/shard_map/ppermute | solution.py:395
  27.1 2.8 %collective-permute-done.11.got = bf16[648,128]{1,0:T(8,128)(2,1)S(1)} collective-permute-done((bf16[648,128]{1,0:T(8,128)(2,1)S(1)}, bf16[648,128]{1,0:T(8,128)(2,1)S(1)}, u32[]{:S(2)}, u32[]{:S(2)}) %collective-permute-start.11) | collective-permute-done | bytes 165920 | tf_op jit(solution)/shard_map/ppermute | solution.py:371
  29.9 3.6 %collective-permute-start.12 = (bf16[648,128]{1,0:T(8,128)(2,1)S(1)}, bf16[648,128]{1,0:T(8,128)(2,1)S(1)}, u32[]{:S(2)}, u32[]{:S(2)}) collective-permute-start(bf16[648,128]{1,0:T(8,128)(2,1)S(1)} %shard_map.89.mine), channel_id=1, source_target_pairs={{0,24},{8,16},{16,8},{24,0},{1,25},{9,17},{17,9},{25,1},{2,26},{10... | collective-permute-start | bytes 497672 | tf_op jit(solution)/shard_map/ppermute | solution.py:371
  33.5 0.0 collective-permute-done.rest_1_
  33.5 0.6 %shard_map.79 = (bf16[2,128,384]{2,1,0:T(8,128)(2,1)S(1)}, bf16[2,64,384]{2,1,0:T(8,128)(2,1)S(1)}) custom-call(s32[8]{0:T(128)S(1)} %bitcast.21, bf16[4,32,384]{2,1,0:T(8,128)(2,1)S(1)} %get-tuple-element.11.rest_0_, bf16[4,32,384]{2,1,0:T(8,128)(2,1)S(1)} %collective-permute-done.rest_1_), custom_call_target="tpu_custom_call" | custom-call | bytes 491552 | tf_op jit(solution)/shard_map/pallas_call | solution.py:27
  34.1 1.7 %collective-permute-start.1 = (bf16[2,64,384]{2,1,0:T(8,128)(2,1)S(1)}, bf16[2,64,384]{2,1,0:T(8,128)(2,1)S(1)}, u32[]{:S(2)}, u32[]{:S(2)}) collective-permute-start(bf16[2,64,384]{2,1,0:T(8,128)(2,1)S(1)} %get-tuple-element.14), channel_id=1, source_target_pairs={{2,0},{4,2},{6,4},{0,6},{3,1},{5,3},{7,5},{1,7},{10,8},{12,10},{14... | collective-permute-start | bytes 294920 | tf_op jit(solution)/shard_map/ppermute | solution.py:404
  35.8 3.2 %collective-permute-done.1.later = bf16[2,64,384]{2,1,0:T(8,128)(2,1)S(1)} collective-permute-done((bf16[2,64,384]{2,1,0:T(8,128)(2,1)S(1)}, bf16[2,64,384]{2,1,0:T(8,128)(2,1)S(1)}, u32[]{:S(2)}, u32[]{:S(2)}) %collective-permute-start.1) | collective-permute-done | bytes 98336 | tf_op jit(solution)/shard_map/ppermute | solution.py:404
  39.0 1.4 %shard_map.80 = bf16[128,384]{1,0:T(8,128)(2,1)} custom-call(bf16[2,128,384]{2,1,0:T(8,128)(2,1)S(1)} %get-tuple-element.13.natural, bf16[2,64,384]{2,1,0:T(8,128)(2,1)S(1)} %collective-permute-done.1.later, bf16[3,384,768]{2,1,0:T(8,128)(2,1)S(1)} %copy-done), custom_call_target="tpu_custom_call" | custom-call | flops 226492416 | bytes 2162688 | tf_op jit(solution)/shard_map/pallas_call | solution.py:27
  40.4 0.0 collective-permute-done.12.got
  40.4 0.9 %shard_map.90 = f32[648,128]{1,0:T(8,128)} custom-call(bf16[648,128]{1,0:T(8,128)(2,1)S(1)} %shard_map.89.mine, bf16[648,128]{1,0:T(8,128)(2,1)S(1)} %collective-permute-done.12.got), custom_call_target="tpu_custom_call" | custom-call | bytes 663552 | tf_op jit(solution)/shard_map/pallas_call | solution.py:27
  (4 shorter events, 0.1 us)
Async XLA Ops:
  0.6 4.3 %copy-start.1 = (bf16[3,3,384,192]{2,3,1,0:T(8,128)(2,1)S(1)}, bf16[3,3,384,192]{2,3,1,0:T(8,128)(2,1)}, u32[]{:S(2)}) copy-start(bf16[3,3,384,192]{2,3,1,0:T(8,128)(2,1)} %param.9) | copy-start | bytes 3981316
  0.6 4.3 %copy-start.2 = (bf16[1,4,4,64,192]{4,3,2,1,0:T(8,128)(2,1)S(1)}, bf16[1,4,4,64,192]{4,3,2,1,0:T(8,128)(2,1)}, u32[]{:S(2)}) copy-start(bf16[1,4,4,64,192]{4,3,2,1,0:T(8,128)(2,1)} %param.10) | copy-start | bytes 1179652
  0.6 5.8 %collective-permute-start.2 = (bf16[4,32,384]{2,1,0:T(8,128)(2,1)}, bf16[4,32,384]{2,1,0:T(8,128)(2,1)S(1)}, u32[]{:S(2)}, u32[]{:S(2)}) collective-permute-start(bf16[4,32,384]{2,1,0:T(8,128)(2,1)} %bitcast.13), channel_id=1, source_target_pairs={{0,1},{1,0},{2,3},{3,2},{4,5},{5,4},{6,7},{7,6},{8,9},{9,8},{10,11... | collective-permute-start | bytes 294920 | tf_op jit(solution)/shard_map/ppermute | solution.py:272
  2.8 4.2 %collective-permute-start.3 = (bf16[4,32,384]{2,1,0:T(8,128)(2,1)}, bf16[4,32,384]{2,1,0:T(8,128)(2,1)S(1)}, u32[]{:S(2)}, u32[]{:S(2)}) collective-permute-start(bf16[4,32,384]{2,1,0:T(8,128)(2,1)} %bitcast.14), channel_id=1, source_target_pairs={{0,2},{2,4},{4,6},{6,0},{1,3},{3,5},{5,7},{7,1},{8,10},{10,12},{12... | collective-permute-start | bytes 294920 | tf_op jit(solution)/shard_map/ppermute | solution.py:270
  4.8 4.4 %collective-permute-start.4 = (bf16[4,32,384]{2,1,0:T(8,128)(2,1)}, bf16[4,32,384]{2,1,0:T(8,128)(2,1)S(1)}, u32[]{:S(2)}, u32[]{:S(2)}) collective-permute-start(bf16[4,32,384]{2,1,0:T(8,128)(2,1)} %bitcast.15), channel_id=1, source_target_pairs={{0,3},{1,2},{2,5},{3,4},{4,7},{5,6},{6,1},{7,0},{8,11},{9,10},{10,... | collective-permute-start | bytes 294920 | tf_op jit(solution)/shard_map/ppermute | solution.py:277
  4.9 1.6 %copy-start = (bf16[3,384,768]{2,1,0:T(8,128)(2,1)S(1)}, bf16[3,384,768]{2,1,0:T(8,128)(2,1)}, u32[]{:S(2)}) copy-start(bf16[3,384,768]{2,1,0:T(8,128)(2,1)} %rest_2_.1) | copy-start | bytes 5308420
  4.9 1.6 %copy-start.3 = (bf16[1,4,1,32,384]{4,3,2,1,0:T(8,128)(2,1)S(1)}, bf16[1,4,1,32,384]{4,3,2,1,0:T(8,128)(2,1)}, u32[]{:S(2)}) copy-start(bf16[1,4,1,32,384]{4,3,2,1,0:T(8,128)(2,1)} %param.6) | copy-start | bytes 294916
  4.9 1.6 %copy-start.4 = (f32[768]{0:T(1024)S(1)}, f32[768]{0:T(1024)}, u32[]{:S(2)}) copy-start(f32[768]{0:T(1024)} %param.8) | copy-start | bytes 9220
  6.4 2.8 %copy-start.5 = (s32[1,1,8]{2,1,0:T(1,128)S(1)}, s32[1,1,8]{2,1,0:T(1,128)}, u32[]{:S(2)}) copy-start(s32[1,1,8]{2,1,0:T(1,128)} %param.11) | copy-start | bytes 100
  11.5 4.0 %collective-permute-start.8 = (bf16[2,648,128]{2,1,0:T(8,128)(2,1)S(1)}, bf16[2,648,128]{2,1,0:T(8,128)(2,1)S(1)}, u32[]{:S(2)}, u32[]{:S(2)}) collective-permute-start(bf16[2,648,128]{2,1,0:T(8,128)(2,1)S(1)} %shard_map.86), channel_id=1, source_target_pairs={{0,2},{1,3},{2,0},{3,1},{4,6},{5,7},{6,4},{7,5},{8,10},{9,11},{10,... | collective-permute-start | bytes 995336 | tf_op jit(solution)/shard_map/ppermute | solution.py:351
  11.6 1.9 %collective-permute-start.6 = (bf16[1,648,128]{2,1,0:T(8,128)(2,1)S(1)}, bf16[1,648,128]{2,1,0:T(8,128)(2,1)S(1)}, u32[]{:S(2)}, u32[]{:S(2)}) collective-permute-start(bf16[1,648,128]{2,1,0:T(8,128)(2,1)S(1)} %get-tuple-element.17), channel_id=1, source_target_pairs={{0,2},{1,3},{2,0},{3,1},{4,6},{5,7},{6,4},{7,5},{8,10},{9,11},{10,... | collective-permute-start | bytes 497672 | tf_op jit(solution)/shard_map/ppermute | solution.py:351
  12.5 4.8 %collective-permute-start.5 = (bf16[1,648,128]{2,1,0:T(8,128)(2,1)S(1)}, bf16[1,648,128]{2,1,0:T(8,128)(2,1)S(1)}, u32[]{:S(2)}, u32[]{:S(2)}) collective-permute-start(bf16[1,648,128]{2,1,0:T(8,128)(2,1)S(1)} %shard_map.83), channel_id=1, source_target_pairs={{0,2},{1,3},{2,0},{3,1},{4,6},{5,7},{6,4},{7,5},{8,10},{9,11},{10,... | collective-permute-start | bytes 497672 | tf_op jit(solution)/shard_map/ppermute | solution.py:351
  13.8 6.6 %collective-permute-start.7 = (bf16[648,128]{1,0:T(8,128)(2,1)S(1)}, bf16[648,128]{1,0:T(8,128)(2,1)S(1)}, u32[]{:S(2)}, u32[]{:S(2)}) collective-permute-start(bf16[648,128]{1,0:T(8,128)(2,1)S(1)} %shard_map.85), channel_id=1, source_target_pairs={{0,5},{1,4},{2,7},{3,6},{4,1},{5,0},{6,3},{7,2},{8,13},{9,12},{10,... | collective-permute-start | bytes 497672 | tf_op jit(solution)/shard_map/ppermute | solution.py:363
  16.2 7.7 %collective-permute-start.10 = (bf16[648,128]{1,0:T(8,128)(2,1)S(1)}, bf16[648,128]{1,0:T(8,128)(2,1)S(1)}, u32[]{:S(2)}, u32[]{:S(2)}) collective-permute-start(bf16[648,128]{1,0:T(8,128)(2,1)S(1)} %get-tuple-element.19), channel_id=1, source_target_pairs={{0,4},{1,5},{2,6},{3,7},{4,0},{5,1},{6,2},{7,3},{8,12},{9,13},{10,... | collective-permute-start | bytes 497672 | tf_op jit(solution)/shard_map/ppermute | solution.py:363
  16.9 7.5 %collective-permute-start.9 = (bf16[648,128]{1,0:T(8,128)(2,1)S(1)}, bf16[648,128]{1,0:T(8,128)(2,1)S(1)}, u32[]{:S(2)}, u32[]{:S(2)}) collective-permute-start(bf16[648,128]{1,0:T(8,128)(2,1)S(1)} %get-tuple-element.18), channel_id=1, source_target_pairs={{0,1},{1,0},{2,3},{3,2},{4,5},{5,4},{6,7},{7,6},{8,9},{9,8},{10,11... | collective-permute-start | bytes 497672 | tf_op jit(solution)/shard_map/ppermute | solution.py:363
  24.5 5.3 %collective-permute-start.11 = (bf16[648,128]{1,0:T(8,128)(2,1)S(1)}, bf16[648,128]{1,0:T(8,128)(2,1)S(1)}, u32[]{:S(2)}, u32[]{:S(2)}) collective-permute-start(bf16[648,128]{1,0:T(8,128)(2,1)S(1)} %shard_map.88.mine), channel_id=1, source_target_pairs={{0,8},{8,0},{16,24},{24,16},{1,9},{9,1},{17,25},{25,17},{2,10},{10... | collective-permute-start | bytes 497672 | tf_op jit(solution)/shard_map/ppermute | solution.py:371
  26.0 7.4 %collective-permute-start = (bf16[4,32,384]{2,1,0:T(8,128)(2,1)S(1)}, bf16[4,32,384]{2,1,0:T(8,128)(2,1)S(1)}, u32[]{:S(2)}, u32[]{:S(2)}) collective-permute-start(bf16[4,32,384]{2,1,0:T(8,128)(2,1)S(1)} %get-tuple-element.12), channel_id=1, source_target_pairs={{0,1},{1,0},{2,3},{3,2},{4,5},{5,4},{6,7},{7,6},{8,9},{9,8},{10,11... | collective-permute-start | bytes 294920 | tf_op jit(solution)/shard_map/ppermute | solution.py:395
  29.9 10.5 %collective-permute-start.12 = (bf16[648,128]{1,0:T(8,128)(2,1)S(1)}, bf16[648,128]{1,0:T(8,128)(2,1)S(1)}, u32[]{:S(2)}, u32[]{:S(2)}) collective-permute-start(bf16[648,128]{1,0:T(8,128)(2,1)S(1)} %shard_map.89.mine), channel_id=1, source_target_pairs={{0,24},{8,16},{16,8},{24,0},{1,25},{9,17},{17,9},{25,1},{2,26},{10... | collective-permute-start | bytes 497672 | tf_op jit(solution)/shard_map/ppermute | solution.py:371
  34.1 4.9 %collective-permute-start.1 = (bf16[2,64,384]{2,1,0:T(8,128)(2,1)S(1)}, bf16[2,64,384]{2,1,0:T(8,128)(2,1)S(1)}, u32[]{:S(2)}, u32[]{:S(2)}) collective-permute-start(bf16[2,64,384]{2,1,0:T(8,128)(2,1)S(1)} %get-tuple-element.14), channel_id=1, source_target_pairs={{2,0},{4,2},{6,4},{0,6},{3,1},{5,3},{7,5},{1,7},{10,8},{12,10},{14... | collective-permute-start | bytes 294920 | tf_op jit(solution)/shard_map/ppermute | solution.py:404

commit v9 on v8

--- a/solution.py
+++ b/solution.py
@@ -164,12 +164,20 @@
     return jnp.concatenate([terms[:, :128], side], axis=0)
 
 
-def chunk_index(d, other):
+def step_mask(d, core, n_dev):
+    if n_dev > 4 and d in (1, 2):
+        return 1 + core if d == 1 else 2 - core
+    return d
+
+
+def chunk_index(d, other, n_dev):
     n_row = lax.axis_size("row")
     frame = lax.axis_index("frame")
-    q = jnp.bitwise_xor((frame // 2) * n_row + lax.axis_index("row"), d)
     core = lax.rem(frame, 2)
-    return ((q // n_row) * 2 + (1 - core if other else core)) * n_row + lax.rem(q, n_row)
+    core = 1 - core if other else core
+    q = (frame // 2) * n_row + lax.axis_index("row")
+    q = jnp.bitwise_xor(q, step_mask(d, core, n_dev))
+    return ((q // n_row) * 2 + core) * n_row + lax.rem(q, n_row)
 
 
 def send_kernel(sizes, plan, group, *rest):
@@ -181,13 +189,13 @@
     else:
         g, left, out, terms = rest
     for j, d in enumerate(group):
-        out[j] = packed_chunk(plan, chunk_index(d, True), left, g, terms).astype(BF16)
+        out[j] = packed_chunk(plan, chunk_index(d, True, plan[0]), left, g, terms).astype(BF16)
 
 
 def keep_kernel(plan, group, g, left, got, *rest):
     outs, terms = rest[:-1], rest[-1]
     for j, d in enumerate(group):
-        value = packed_chunk(plan, chunk_index(d, False), left, g, terms) + got[j].astype(F32)
+        value = packed_chunk(plan, chunk_index(d, False, plan[0]), left, g, terms) + got[j].astype(F32)
         outs[j][...] = value.astype(outs[j].dtype)
 
 
@@ -333,7 +341,7 @@
 
         def square(i, d):
             f, j = i // n_row, i % n_row
-            p = ((f // 2) * n_row + j) ^ d
+            p = ((f // 2) * n_row + j) ^ step_mask(d, f % 2, n_dev)
             return ((p // n_row) * 2 + f % 2) * n_row + p % n_row
 
         got = []

time: 41.4 us -> 41.4 us (level)
  transfers between devices with their start and end apart: 13 -> 13, of which waited for: 7 -> 6; matrix products, arithmetic and copies ran while one was open for 0% -> 0% of each run, Pallas kernels for 14% -> 14%
where the time goes in v9:
time: 41.4 us; the launch traced here: 41.3 us
  waiting for transfers between devices  16 us (39%)
  starting transfers between devices  15.4 us (37%)
  Pallas kernels  9.02 us (22%)
  between operations  0.81 us (2%)
    pallas_call x14, Pallas kernels, kernel_call(): pl.pallas_call(body, out_shape=outs, in_specs=specs, out_specs=[VMEM] * l...  9.02 us
    ppermute x3, waiting for transfers between devices, local(): got.append(lax.ppermute(share, both, route))  6.8 us
    ppermute x2, starting transfers between devices, local(): got = lax.ppermute(mine, 'clip', [(i, i ^ mask) for i in range(n_clip)])  5.05 us
    ppermute x1, waiting for transfers between devices, local(): later = lax.ppermute(first, 'frame', [(j, i) for i, j in forward])  3.19 us
    ppermute x2, waiting for transfers between devices, local(): got = lax.ppermute(mine, 'clip', [(i, i ^ mask) for i in range(n_clip)])  2.81 us
    ppermute x3, starting transfers between devices, local(): got.append(lax.ppermute(share, both, route))  2.79 us
    ppermute x1, waiting for transfers between devices, local(): prior.append(lax.ppermute(feats, both, route))  2.26 us
    ppermute x1, starting transfers between devices, local(): lax.ppermute(feats, 'row', [(i, (i + d) % n_row) for i in range(n_row)])  2.12 us
  transfers between devices with their start and end apart: 13, of which 6 were waited for; matrix products, arithmetic and copies ran while one was open for 0% of the time, Pallas kernels for 14%

profile of v9, /device:TPU:1, one launch (start us, length us, event | category | flops | bytes accessed | tf_op | source)
XLA Modules:
  0.0 41.3 jit_solution(12910845728688498836)
XLA Ops:
  0.6 0.0 copy-start.1
  0.6 0.0 copy-start.2
  0.6 2.1 %collective-permute-start.2 = (bf16[4,32,384]{2,1,0:T(8,128)(2,1)}, bf16[4,32,384]{2,1,0:T(8,128)(2,1)S(1)}, u32[]{:S(2)}, u32[]{:S(2)}) collective-permute-start(bf16[4,32,384]{2,1,0:T(8,128)(2,1)} %bitcast.13), channel_id=1, source_target_pairs={{0,1},{1,0},{2,3},{3,2},{4,5},{5,4},{6,7},{7,6},{8,9},{9,8},{10,11... | collective-permute-start | bytes 294920 | tf_op jit(solution)/shard_map/ppermute | solution.py:280
  2.8 2.1 %collective-permute-start.3 = (bf16[4,32,384]{2,1,0:T(8,128)(2,1)}, bf16[4,32,384]{2,1,0:T(8,128)(2,1)S(1)}, u32[]{:S(2)}, u32[]{:S(2)}) collective-permute-start(bf16[4,32,384]{2,1,0:T(8,128)(2,1)} %bitcast.14), channel_id=1, source_target_pairs={{0,2},{2,4},{4,6},{6,0},{1,3},{3,5},{5,7},{7,1},{8,10},{10,12},{12... | collective-permute-start | bytes 294920 | tf_op jit(solution)/shard_map/ppermute | solution.py:278
  4.8 0.0 collective-permute-start.4
  4.9 0.0 copy-start
  4.9 0.0 copy-start.3
  4.9 0.0 copy-start.4
  4.9 0.0 copy-done.1
  4.9 0.0 copy-done.2
  4.9 1.5 %shard_map.78 = (bf16[9,256,192]{2,1,0:T(8,128)(2,1)S(1)}, bf16[4,32,384]{2,1,0:T(8,128)(2,1)S(1)}, bf16[4,32,384]{2,1,0:T(8,128)(2,1)S(1)}) custom-call(bf16[4,256,192]{2,1,0:T(8,128)(2,1)S(1)} %bitcast.12, bf16[9,192,384]{2,1,0:T(8,128)(2,1)S(1)} %bitcast.11, bf16[288,256]{1,0:T(8,128)(2,1)S(1)} %shard_map.77.box), custom_call_target="tpu_custom_call" | custom-call | flops 339738624 | bytes 2949120 | tf_op jit(solution)/shard_map/pallas_call | solution.py:27
  6.4 0.0 copy-start.5
  6.4 0.0 collective-permute-done.2.rest_1_.rest_6_
  6.4 0.0 copy-done
  6.4 0.0 copy-done.3
  6.5 0.5 %shard_map.81.rest_3_ = bf16[2,2,64,384]{3,2,1,0:T(8,128)(2,1)S(1)} custom-call(f32[6,128]{1,0:T(8,128)S(1)} %bitcast.18, bf16[3,384,768]{2,1,0:T(8,128)(2,1)S(1)} %copy-done, bf16[4,32,384]{2,1,0:T(8,128)(2,1)S(1)} %bitcast.16, bf16[4,32,384]{2,1,0:T(8,128)(2,1)S(1)} %collective-permute-done.2.rest_1_.rest_6_), custom_call_target="tpu_custom_call" | custom-call | flops 226492416 | bytes 2165760 | tf_op jit(solution)/shard_map/pallas_call | solution.py:27
  7.0 0.0 collective-permute-done.3.rest_7_
  7.0 2.3 %collective-permute-done.4.rest_8_ = bf16[4,32,384]{2,1,0:T(8,128)(2,1)S(1)} collective-permute-done((bf16[4,32,384]{2,1,0:T(8,128)(2,1)}, bf16[4,32,384]{2,1,0:T(8,128)(2,1)S(1)}, u32[]{:S(2)}, u32[]{:S(2)}) %collective-permute-start.4) | collective-permute-done | bytes 98336 | tf_op jit(solution)/shard_map/ppermute | solution.py:285
  9.2 1.6 %shard_map.82 = (bf16[384,256]{1,0:T(8,128)(2,1)S(1)}, bf16[1,648,128]{2,1,0:T(8,128)(2,1)S(1)}) custom-call(s32[8]{0:T(128)S(1)} %bitcast.20, f32[6,128]{1,0:T(8,128)S(1)} %bitcast.19, bf16[3,384,768]{2,1,0:T(8,128)(2,1)S(1)} %copy-done, bf16[2,2,64,384]{3,2,1,0:T(8,128)(2,1)S(1)} %shard_map.81.rest_3_, ...), custom_call_target="tpu_custom_call" | custom-call | flops 42467328 | bytes 3609632 | tf_op jit(solution)/shard_map/pallas_call | solution.py:27
  10.8 0.7 %shard_map.86 = bf16[2,648,128]{2,1,0:T(8,128)(2,1)S(1)} custom-call(bf16[9,256,192]{2,1,0:T(8,128)(2,1)S(1)} %get-tuple-element.15.rest_4_.rest_0_.g, bf16[384,256]{1,0:T(8,128)(2,1)S(1)} %get-tuple-element.16.rest_1_.left), custom_call_target="tpu_custom_call" | custom-call | flops 84934656 | bytes 1413120 | tf_op jit(solution)/shard_map/pallas_call | solution.py:27
  11.5 0.1 collective-permute-start.8
  11.6 0.5 %collective-permute-start.6 = (bf16[1,648,128]{2,1,0:T(8,128)(2,1)S(1)}, bf16[1,648,128]{2,1,0:T(8,128)(2,1)S(1)}, u32[]{:S(2)}, u32[]{:S(2)}) collective-permute-start(bf16[1,648,128]{2,1,0:T(8,128)(2,1)S(1)} %get-tuple-element.17), channel_id=1, source_target_pairs={{0,2},{1,3},{2,0},{3,1},{4,6},{5,7},{6,4},{7,5},{8,10},{9,11},{10,... | collective-permute-start | bytes 497672 | tf_op jit(solution)/shard_map/ppermute | solution.py:359
  12.1 0.3 shard_map.83
  12.5 0.1 collective-permute-start.5
  12.6 0.9 %collective-permute-done.6.got = bf16[1,648,128]{2,1,0:T(8,128)(2,1)S(1)} collective-permute-done((bf16[1,648,128]{2,1,0:T(8,128)(2,1)S(1)}, bf16[1,648,128]{2,1,0:T(8,128)(2,1)S(1)}, u32[]{:S(2)}, u32[]{:S(2)}) %collective-permute-start.6) | collective-permute-done | bytes 165920 | tf_op jit(solution)/shard_map/ppermute | solution.py:359
  13.5 0.3 shard_map.85
  13.8 1.7 %collective-permute-start.7 = (bf16[648,128]{1,0:T(8,128)(2,1)S(1)}, bf16[648,128]{1,0:T(8,128)(2,1)S(1)}, u32[]{:S(2)}, u32[]{:S(2)}) collective-permute-start(bf16[648,128]{1,0:T(8,128)(2,1)S(1)} %shard_map.85), channel_id=1, source_target_pairs={{0,5},{1,4},{2,7},{3,6},{4,1},{5,0},{6,3},{7,2},{8,13},{9,12},{10,... | collective-permute-start | bytes 497672 | tf_op jit(solution)/shard_map/ppermute | solution.py:371
  15.5 0.0 collective-permute-done.8.got
  15.5 0.7 %shard_map.87 = (bf16[648,128]{1,0:T(8,128)(2,1)S(1)}, bf16[648,128]{1,0:T(8,128)(2,1)S(1)}) custom-call(bf16[9,256,192]{2,1,0:T(8,128)(2,1)S(1)} %get-tuple-element.15.rest_4_.rest_0_.g, bf16[384,256]{1,0:T(8,128)(2,1)S(1)} %get-tuple-element.16.rest_1_.left, bf16[2,648,128]{2,1,0:T(8,128)(2,1)S(1)} %collective-permute-done.8.got), custom_call_target="tpu_custom_call" | custom-call | flops 84934656 | bytes 1744896 | tf_op jit(solution)/shard_map/pallas_call | solution.py:27
  16.2 0.8 %collective-permute-start.10 = (bf16[648,128]{1,0:T(8,128)(2,1)S(1)}, bf16[648,128]{1,0:T(8,128)(2,1)S(1)}, u32[]{:S(2)}, u32[]{:S(2)}) collective-permute-start(bf16[648,128]{1,0:T(8,128)(2,1)S(1)} %get-tuple-element.19), channel_id=1, source_target_pairs={{0,4},{1,5},{2,3},{3,2},{4,0},{5,1},{6,7},{7,6},{8,12},{9,13},{10,... | collective-permute-start | bytes 497672 | tf_op jit(solution)/shard_map/ppermute | solution.py:371
  17.0 0.3 collective-permute-start.9
  17.3 0.0 collective-permute-done.5.got
  17.3 0.4 shard_map.84.keep
  17.6 2.8 %collective-permute-done.7.rest_0_ = bf16[648,128]{1,0:T(8,128)(2,1)S(1)} collective-permute-done((bf16[648,128]{1,0:T(8,128)(2,1)S(1)}, bf16[648,128]{1,0:T(8,128)(2,1)S(1)}, u32[]{:S(2)}, u32[]{:S(2)}) %collective-permute-start.7) | collective-permute-done | bytes 165920 | tf_op jit(solution)/shard_map/ppermute | solution.py:371
  20.4 4.0 %collective-permute-done.10.rest_2_ = bf16[648,128]{1,0:T(8,128)(2,1)S(1)} collective-permute-done((bf16[648,128]{1,0:T(8,128)(2,1)S(1)}, bf16[648,128]{1,0:T(8,128)(2,1)S(1)}, u32[]{:S(2)}, u32[]{:S(2)}) %collective-permute-start.10) | collective-permute-done | bytes 165920 | tf_op jit(solution)/shard_map/ppermute | solution.py:371
  24.4 0.0 collective-permute-done.9.rest_1_
  24.4 0.1 shard_map.88.mine
  24.5 1.5 %collective-permute-start.11 = (bf16[648,128]{1,0:T(8,128)(2,1)S(1)}, bf16[648,128]{1,0:T(8,128)(2,1)S(1)}, u32[]{:S(2)}, u32[]{:S(2)}) collective-permute-start(bf16[648,128]{1,0:T(8,128)(2,1)S(1)} %shard_map.88.mine), channel_id=1, source_target_pairs={{0,8},{8,0},{16,24},{24,16},{1,9},{9,1},{17,25},{25,17},{2,10},{10... | collective-permute-start | bytes 497672 | tf_op jit(solution)/shard_map/ppermute | solution.py:379
  26.0 1.0 %collective-permute-start = (bf16[4,32,384]{2,1,0:T(8,128)(2,1)S(1)}, bf16[4,32,384]{2,1,0:T(8,128)(2,1)S(1)}, u32[]{:S(2)}, u32[]{:S(2)}) collective-permute-start(bf16[4,32,384]{2,1,0:T(8,128)(2,1)S(1)} %get-tuple-element.12), channel_id=1, source_target_pairs={{0,1},{1,0},{2,3},{3,2},{4,5},{5,4},{6,7},{7,6},{8,9},{9,8},{10,11... | collective-permute-start | bytes 294920 | tf_op jit(solution)/shard_map/ppermute | solution.py:403
  27.1 2.8 %collective-permute-done.11.got = bf16[648,128]{1,0:T(8,128)(2,1)S(1)} collective-permute-done((bf16[648,128]{1,0:T(8,128)(2,1)S(1)}, bf16[648,128]{1,0:T(8,128)(2,1)S(1)}, u32[]{:S(2)}, u32[]{:S(2)}) %collective-permute-start.11) | collective-permute-done | bytes 165920 | tf_op jit(solution)/shard_map/ppermute | solution.py:379
  29.9 3.6 %collective-permute-start.12 = (bf16[648,128]{1,0:T(8,128)(2,1)S(1)}, bf16[648,128]{1,0:T(8,128)(2,1)S(1)}, u32[]{:S(2)}, u32[]{:S(2)}) collective-permute-start(bf16[648,128]{1,0:T(8,128)(2,1)S(1)} %shard_map.89.mine), channel_id=1, source_target_pairs={{0,24},{8,16},{16,8},{24,0},{1,25},{9,17},{17,9},{25,1},{2,26},{10... | collective-permute-start | bytes 497672 | tf_op jit(solution)/shard_map/ppermute | solution.py:379
  33.5 0.0 collective-permute-done.rest_1_
  33.5 0.6 %shard_map.79 = (bf16[2,128,384]{2,1,0:T(8,128)(2,1)S(1)}, bf16[2,64,384]{2,1,0:T(8,128)(2,1)S(1)}) custom-call(s32[8]{0:T(128)S(1)} %bitcast.21, bf16[4,32,384]{2,1,0:T(8,128)(2,1)S(1)} %get-tuple-element.11.rest_0_, bf16[4,32,384]{2,1,0:T(8,128)(2,1)S(1)} %collective-permute-done.rest_1_), custom_call_target="tpu_custom_call" | custom-call | bytes 491552 | tf_op jit(solution)/shard_map/pallas_call | solution.py:27
  34.1 1.7 %collective-permute-start.1 = (bf16[2,64,384]{2,1,0:T(8,128)(2,1)S(1)}, bf16[2,64,384]{2,1,0:T(8,128)(2,1)S(1)}, u32[]{:S(2)}, u32[]{:S(2)}) collective-permute-start(bf16[2,64,384]{2,1,0:T(8,128)(2,1)S(1)} %get-tuple-element.14), channel_id=1, source_target_pairs={{2,0},{4,2},{6,4},{0,6},{3,1},{5,3},{7,5},{1,7},{10,8},{12,10},{14... | collective-permute-start | bytes 294920 | tf_op jit(solution)/shard_map/ppermute | solution.py:412
  35.8 3.2 %collective-permute-done.1.later = bf16[2,64,384]{2,1,0:T(8,128)(2,1)S(1)} collective-permute-done((bf16[2,64,384]{2,1,0:T(8,128)(2,1)S(1)}, bf16[2,64,384]{2,1,0:T(8,128)(2,1)S(1)}, u32[]{:S(2)}, u32[]{:S(2)}) %collective-permute-start.1) | collective-permute-done | bytes 98336 | tf_op jit(solution)/shard_map/ppermute | solution.py:412
  39.0 1.4 %shard_map.80 = bf16[128,384]{1,0:T(8,128)(2,1)} custom-call(bf16[2,128,384]{2,1,0:T(8,128)(2,1)S(1)} %get-tuple-element.13.natural, bf16[2,64,384]{2,1,0:T(8,128)(2,1)S(1)} %collective-permute-done.1.later, bf16[3,384,768]{2,1,0:T(8,128)(2,1)S(1)} %copy-done), custom_call_target="tpu_custom_call" | custom-call | flops 226492416 | bytes 2162688 | tf_op jit(solution)/shard_map/pallas_call | solution.py:27
  40.4 0.0 collective-permute-done.12.got
  40.4 0.9 %shard_map.90 = f32[648,128]{1,0:T(8,128)} custom-call(bf16[648,128]{1,0:T(8,128)(2,1)S(1)} %shard_map.89.mine, bf16[648,128]{1,0:T(8,128)(2,1)S(1)} %collective-permute-done.12.got), custom_call_target="tpu_custom_call" | custom-call | bytes 663552 | tf_op jit(solution)/shard_map/pallas_call | solution.py:27
  (4 shorter events, 0.1 us)
Async XLA Ops:
  0.6 4.3 %copy-start.1 = (bf16[3,3,384,192]{2,3,1,0:T(8,128)(2,1)S(1)}, bf16[3,3,384,192]{2,3,1,0:T(8,128)(2,1)}, u32[]{:S(2)}) copy-start(bf16[3,3,384,192]{2,3,1,0:T(8,128)(2,1)} %param.9) | copy-start | bytes 3981316
  0.6 4.3 %copy-start.2 = (bf16[1,4,4,64,192]{4,3,2,1,0:T(8,128)(2,1)S(1)}, bf16[1,4,4,64,192]{4,3,2,1,0:T(8,128)(2,1)}, u32[]{:S(2)}) copy-start(bf16[1,4,4,64,192]{4,3,2,1,0:T(8,128)(2,1)} %param.10) | copy-start | bytes 1179652
  0.6 5.8 %collective-permute-start.2 = (bf16[4,32,384]{2,1,0:T(8,128)(2,1)}, bf16[4,32,384]{2,1,0:T(8,128)(2,1)S(1)}, u32[]{:S(2)}, u32[]{:S(2)}) collective-permute-start(bf16[4,32,384]{2,1,0:T(8,128)(2,1)} %bitcast.13), channel_id=1, source_target_pairs={{0,1},{1,0},{2,3},{3,2},{4,5},{5,4},{6,7},{7,6},{8,9},{9,8},{10,11... | collective-permute-start | bytes 294920 | tf_op jit(solution)/shard_map/ppermute | solution.py:280
  2.8 4.2 %collective-permute-start.3 = (bf16[4,32,384]{2,1,0:T(8,128)(2,1)}, bf16[4,32,384]{2,1,0:T(8,128)(2,1)S(1)}, u32[]{:S(2)}, u32[]{:S(2)}) collective-permute-start(bf16[4,32,384]{2,1,0:T(8,128)(2,1)} %bitcast.14), channel_id=1, source_target_pairs={{0,2},{2,4},{4,6},{6,0},{1,3},{3,5},{5,7},{7,1},{8,10},{10,12},{12... | collective-permute-start | bytes 294920 | tf_op jit(solution)/shard_map/ppermute | solution.py:278
  4.8 4.4 %collective-permute-start.4 = (bf16[4,32,384]{2,1,0:T(8,128)(2,1)}, bf16[4,32,384]{2,1,0:T(8,128)(2,1)S(1)}, u32[]{:S(2)}, u32[]{:S(2)}) collective-permute-start(bf16[4,32,384]{2,1,0:T(8,128)(2,1)} %bitcast.15), channel_id=1, source_target_pairs={{0,3},{1,2},{2,5},{3,4},{4,7},{5,6},{6,1},{7,0},{8,11},{9,10},{10,... | collective-permute-start | bytes 294920 | tf_op jit(solution)/shard_map/ppermute | solution.py:285
  4.9 1.6 %copy-start = (bf16[3,384,768]{2,1,0:T(8,128)(2,1)S(1)}, bf16[3,384,768]{2,1,0:T(8,128)(2,1)}, u32[]{:S(2)}) copy-start(bf16[3,384,768]{2,1,0:T(8,128)(2,1)} %rest_2_.1) | copy-start | bytes 5308420
  4.9 1.6 %copy-start.3 = (bf16[1,4,1,32,384]{4,3,2,1,0:T(8,128)(2,1)S(1)}, bf16[1,4,1,32,384]{4,3,2,1,0:T(8,128)(2,1)}, u32[]{:S(2)}) copy-start(bf16[1,4,1,32,384]{4,3,2,1,0:T(8,128)(2,1)} %param.6) | copy-start | bytes 294916
  4.9 1.6 %copy-start.4 = (f32[768]{0:T(1024)S(1)}, f32[768]{0:T(1024)}, u32[]{:S(2)}) copy-start(f32[768]{0:T(1024)} %param.8) | copy-start | bytes 9220
  6.4 2.8 %copy-start.5 = (s32[1,1,8]{2,1,0:T(1,128)S(1)}, s32[1,1,8]{2,1,0:T(1,128)}, u32[]{:S(2)}) copy-start(s32[1,1,8]{2,1,0:T(1,128)} %param.11) | copy-start | bytes 100
  11.5 4.0 %collective-permute-start.8 = (bf16[2,648,128]{2,1,0:T(8,128)(2,1)S(1)}, bf16[2,648,128]{2,1,0:T(8,128)(2,1)S(1)}, u32[]{:S(2)}, u32[]{:S(2)}) collective-permute-start(bf16[2,648,128]{2,1,0:T(8,128)(2,1)S(1)} %shard_map.86), channel_id=1, source_target_pairs={{0,2},{1,3},{2,0},{3,1},{4,6},{5,7},{6,4},{7,5},{8,10},{9,11},{10,... | collective-permute-start | bytes 995336 | tf_op jit(solution)/shard_map/ppermute | solution.py:359
  11.6 1.9 %collective-permute-start.6 = (bf16[1,648,128]{2,1,0:T(8,128)(2,1)S(1)}, bf16[1,648,128]{2,1,0:T(8,128)(2,1)S(1)}, u32[]{:S(2)}, u32[]{:S(2)}) collective-permute-start(bf16[1,648,128]{2,1,0:T(8,128)(2,1)S(1)} %get-tuple-element.17), channel_id=1, source_target_pairs={{0,2},{1,3},{2,0},{3,1},{4,6},{5,7},{6,4},{7,5},{8,10},{9,11},{10,... | collective-permute-start | bytes 497672 | tf_op jit(solution)/shard_map/ppermute | solution.py:359
  12.5 4.8 %collective-permute-start.5 = (bf16[1,648,128]{2,1,0:T(8,128)(2,1)S(1)}, bf16[1,648,128]{2,1,0:T(8,128)(2,1)S(1)}, u32[]{:S(2)}, u32[]{:S(2)}) collective-permute-start(bf16[1,648,128]{2,1,0:T(8,128)(2,1)S(1)} %shard_map.83), channel_id=1, source_target_pairs={{0,2},{1,3},{2,0},{3,1},{4,6},{5,7},{6,4},{7,5},{8,10},{9,11},{10,... | collective-permute-start | bytes 497672 | tf_op jit(solution)/shard_map/ppermute | solution.py:359
  13.8 6.6 %collective-permute-start.7 = (bf16[648,128]{1,0:T(8,128)(2,1)S(1)}, bf16[648,128]{1,0:T(8,128)(2,1)S(1)}, u32[]{:S(2)}, u32[]{:S(2)}) collective-permute-start(bf16[648,128]{1,0:T(8,128)(2,1)S(1)} %shard_map.85), channel_id=1, source_target_pairs={{0,5},{1,4},{2,7},{3,6},{4,1},{5,0},{6,3},{7,2},{8,13},{9,12},{10,... | collective-permute-start | bytes 497672 | tf_op jit(solution)/shard_map/ppermute | solution.py:371
  16.2 8.2 %collective-permute-start.10 = (bf16[648,128]{1,0:T(8,128)(2,1)S(1)}, bf16[648,128]{1,0:T(8,128)(2,1)S(1)}, u32[]{:S(2)}, u32[]{:S(2)}) collective-permute-start(bf16[648,128]{1,0:T(8,128)(2,1)S(1)} %get-tuple-element.19), channel_id=1, source_target_pairs={{0,4},{1,5},{2,3},{3,2},{4,0},{5,1},{6,7},{7,6},{8,12},{9,13},{10,... | collective-permute-start | bytes 497672 | tf_op jit(solution)/shard_map/ppermute | solution.py:371
  17.0 7.5 %collective-permute-start.9 = (bf16[648,128]{1,0:T(8,128)(2,1)S(1)}, bf16[648,128]{1,0:T(8,128)(2,1)S(1)}, u32[]{:S(2)}, u32[]{:S(2)}) collective-permute-start(bf16[648,128]{1,0:T(8,128)(2,1)S(1)} %get-tuple-element.18), channel_id=1, source_target_pairs={{0,1},{1,0},{2,6},{3,7},{4,5},{5,4},{6,2},{7,3},{8,9},{9,8},{10,14... | collective-permute-start | bytes 497672 | tf_op jit(solution)/shard_map/ppermute | solution.py:371
  24.5 5.3 %collective-permute-start.11 = (bf16[648,128]{1,0:T(8,128)(2,1)S(1)}, bf16[648,128]{1,0:T(8,128)(2,1)S(1)}, u32[]{:S(2)}, u32[]{:S(2)}) collective-permute-start(bf16[648,128]{1,0:T(8,128)(2,1)S(1)} %shard_map.88.mine), channel_id=1, source_target_pairs={{0,8},{8,0},{16,24},{24,16},{1,9},{9,1},{17,25},{25,17},{2,10},{10... | collective-permute-start | bytes 497672 | tf_op jit(solution)/shard_map/ppermute | solution.py:379
  26.0 7.4 %collective-permute-start = (bf16[4,32,384]{2,1,0:T(8,128)(2,1)S(1)}, bf16[4,32,384]{2,1,0:T(8,128)(2,1)S(1)}, u32[]{:S(2)}, u32[]{:S(2)}) collective-permute-start(bf16[4,32,384]{2,1,0:T(8,128)(2,1)S(1)} %get-tuple-element.12), channel_id=1, source_target_pairs={{0,1},{1,0},{2,3},{3,2},{4,5},{5,4},{6,7},{7,6},{8,9},{9,8},{10,11... | collective-permute-start | bytes 294920 | tf_op jit(solution)/shard_map/ppermute | solution.py:403
  29.9 10.5 %collective-permute-start.12 = (bf16[648,128]{1,0:T(8,128)(2,1)S(1)}, bf16[648,128]{1,0:T(8,128)(2,1)S(1)}, u32[]{:S(2)}, u32[]{:S(2)}) collective-permute-start(bf16[648,128]{1,0:T(8,128)(2,1)S(1)} %shard_map.89.mine), channel_id=1, source_target_pairs={{0,24},{8,16},{16,8},{24,0},{1,25},{9,17},{17,9},{25,1},{2,26},{10... | collective-permute-start | bytes 497672 | tf_op jit(solution)/shard_map/ppermute | solution.py:379
  34.1 4.9 %collective-permute-start.1 = (bf16[2,64,384]{2,1,0:T(8,128)(2,1)S(1)}, bf16[2,64,384]{2,1,0:T(8,128)(2,1)S(1)}, u32[]{:S(2)}, u32[]{:S(2)}) collective-permute-start(bf16[2,64,384]{2,1,0:T(8,128)(2,1)S(1)} %get-tuple-element.14), channel_id=1, source_target_pairs={{2,0},{4,2},{6,4},{0,6},{3,1},{5,3},{7,5},{1,7},{10,8},{12,10},{14... | collective-permute-start | bytes 294920 | tf_op jit(solution)/shard_map/ppermute | solution.py:412
